TPU v7x, 32 devices: a whole 2x2x4 slice. The times are simulated.
32 devices in a mesh: dp: 4 (over x, core), fsdp: 8 (over z, y).
Axes of the slice: x: 2, y: 2, z: 4, core: 2. Of those that a mesh axis runs over, the one named last changes fastest.
Arguments:
- tokens: bfloat16 [2, 4, 2048, 1152], P(None, 'dp', 'fsdp'), may hold values from -6 to 6
- cotangent: bfloat16 [2, 4, 2048, 1152], P(None, 'dp', 'fsdp'), may hold values from -6 to 6
- lengths: int32 [2, 4, 8], P(None, 'dp'), may hold values from 1 to 128, 768 in all within a row
- master: float32 [1152, 23296], P('fsdp'), may hold values from -0.1875 to 0.1875
- gains: float32 [5120], replicated, may hold values from 0.5 to 1.5
- gain_stats: float32 [5120], replicated, may hold values from 1024 to 65536
- owner: int32 [1456, 1], P('fsdp'), may hold values from 0 to 3; in each aligned block of 182 rows (0 to 181, 182 to 363, ...) at most 57 rows name the same one
- stat_left: float32 [8, 228, 144, 144], P('fsdp', 'dp'), may hold values from -3145728 to 3145728
- stat_right: float32 [8, 228, 128, 128], P('fsdp', 'dp'), may hold values from -3670016 to 3670016
- root_left: bfloat16 [8, 228, 144, 144], P('fsdp', 'dp')
- root_right: bfloat16 [8, 228, 128, 128], P('fsdp', 'dp')
Outputs:
- output: bfloat16 [2, 4, 2048, 1152], P(None, 'dp', 'fsdp')
- input_grad: bfloat16 [2, 4, 2048, 1152], P(None, 'dp', 'fsdp')
- weight_grad: float32 [8, 228, 144, 128], P('fsdp', 'dp')
- gain_grad: float32 [5120], replicated
- new_left: float32 [8, 228, 144, 144], P('fsdp', 'dp')
- new_right: float32 [8, 228, 128, 128], P('fsdp', 'dp')
- new_master: float32 [1152, 23296], P('fsdp')
- new_weights: bfloat16 [1152, 23296], P('fsdp')
- new_gain_stats: float32 [5120], replicated
- gain_change: float32 [5120], replicated
Inputs may be any that keep to these rules, and one draw needn't show every extreme that they name: `lengths`: each row lists the used slots of the 8 continuations of one group; a row sums to 768 and holds at least one 128. `owner`: entry j * 182 + b names the dp index that owns block b of row band j; among one band's 182 entries no index appears more than 57 times.
All inputs are finite; a program needn't handle non-finite values.
Results may differ from a plain program's by a relative error of at most 0.02.
The roundings to bfloat16 on the way count: a program that leaves them out, or rounds other values in their place, can miss the bound.
Values may be sent and summed in bfloat16 or wider, within the bound.
No kernel may reach another device: no remote copies, remote signals or barrier semaphores. Data moves between devices by JAX's collectives and lax.ppermute only.
A program may use at most 448 MiB of HBM per device.

v0:
```python
import jax
import jax.numpy as jnp
from jax import lax
from jax.sharding import PartitionSpec as P

D = 1152
HEADS = 4
HD = 256
FF = 6912
WIN = 512
PROMPT = 1024
CONT = 8
CLEN = 128
BC = 128
GLEN = 2048
QKVW = 1536
NBLK = 182


EPSILON = 1e-06
HIGHEST = lax.Precision.HIGHEST
MASKED = -1e30
RATE = 0.02
GAIN_RATE = 0.05
DECAY = 0.5


def shortened(array):

    def short(part):
        return part.astype(jnp.bfloat16) if part.dtype == jnp.float32 else part

    return jax.tree.map(short, array)


def rms_gain(values, gain):
    return values * lax.rsqrt(jnp.mean(values * values, axis=-1, keepdims=True) + EPSILON) * gain


def rope_tables(positions):
    half_width = HD // 2
    freqs = 10000.0 ** (-2.0 * jnp.arange(half_width, dtype=jnp.float32) / HD)
    angles = positions.astype(jnp.float32)[:, None] * freqs[None, :]
    return (jnp.cos(angles), jnp.sin(angles))


def rotate(values, cosine, sine):
    half_width = values.shape[-1] // 2
    first_half = values[..., :half_width]
    second_half = values[..., half_width:]
    return jnp.concatenate(
        [first_half * cosine - second_half * sine, second_half * cosine + first_half * sine],
        axis=-1,
    )


def slot_layout(slots):
    in_prompt = slots < PROMPT
    offset = slots - PROMPT
    segment = jnp.where(in_prompt, -1, offset // CLEN)
    position = jnp.where(in_prompt, slots, PROMPT + offset % CLEN)
    return (segment, position)


def visibility(query_slots, key_slots, lens):
    query_seg, query_pos = slot_layout(query_slots)
    key_seg, key_pos = slot_layout(key_slots)
    picks = key_seg[:, None] == jnp.arange(CONT, dtype=jnp.int32)[None, :]
    key_len = jnp.sum(jnp.where(picks, lens[None, :], 0), axis=1)
    key_used = (key_seg < 0) | (key_pos - PROMPT < key_len)
    distance = query_pos[:, None] - key_pos[None, :]
    same_part = (key_seg[None, :] < 0) | (key_seg[None, :] == query_seg[:, None])
    return (distance >= 0) & (distance < WIN) & same_part & key_used[None, :]


def split_gains(gains):
    return (
        gains[:D],
        gains[D : 2 * D],
        gains[2 * D : 3 * D],
        gains[3 * D : 4 * D],
        gains[4 * D : 4 * D + HD],
        gains[4 * D + HD :],
    )


def prepare_heads(queries, keys, query_gain, key_gain, cosine, sine):
    rot_queries = rotate(rms_gain(queries, query_gain), cosine[:, None, :], sine[:, None, :])
    rot_keys = rotate(rms_gain(keys, key_gain), cosine, sine)
    return (rot_queries, rot_keys)


def contract_last(left, right):
    return lax.dot_general(
        left, right, (((1,), (1,)), ((), ())), preferred_element_type=jnp.float32
    )


def masked_scores(query_low, keys_all, visible):
    scores = jnp.einsum(
        "gthd,gkd->gthk", query_low, keys_all, preferred_element_type=jnp.float32
    ) * HD ** (-0.5)
    return jnp.where(visible[:, :, None, :], scores, MASKED)


def forward_step(group_in, lens, weights, gains, first):
    groups, rows = (group_in.shape[0], group_in.shape[1])
    count = groups * rows
    pre_attn, post_attn, pre_ffw, post_ffw, query_gain, key_gain = split_gains(gains)
    gate_start = QKVW + HEADS * HD
    flat_in = group_in.astype(jnp.float32).reshape(count, D)
    normed = rms_gain(flat_in, pre_attn).astype(jnp.bfloat16)
    projected = jnp.dot(normed, weights[:, :QKVW], preferred_element_type=jnp.float32)
    queries = projected[:, : HEADS * HD].reshape(count, HEADS, HD)
    keys = projected[:, HEADS * HD : (HEADS + 1) * HD]
    values = projected[:, (HEADS + 1) * HD :]
    slots = first + jnp.arange(rows, dtype=jnp.int32)
    segment, positions = slot_layout(slots)
    cosine, sine = rope_tables(jnp.tile(positions, groups))
    rot_queries, rot_keys = prepare_heads(queries, keys, query_gain, key_gain, cosine, sine)
    query_low = rot_queries.astype(jnp.bfloat16).reshape(groups, rows, HEADS, HD)
    key_low = rot_keys.astype(jnp.bfloat16).reshape(groups, rows, HD)
    value_low = values.astype(jnp.bfloat16).reshape(groups, rows, HD)
    keys_all, values_all = (
        lax.all_gather(key_low, "fsdp", axis=1, tiled=True),
        lax.all_gather(value_low, "fsdp", axis=1, tiled=True),
    )
    key_slots = jnp.arange(GLEN, dtype=jnp.int32)
    visible = jax.vmap(lambda lens_row: visibility(slots, key_slots, lens_row))(lens)
    scores = masked_scores(query_low, keys_all, visible)
    highest = jnp.max(scores, axis=-1, keepdims=True)
    expo = jnp.exp(scores - highest)
    totals = jnp.sum(expo, axis=-1, keepdims=True)
    probs = expo / totals
    log_total = highest + jnp.log(totals)
    mixed = jnp.einsum(
        "gthk,gkd->gthd", probs.astype(jnp.bfloat16), values_all, preferred_element_type=jnp.float32
    )
    attended = mixed.reshape(count, HEADS * HD).astype(jnp.bfloat16)
    branch_one = contract_last(attended, weights[:, QKVW:gate_start])
    resid = flat_in + rms_gain(branch_one, post_attn)
    ffw_in = rms_gain(resid, pre_ffw).astype(jnp.bfloat16)
    both = jnp.dot(
        ffw_in, weights[:, gate_start : gate_start + 2 * FF], preferred_element_type=jnp.float32
    )
    gate = both[:, :FF]
    up_proj = both[:, FF:]
    hidden = (jax.nn.gelu(gate, approximate=True) * up_proj).astype(jnp.bfloat16)
    branch_two = contract_last(hidden, weights[:, gate_start + 2 * FF :])
    result = (resid + rms_gain(branch_two, post_ffw)).astype(jnp.bfloat16).reshape(groups, rows, D)
    kept = (
        flat_in,
        normed,
        queries,
        keys,
        cosine,
        sine,
        query_low,
        keys_all,
        values_all,
        visible,
        log_total,
        attended,
        branch_one,
        resid,
        ffw_in,
        gate,
        up_proj,
        hidden,
        branch_two,
    )
    return (result, kept)


def backward_step(upstream_low, kept, weights, gains):
    (
        flat_in,
        normed,
        queries,
        keys,
        cosine,
        sine,
        query_low,
        keys_all,
        values_all,
        visible,
        log_total,
        attended,
        branch_one,
        resid,
        ffw_in,
        gate,
        up_proj,
        hidden,
        branch_two,
    ) = kept
    groups, rows = (query_low.shape[0], query_low.shape[1])
    count = groups * rows
    pre_attn, post_attn, pre_ffw, post_ffw, query_gain, key_gain = split_gains(gains)
    gate_start = QKVW + HEADS * HD
    upstream = upstream_low.astype(jnp.float32).reshape(count, D)
    grad_two, grad_post_ffw = jax.vjp(rms_gain, branch_two, post_ffw)[1](upstream)
    low_two = grad_two.astype(jnp.bfloat16)
    grad_hidden = jnp.dot(
        low_two, weights[:, gate_start + 2 * FF :], preferred_element_type=jnp.float32
    )
    grad_gate, grad_up = jax.vjp(
        lambda gate_in, up_in: jax.nn.gelu(gate_in, approximate=True) * up_in, gate, up_proj
    )[1](grad_hidden)
    low_gate_up = jnp.concatenate([grad_gate, grad_up], axis=1).astype(jnp.bfloat16)
    grad_ffw_in = contract_last(low_gate_up, weights[:, gate_start : gate_start + 2 * FF])
    grad_resid, grad_pre_ffw = jax.vjp(rms_gain, resid, pre_ffw)[1](grad_ffw_in)
    grad_resid = upstream + grad_resid
    grad_one, grad_post_attn = jax.vjp(rms_gain, branch_one, post_attn)[1](grad_resid)
    low_one = grad_one.astype(jnp.bfloat16)
    grad_mixed = jnp.dot(low_one, weights[:, QKVW:gate_start], preferred_element_type=jnp.float32)
    low_mixed = grad_mixed.astype(jnp.bfloat16).reshape(groups, rows, HEADS, HD)
    scores = masked_scores(query_low, keys_all, visible)
    probs = jnp.exp(scores - log_total)
    grad_probs = jnp.einsum(
        "gthd,gkd->gthk", low_mixed, values_all, preferred_element_type=jnp.float32
    )
    row_dot = jnp.sum(grad_probs * probs, axis=-1, keepdims=True)
    grad_scores = (probs * (grad_probs - row_dot)).astype(jnp.bfloat16)
    scale = HD ** (-0.5)
    grad_queries = (
        jnp.einsum("gthk,gkd->gthd", grad_scores, keys_all, preferred_element_type=jnp.float32)
        * scale
    )
    key_terms = (
        jnp.einsum("gthk,gthd->gkd", grad_scores, query_low, preferred_element_type=jnp.float32)
        * scale
    )
    value_terms = jnp.einsum(
        "gthk,gthd->gkd", probs.astype(jnp.bfloat16), low_mixed, preferred_element_type=jnp.float32
    )
    grad_keys, grad_values = (
        lax.psum_scatter(
            key_terms.astype(jnp.bfloat16), "fsdp", scatter_dimension=1, tiled=True
        ).astype(jnp.float32),
        lax.psum_scatter(
            value_terms.astype(jnp.bfloat16), "fsdp", scatter_dimension=1, tiled=True
        ).astype(jnp.float32),
    )

    def heads_only(query_in, key_in, query_scale, key_scale):
        return prepare_heads(query_in, key_in, query_scale, key_scale, cosine, sine)

    pull_heads = jax.vjp(heads_only, queries, keys, query_gain, key_gain)[1]
    grad_query_pre, grad_key_pre, grad_query_gain, grad_key_gain = pull_heads(
        (grad_queries.reshape(count, HEADS, HD), grad_keys.reshape(count, HD))
    )
    low_projected = jnp.concatenate(
        [grad_query_pre.reshape(count, HEADS * HD), grad_key_pre, grad_values.reshape(count, HD)],
        axis=1,
    ).astype(jnp.bfloat16)
    grad_normed = contract_last(low_projected, weights[:, :QKVW])
    grad_in, grad_pre_attn = jax.vjp(rms_gain, flat_in, pre_attn)[1](grad_normed)
    input_grad = (grad_resid + grad_in).astype(jnp.bfloat16).reshape(groups, rows, D)
    gain_terms = jnp.concatenate(
        [grad_pre_attn, grad_post_attn, grad_pre_ffw, grad_post_ffw, grad_query_gain, grad_key_gain]
    )
    lefts = (normed, low_one, ffw_in, low_two)
    rights = (low_projected, attended, low_gate_up, hidden)
    return (input_grad, gain_terms, lefts, rights)


def column_band(lefts, rights):
    every_left = jax.tree.map(
        lambda part, own: part.astype(own.dtype),
        lax.all_gather(shortened(lefts), "fsdp", axis=0, tiled=True),
        lefts,
    )
    every_right = jax.tree.map(
        lambda part, own: part.astype(own.dtype),
        lax.all_to_all(shortened(rights), "fsdp", split_axis=1, concat_axis=0, tiled=True),
        rights,
    )
    parts = [
        lax.dot_general(left, right, (((0,), (0,)), ((), ())), preferred_element_type=jnp.float32)
        for left, right in zip(every_left, every_right)
    ]
    widths = [piece.shape[1] for piece in parts]
    local_cols = jnp.concatenate(parts, axis=1)
    bands = lax.all_to_all(
        local_cols.astype(jnp.bfloat16), "fsdp", split_axis=0, concat_axis=1, tiled=True
    ).astype(local_cols.dtype)
    fsdp_count = lax.axis_size("fsdp")
    grouped = bands.reshape(bands.shape[0], fsdp_count, sum(widths))
    ordered = []
    offset = 0
    for width in widths:
        ordered.append(
            grouped[:, :, offset : offset + width].reshape(bands.shape[0], fsdp_count * width)
        )
        offset = offset + width
    return jnp.concatenate(ordered, axis=1)


def local(
    tokens,
    cotangent,
    lengths,
    master,
    gains,
    gain_stats,
    owner,
    stat_left,
    stat_right,
    root_left,
    root_right,
):
    micro_count = tokens.shape[0]
    rows = tokens.shape[2]
    band = master.shape[0]
    first = lax.axis_index("fsdp") * rows
    low_master = master.astype(jnp.bfloat16)
    outputs = []
    input_grads = []
    gain_sum = jnp.zeros(gains.shape, jnp.float32)
    all_lefts = []
    all_rights = []
    for micro in range(micro_count):
        forward_weights = lax.all_gather(low_master, "fsdp", axis=0, tiled=True)
        result, kept = forward_step(tokens[micro], lengths[micro], forward_weights, gains, first)
        backward_weights = lax.all_gather(low_master, "fsdp", axis=0, tiled=True)
        input_grad, gain_terms, lefts, rights = backward_step(
            cotangent[micro], kept, backward_weights, gains
        )
        outputs.append(result)
        input_grads.append(input_grad)
        gain_sum = gain_sum + gain_terms
        all_lefts.append(lefts)
        all_rights.append(rights)
    joined_lefts = tuple(
        (jnp.concatenate([entry[which] for entry in all_lefts], axis=0) for which in range(4))
    )
    joined_rights = tuple(
        (jnp.concatenate([entry[which] for entry in all_rights], axis=0) for which in range(4))
    )
    grad_band = column_band(joined_lefts, joined_rights)
    gain_grad = lax.psum(gain_sum, ("dp", "fsdp"))
    dp_count = lax.axis_size("dp")
    capacity = stat_left.shape[1]
    owners = owner[:, 0]
    member = (owners[:, None] == jnp.arange(dp_count, dtype=jnp.int32)[None, :]).astype(jnp.int32)
    ranks = jnp.sum((jnp.cumsum(member, axis=0) - 1) * member, axis=1)
    slot = owners * capacity + ranks
    every_slot = (
        slot[None, :] == jnp.arange(dp_count * capacity, dtype=jnp.int32)[:, None]
    ).astype(jnp.float32)
    blocks = grad_band.reshape(band, NBLK, BC).transpose(1, 0, 2)
    slot_terms = jnp.einsum("sb,brc->src", every_slot, blocks, precision=HIGHEST)
    slot_grads = lax.psum_scatter(
        slot_terms.astype(jnp.bfloat16), "dp", scatter_dimension=0, tiled=True
    ).astype(jnp.float32)
    new_left = DECAY * stat_left[0] + (1.0 - DECAY) * jnp.einsum(
        "src,stc->srt", slot_grads, slot_grads, precision=HIGHEST
    )
    new_right = DECAY * stat_right[0] + (1.0 - DECAY) * jnp.einsum(
        "src,srd->scd", slot_grads, slot_grads, precision=HIGHEST
    )
    shaped = jnp.einsum(
        "srt,stc->src", root_left[0].astype(jnp.float32), slot_grads, precision=HIGHEST
    )
    shaped = jnp.einsum(
        "src,scd->srd", shaped, root_right[0].astype(jnp.float32), precision=HIGHEST
    )
    factor = lax.rsqrt(jnp.mean(shaped * shaped, axis=(1, 2), keepdims=True) + EPSILON)
    changes = -RATE * shaped * factor
    every_change = lax.all_gather(changes.astype(jnp.bfloat16), "dp", axis=0, tiled=True).astype(
        changes.dtype
    )
    placed = jnp.take(every_change, slot, axis=0)
    new_master = master + placed.transpose(1, 0, 2).reshape(band, NBLK * BC)
    new_weights = new_master.astype(jnp.bfloat16)
    new_gain_stats = DECAY * gain_stats + (1.0 - DECAY) * gain_grad * gain_grad
    gain_change = -GAIN_RATE * gain_grad * lax.rsqrt(new_gain_stats)
    return (
        jnp.stack(outputs),
        jnp.stack(input_grads),
        slot_grads[None],
        gain_grad,
        new_left[None],
        new_right[None],
        new_master,
        new_weights,
        new_gain_stats,
        gain_change,
    )


def solution(mesh):
    in_specs = (
        P(None, "dp", "fsdp", None),
        P(None, "dp", "fsdp", None),
        P(None, "dp", None),
        P("fsdp", None),
        P(),
        P(),
        P("fsdp", None),
        P("fsdp", "dp", None, None),
        P("fsdp", "dp", None, None),
        P("fsdp", "dp", None, None),
        P("fsdp", "dp", None, None),
    )
    out_specs = (
        P(None, "dp", "fsdp", None),
        P(None, "dp", "fsdp", None),
        P("fsdp", "dp", None, None),
        P(),
        P("fsdp", "dp", None, None),
        P("fsdp", "dp", None, None),
        P("fsdp", None),
        P("fsdp", None),
        P(),
        P(),
    )
    return jax.shard_map(local, mesh=mesh, in_specs=in_specs, out_specs=out_specs, check_vma=False)
```

profile of v0, /device:TPU:0, one launch (start us, length us, event | category | flops | bytes accessed | tf_op | source)
XLA Modules:
  0.0 3225.0 jit_solution(2291056606752038479)
XLA Ops:
  19.3 1014.3 %all-gather.13.cloned.1.call-done = bf16[1152,23296]{1,0:T(8,128)(2,1)} async-done(((bf16[144,23296]{1,0:T(8,128)(2,1)}), bf16[1152,23296]{1,0:T(8,128)(2,1)}) %all-gather.13.cloned.1.call-update) | async-done | bytes 53674000 | tf_op jit(solution)/shard_map/all_gather | solution.py:324
  1064.0 20.4 all-gather.15.cloned.1.call-done
  1092.3 33.8 %all-gather.29.cloned.1.call-done = bf16[2048,256]{1,0:T(8,128)(2,1)} async-done(((bf16[256,256]{1,0:T(8,128)(2,1)}), bf16[2048,256]{1,0:T(8,128)(2,1)}) %all-gather.29.cloned.1.call-update) | async-done | bytes 1048592 | tf_op jit(solution)/shard_map/all_gather | solution.py:126
  1136.7 30.3 all-gather.17.cloned.1.call-done
  1174.0 33.9 %all-gather.31.cloned.1.call-done = bf16[2048,256]{1,0:T(8,128)(2,1)} async-done(((bf16[256,256]{1,0:T(8,128)(2,1)}), bf16[2048,256]{1,0:T(8,128)(2,1)}) %all-gather.31.cloned.1.call-update) | async-done | bytes 1048592 | tf_op jit(solution)/shard_map/all_gather | solution.py:126
  1220.1 18.2 fusion.6
  1258.2 18.5 fusion.4
  1335.1 18.7 fusion
  1353.8 20.2 multiply_reduce_fusion.5
  1439.2 17.8 reduce-scatter.6.cloned.1.call-done
  1458.7 67.4 %reduce-scatter.10.cloned.1.call-done = bf16[1,256,256]{2,1,0:T(8,128)(2,1)} async-done(((bf16[1,2048,256]{2,1,0:T(8,128)(2,1)}), bf16[1,256,256]{2,1,0:T(8,128)(2,1)}) %reduce-scatter.10.cloned.1.call-update) | async-done | bytes 131088 | tf_op jit(solution)/shard_map/reduce_scatter | solution.py:238
  1527.7 64.2 %reduce-scatter.12.cloned.1.call-done = bf16[1,256,256]{2,1,0:T(8,128)(2,1)} async-done(((bf16[1,2048,256]{2,1,0:T(8,128)(2,1)}), bf16[1,256,256]{2,1,0:T(8,128)(2,1)}) %reduce-scatter.12.cloned.1.call-update) | async-done | bytes 131088 | tf_op jit(solution)/shard_map/reduce_scatter | solution.py:241
  1600.8 58.0 %reduce-scatter.8.cloned.1.call-done = bf16[1,256,256]{2,1,0:T(8,128)(2,1)} async-done(((bf16[1,2048,256]{2,1,0:T(8,128)(2,1)}), bf16[1,256,256]{2,1,0:T(8,128)(2,1)}) %reduce-scatter.8.cloned.1.call-update) | async-done | bytes 131088 | tf_op jit(solution)/shard_map/reduce_scatter | solution.py:241
  1687.2 54.9 %all-to-all-done = bf16[512,8,192]{0,2,1:T(8,128)(2,1)S(1)} async-done(((bf16[512,8,192]{0,2,1:T(8,128)(2,1)}), bf16[512,8,192]{0,2,1:T(8,128)(2,1)S(1)}, u32[]{:S(2)}, u32[]{:S(2)}) %all-to-all-start) | async-done | bytes 1572896 | tf_op jit(solution)/shard_map/all_to_all | solution.py:276
  1786.2 228.7 %all-to-all-done.3 = bf16[512,8,864]{0,2,1:T(8,128)(2,1)} async-done(((bf16[512,8,864]{0,2,1:T(8,128)(2,1)}), bf16[512,8,864]{0,2,1:T(8,128)(2,1)}, u32[]{:S(2)}, u32[]{:S(2)}) %all-to-all-start.3) | async-done | bytes 7077920 | tf_op jit(solution)/shard_map/all_to_all | solution.py:276
  2071.9 127.8 %all-gather.21.cloned.1.call-done = bf16[4096,1152]{1,0:T(8,128)(2,1)} async-done(((bf16[512,1152]{1,0:T(8,128)(2,1)}), bf16[4096,1152]{1,0:T(8,128)(2,1)}) %all-gather.21.cloned.1.call-update) | async-done | bytes 9437200 | tf_op jit(solution)/shard_map/all_gather | solution.py:271
  2212.3 305.2 %all-gather.23.cloned.1.call-done = bf16[4096,1152]{1,0:T(8,128)(2,1)} async-done(((bf16[512,1152]{1,0:T(8,128)(2,1)}), bf16[4096,1152]{1,0:T(8,128)(2,1)}) %all-gather.23.cloned.1.call-update) | async-done | bytes 9437200 | tf_op jit(solution)/shard_map/all_gather | solution.py:271
  2530.5 124.9 %all-gather.25.cloned.1.call-done = bf16[4096,1152]{1,0:T(8,128)(2,1)} async-done(((bf16[512,1152]{1,0:T(8,128)(2,1)}), bf16[4096,1152]{1,0:T(8,128)(2,1)}) %all-gather.25.cloned.1.call-update) | async-done | bytes 9437200 | tf_op jit(solution)/shard_map/all_gather | solution.py:271
  2688.2 34.3 %copy.309 = bf16[8,512,1728]{1,0,2:T(8,128)(2,1)} copy(bf16[8,512,1728]{1,2,0:T(8,128)(2,1)} %bitcast.69) | data formatting | bytes 28311552 | tf_op jit(solution)/shard_map/all_to_all | solution.py:276
  2722.5 21.9 reshape.1266
  2744.4 24.8 convolution_convert_fusion
  2788.4 146.6 %all-to-all-done.4 = bf16[8,144,2912]{2,1,0:T(8,128)(2,1)} async-done(((bf16[8,144,2912]{2,1,0:T(8,128)(2,1)}), bf16[8,144,2912]{2,1,0:T(8,128)(2,1)}, u32[]{:S(2)}, u32[]{:S(2)}) %all-to-all-start.4) | async-done | bytes 6709280 | tf_op jit(solution)/shard_map/all_to_all | solution.py:285
  3025.4 72.0 %reduce-scatter.14.cloned.1.call-done = bf16[57,144,128]{2,1,0:T(8,128)(2,1)} async-done(((bf16[228,144,128]{2,1,0:T(8,128)(2,1)}), bf16[57,144,128]{2,1,0:T(8,128)(2,1)}) %reduce-scatter.14.cloned.1.call-update) | async-done | bytes 2101264 | tf_op jit(solution)/shard_map/reduce_scatter | solution.py:354
  3116.5 40.3 %psum.7 = f32[5120]{0:T(1024)S(1)} all-reduce(f32[5120]{0:T(1024)S(1)} %add.486), channel_id=1, replica_groups=mesh['dp'=4,'fsdp'=8] {'dp','fsdp'}, use_global_device_ids=true, to_apply=%region_52.53 | all-reduce | flops 5120 | bytes 40960 | tf_op jit(solution)/shard_map/psum | solution.py:342
  (511 shorter events, 611.2 us)
Async XLA Ops:
  7.2 3094.4 %copy-start = (bf16[1,57,128,128]{3,2,1,0:T(8,128)(2,1)S(1)}, bf16[1,57,128,128]{3,2,1,0:T(8,128)(2,1)}, u32[]{:S(2)}) copy-start(bf16[1,57,128,128]{3,2,1,0:T(8,128)(2,1)} %param.21) | copy-start | bytes 5603332
  7.2 1026.4 %all-gather.13.cloned.1.call-start = ((), (), s32[]{:S(2)}) async-start(), calls=%async_computation.10 | async-start | bytes 60383232 | tf_op jit(solution)/shard_map/all_gather | solution.py:324
  15.7 1068.8 %all-gather.15.cloned.1.call-start = ((), (), s32[]{:S(2)}) async-start(), calls=%async_computation.11 | async-start | bytes 1179648 | tf_op jit(solution)/shard_map/all_gather | solution.py:125
  15.8 1026.4 %copy-start.125 = (f32[128]{0:T(128)}, f32[128]{0:T(128)S(1)}, u32[]{:S(2)}) copy-start(f32[128]{0:T(128)S(1)} %multiply_power_fusion) | copy-start | bytes 1540
  17.9 1044.2 %copy-start.95 = (f32[256]{0:T(256)}, f32[256]{0:T(256)S(1)}, u32[]{:S(2)}) copy-start(f32[256]{0:T(256)S(1)} %get-tuple-element.119) | copy-start | bytes 3076
  17.9 1199.2 %copy-start.63 = (f32[1152]{0:T(1024)}, f32[1152]{0:T(1024)S(1)}, u32[]{:S(2)}) copy-start(f32[1152]{0:T(1024)S(1)} %get-tuple-element.116) | copy-start | bytes 13828
  1044.2 81.9 %all-gather.29.cloned.1.call-start = ((), (), s32[]{:S(2)}) async-start(), calls=%async_computation.23 | async-start | bytes 1179648 | tf_op jit(solution)/shard_map/all_gather | solution.py:126
  1045.0 122.1 %all-gather.17.cloned.1.call-start = ((), (), s32[]{:S(2)}) async-start(), calls=%async_computation.12 | async-start | bytes 1179648 | tf_op jit(solution)/shard_map/all_gather | solution.py:125
  1046.6 161.3 %all-gather.31.cloned.1.call-start = ((), (), s32[]{:S(2)}) async-start(), calls=%async_computation.24 | async-start | bytes 1179648 | tf_op jit(solution)/shard_map/all_gather | solution.py:126
  1061.8 395.3 %reduce-scatter.6.cloned.1.call-start = ((), (), s32[]{:S(2)}) async-start(), calls=%async_computation.13 | async-start | bytes 1179648 | tf_op jit(solution)/shard_map/reduce_scatter | solution.py:238
  1391.5 134.7 %reduce-scatter.10.cloned.1.call-start = ((), (), s32[]{:S(2)}) async-start(), calls=%async_computation.15 | async-start | bytes 1179648 | tf_op jit(solution)/shard_map/reduce_scatter | solution.py:238
  1406.7 185.3 %reduce-scatter.12.cloned.1.call-start = ((), (), s32[]{:S(2)}) async-start(), calls=%async_computation.16 | async-start | bytes 1179648 | tf_op jit(solution)/shard_map/reduce_scatter | solution.py:241
  1413.2 245.6 %reduce-scatter.8.cloned.1.call-start = ((), (), s32[]{:S(2)}) async-start(), calls=%async_computation.14 | async-start | bytes 1179648 | tf_op jit(solution)/shard_map/reduce_scatter | solution.py:241
  1419.4 604.1 %all-gather.19.cloned.1.call-start = ((), (), s32[]{:S(2)}) async-start(), calls=%async_computation.17 | async-start | bytes 10616832 | tf_op jit(solution)/shard_map/all_gather | solution.py:271
  1421.9 777.8 %all-gather.21.cloned.1.call-start = ((), (), s32[]{:S(2)}) async-start(), calls=%async_computation.18 | async-start | bytes 10616832 | tf_op jit(solution)/shard_map/all_gather | solution.py:271
  1435.6 230.0 %all-to-all-start.1 = ((bf16[512,8,128]{0,2,1:T(8,128)(2,1)}), bf16[512,8,128]{0,2,1:T(8,128)(2,1)S(1)}, u32[]{:S(2)}, u32[]{:S(2)}) async-start(bf16[512,8,128]{0,2,1:T(8,128)(2,1)} %pad_maximum_fusion.9), calls=%async_computation.5 | async-start | bytes 2097152 | tf_op jit(solution)/shard_map/all_to_all | solution.py:276
  1666.6 75.5 %all-to-all-start = ((bf16[512,8,192]{0,2,1:T(8,128)(2,1)}), bf16[512,8,192]{0,2,1:T(8,128)(2,1)S(1)}, u32[]{:S(2)}, u32[]{:S(2)}) async-start(bf16[512,8,192]{0,2,1:T(8,128)(2,1)} %pad_maximum_fusion.2), calls=%async_computation.4 | async-start | bytes 3145728 | tf_op jit(solution)/shard_map/all_to_all | solution.py:276
  1742.1 272.7 %all-to-all-start.3 = ((bf16[512,8,864]{0,2,1:T(8,128)(2,1)}), bf16[512,8,864]{0,2,1:T(8,128)(2,1)}, u32[]{:S(2)}, u32[]{:S(2)}) async-start(bf16[512,8,864]{0,2,1:T(8,128)(2,1)} %bitcast.298), calls=%async_computation.7 | async-start | bytes 14155776 | tf_op jit(solution)/shard_map/all_to_all | solution.py:276
  1747.0 770.5 %all-gather.23.cloned.1.call-start = ((), (), s32[]{:S(2)}) async-start(), calls=%async_computation.19 | async-start | bytes 10616832 | tf_op jit(solution)/shard_map/all_gather | solution.py:271
  2014.8 673.4 %all-to-all-start.2 = ((bf16[512,8,1728]{0,2,1:T(8,128)(2,1)}), bf16[512,8,1728]{0,2,1:T(8,128)(2,1)}, u32[]{:S(2)}, u32[]{:S(2)}) async-start(bf16[512,8,1728]{0,2,1:T(8,128)(2,1)} %maximum_maximum_fusion), calls=%async_computation.6 | async-start | bytes 28311552 | tf_op jit(solution)/shard_map/all_to_all | solution.py:276
  2020.7 634.8 %all-gather.25.cloned.1.call-start = ((), (), s32[]{:S(2)}) async-start(), calls=%async_computation.20 | async-start | bytes 10616832 | tf_op jit(solution)/shard_map/all_gather | solution.py:271
  2781.4 153.5 %all-to-all-start.4 = ((bf16[8,144,2912]{2,1,0:T(8,128)(2,1)}), bf16[8,144,2912]{2,1,0:T(8,128)(2,1)}, u32[]{:S(2)}, u32[]{:S(2)}) async-start(bf16[8,144,2912]{2,1,0:T(8,128)(2,1)} %concatenate.141), calls=%async_computation.8 | async-start | bytes 13565952 | tf_op jit(solution)/shard_map/all_to_all | solution.py:285
  2786.4 311.1 %reduce-scatter.14.cloned.1.call-start = ((), (), s32[]{:S(2)}) async-start(), calls=%async_computation.21 | async-start | bytes 10506240 | tf_op jit(solution)/shard_map/reduce_scatter | solution.py:354
  3025.2 148.2 %all-gather.27.cloned.1.call-start = ((), (), s32[]{:S(2)}) async-start(), calls=%async_computation.22 | async-start | bytes 10506240 | tf_op jit(solution)/shard_map/all_gather | solution.py:371
  (133 other events, 7601.8 us)
Sparse Core Ops, SparseCore 0:
  15.8 1017.6 all-gather.12
  1044.3 40.1 all-gather.14
  1087.2 38.8 all-gather.28
  1128.1 38.8 all-gather.16
  1169.0 38.8 all-gather.30
  1391.6 65.4 reduce-scatter.5
  1460.8 65.2 reduce-scatter.9
  1529.5 62.3 reduce-scatter.11
  1596.3 62.4 reduce-scatter.7
  1661.4 280.2 all-gather.18
  1944.4 255.2 all-gather.20
  2201.8 315.7 all-gather.22
  2520.3 135.1 all-gather.24
  3025.3 72.0 reduce-scatter.13
  3106.1 59.7 all-gather.26
where the time goes:
time: 3240 us; the launch traced here: 3220 us
  waiting for transfers between devices  2400 us (74%)
  local copies, waits for them, and re-layouts  300 us (9%)
  matrix products  288 us (9%)
  other arithmetic  155 us (5%)
  blocking collectives  40.3 us (1%)
    all_gather x1, waiting for transfers between devices, local(): forward_weights = lax.all_gather(low_master, 'fsdp', axis=0, tiled=True)  1010 us
    all_gather x4, waiting for transfers between devices, column_band(): lax.all_gather(shortened(lefts), 'fsdp', axis=0, tiled=True)  558 us
    all_to_all x4, waiting for transfers between devices, column_band(): lax.all_to_all(shortened(rights), 'fsdp', split_axis=1, concat_axis=0, ti...  284 us
    all_to_all x1, waiting for transfers between devices, column_band(): lax.all_to_all(local_cols.astype(jnp.bfloat16), 'fsdp', split_axis=0, con...  147 us
    reduce_scatter x2, waiting for transfers between devices, backward_step(): lax.psum_scatter(value_terms.astype(jnp.bfloat16), 'fsdp', scatter_dimens...  122 us
    reduce_scatter x2, waiting for transfers between devices, backward_step(): lax.psum_scatter(key_terms.astype(jnp.bfloat16), 'fsdp', scatter_dimensio...  85.3 us
    all_to_all x7, local copies, waits for them, and re-layouts, column_band(): lax.all_to_all(shortened(rights), 'fsdp', split_axis=1, concat_axis=0, ti...  84.7 us
    dot_general x8, matrix products, contract_last(): lax.dot_general(left, right, (((1,), (1,)), ((), ())), preferred_element_...  79.1 us
  transfers between devices with their start and end apart: 20, of which 16 were waited for; matrix products, arithmetic and copies ran while one was open for 9% of the time, Pallas kernels for 0%

commit v1 on v0

v1 whole, which is shorter than its diff:
```python
import jax
import jax.numpy as jnp
import numpy as np
from jax import lax
from jax.sharding import PartitionSpec as P

D = 1152
HEADS = 4
HD = 256
FF = 6912
WIN = 512
PROMPT = 1024
CONT = 8
CLEN = 128
BC = 128
GLEN = 2048
QKVW = 1536
OUTW = HEADS * HD
NBLK = 182
ATTN_BLOCKS = (QKVW + OUTW) // BC
FF_BLOCKS = FF // BC

EPSILON = 1e-06
MASKED = -1e30
RATE = 0.02
GAIN_RATE = 0.05
DECAY = 0.5
SCALE = HD ** (-0.5)
MAX_ROUNDS = 16
BF = jnp.bfloat16
F32 = jnp.float32


def rms_gain(values, gain):
    return values * lax.rsqrt(jnp.mean(values * values, axis=-1, keepdims=True) + EPSILON) * gain


def rope_tables(positions):
    half_width = HD // 2
    freqs = 10000.0 ** (-2.0 * jnp.arange(half_width, dtype=F32) / HD)
    angles = positions.astype(F32)[:, None] * freqs[None, :]
    return (jnp.cos(angles), jnp.sin(angles))


def rotate(values, cosine, sine):
    half_width = values.shape[-1] // 2
    first_half = values[..., :half_width]
    second_half = values[..., half_width:]
    return jnp.concatenate(
        [first_half * cosine - second_half * sine, second_half * cosine + first_half * sine],
        axis=-1,
    )


def slot_layout(slots):
    in_prompt = slots < PROMPT
    offset = slots - PROMPT
    segment = jnp.where(in_prompt, -1, offset // CLEN)
    position = jnp.where(in_prompt, slots, PROMPT + offset % CLEN)
    return (segment, position)


def visibility(query_slots, key_slots, lens):
    query_seg, query_pos = slot_layout(query_slots)
    key_seg, key_pos = slot_layout(key_slots)
    picks = key_seg[:, None] == jnp.arange(CONT, dtype=jnp.int32)[None, :]
    key_len = jnp.sum(jnp.where(picks, lens[None, :], 0), axis=1)
    key_used = (key_seg < 0) | (key_pos - PROMPT < key_len)
    distance = query_pos[:, None] - key_pos[None, :]
    same_part = (key_seg[None, :] < 0) | (key_seg[None, :] == query_seg[:, None])
    present = key_slots >= 0
    return (distance >= 0) & (distance < WIN) & same_part & (key_used & present)[None, :]


def split_gains(gains):
    return (
        gains[:D],
        gains[D : 2 * D],
        gains[2 * D : 3 * D],
        gains[3 * D : 4 * D],
        gains[4 * D : 4 * D + HD],
        gains[4 * D + HD :],
    )


def prepare_heads(queries, keys, query_gain, key_gain, cosine, sine):
    rot_queries = rotate(rms_gain(queries, query_gain), cosine[:, None, :], sine[:, None, :])
    rot_keys = rotate(rms_gain(keys, key_gain), cosine, sine)
    return (rot_queries, rot_keys)


def dot_nn(left, right):
    return jnp.dot(left, right, preferred_element_type=F32)


def dot_nt(left, right):
    return lax.dot_general(left, right, (((1,), (1,)), ((), ())), preferred_element_type=F32)


def dot_tn(left, right):
    return lax.dot_general(left, right, (((0,), (0,)), ((), ())), preferred_element_type=F32)


def swap_core(value, nd):
    return lax.ppermute(value, "dp", [(e, e ^ 1) for e in range(nd)])


def shift_x(value, nd, step):
    nx = nd // 2
    pairs = [(e, ((e // 2 + step) % nx) * 2 + e % 2) for e in range(nd)]
    return lax.ppermute(value, "dp", pairs)


def gather_parts(value, nd):
    mine = [value] + [shift_x(value, nd, k) for k in range(1, nd // 2)]
    return mine + [swap_core(part, nd) for part in mine]


def gather_dp(value, nd):
    return jnp.concatenate(gather_parts(value, nd), axis=0)


def part_owners(nd):
    nx = nd // 2
    me = lax.axis_index("dp")
    x, core = me // 2, me % 2
    out = []
    for flip in range(2):
        for k in range(nx):
            out.append(((x + nx - k) % nx) * 2 + (core if flip == 0 else 1 - core))
    return out


def scatter_sum_dp(own_half, other_half, nd):
    nx = nd // 2
    received = swap_core(other_half.astype(BF), nd)
    total = own_half + received.astype(F32)
    rows = total.shape[0] // nx
    result = total[:rows]
    for k in range(1, nx):
        sent = total[k * rows : (k + 1) * rows].astype(BF)
        result = result + shift_x(sent, nd, nx - k).astype(F32)
    return result


def sum_everywhere(value, nd, nf):
    for axis, count in (("dp", nd), ("fsdp", nf)):
        step = 1
        while step < count:
            value = value + lax.ppermute(value, axis, [(e, e ^ step) for e in range(count)])
            step *= 2
    return value


def key_plan(nf):
    rows = GLEN // nf
    slots = np.arange(GLEN)
    seg = np.where(slots < PROMPT, -1, (slots - PROMPT) // CLEN)
    pos = np.where(slots < PROMPT, slots, PROMPT + (slots - PROMPT) % CLEN)
    dist = pos[:, None] - pos[None, :]
    vis = (dist >= 0) & (dist < WIN) & ((seg[None, :] < 0) | (seg[None, :] == seg[:, None]))
    need = vis.reshape(nf, rows, nf, rows).any(axis=(1, 3))
    sources = [[u for u in reversed(range(nf)) if need[t, u] and u != t] for t in range(nf)]
    count = max(len(s) for s in sources)
    plan, tables = [], []
    for k in range(count):
        edges = [(s[k], t) for t, s in enumerate(sources) if len(s) > k]
        rounds = []
        while edges:
            used, now, later = set(), [], []
            for src, dst in edges:
                if src in used:
                    later.append((src, dst))
                else:
                    used.add(src)
                    now.append((src, dst))
            rounds.append(now)
            edges = later
        plan.append(rounds)
        tables.append([s[k] if len(s) > k else -1 for s in sources])
    return (plan, tables)


def pick_static(table, index):
    values = jnp.asarray(table, jnp.int32)
    hit = jnp.arange(len(table), dtype=jnp.int32) == index
    return jnp.sum(jnp.where(hit, values, 0))


def spread_keys(own, nf):
    rows = own.shape[1]
    me = lax.axis_index("fsdp")
    step = jnp.arange(rows, dtype=jnp.int32)
    plan, tables = key_plan(nf)
    if sum(len(r) for r in plan) > MAX_ROUNDS:
        return (
            lax.all_gather(own, "fsdp", axis=1, tiled=True),
            jnp.arange(rows * nf, dtype=jnp.int32),
        )
    parts, ids = [own], [me * rows + step]
    for rounds, table in zip(plan, tables):
        got = [lax.ppermute(own, "fsdp", pairs) for pairs in rounds]
        total = got[0]
        for more in got[1:]:
            total = total + more
        source = pick_static(table, me)
        parts.append(total)
        ids.append(jnp.where(source >= 0, source * rows + step, -1))
    return (jnp.concatenate(parts, axis=1), jnp.concatenate(ids))


def return_key_grads(terms, rows, nf):
    plan, _ = key_plan(nf)
    if sum(len(r) for r in plan) > MAX_ROUNDS:
        return lax.psum_scatter(
            terms.astype(BF), "fsdp", scatter_dimension=1, tiled=True
        ).astype(F32)
    total = terms[:, :rows]
    for k, rounds in enumerate(plan):
        sent = terms[:, (k + 1) * rows : (k + 2) * rows].astype(BF)
        for pairs in rounds:
            back = lax.ppermute(sent, "fsdp", [(dst, src) for src, dst in pairs])
            total = total + back.astype(F32)
    return total


def attend(query_low, keys, values, visible):
    scores = jnp.einsum("thd,kd->thk", query_low, keys, preferred_element_type=F32) * SCALE
    scores = jnp.where(visible[:, None, :], scores, MASKED)
    highest = jnp.max(scores, axis=-1, keepdims=True)
    expo = jnp.exp(scores - highest)
    probs = expo / jnp.sum(expo, axis=-1, keepdims=True)
    mixed = jnp.einsum("thk,kd->thd", probs.astype(BF), values, preferred_element_type=F32)
    return (mixed, probs)


def attend_back(query_low, keys, values, probs, low_mixed):
    grad_probs = jnp.einsum("thd,kd->thk", low_mixed, values, preferred_element_type=F32)
    row_dot = jnp.sum(grad_probs * probs, axis=-1, keepdims=True)
    grad_scores = (probs * (grad_probs - row_dot)).astype(BF)
    grad_queries = jnp.einsum("thk,kd->thd", grad_scores, keys, preferred_element_type=F32) * SCALE
    key_terms = (
        jnp.einsum("thk,thd->kd", grad_scores, query_low, preferred_element_type=F32) * SCALE
    )
    value_terms = jnp.einsum("thk,thd->kd", probs.astype(BF), low_mixed, preferred_element_type=F32)
    return (grad_queries, key_terms, value_terms)


def local(
    tokens,
    cotangent,
    lengths,
    master,
    gains,
    gain_stats,
    owner,
    stat_left,
    stat_right,
    root_left,
    root_right,
):
    nd = lax.axis_size("dp")
    nf = lax.axis_size("fsdp")
    dp_me = lax.axis_index("dp")
    core = dp_me % 2
    micros = tokens.shape[0]
    rows = tokens.shape[2]
    count = micros * rows
    band = master.shape[0]
    capacity = stat_left.shape[1]
    first = lax.axis_index("fsdp") * rows
    pre_attn, post_attn, pre_ffw, post_ffw, query_gain, key_gain = split_gains(gains)

    per = -(-FF_BLOCKS // nd)
    width = per * BC
    start = jnp.minimum(dp_me * per, FF_BLOCKS - per)
    fresh = dp_me * per - start
    gate_at = ATTN_BLOCKS * BC

    def columns(at, size):
        return lax.dynamic_slice(master, (0, at), (band, size)).astype(BF)

    def gather_rows(part):
        return lax.all_gather(part, "fsdp", axis=0, tiled=True)

    def halves(at, size):
        half = size // 2
        mine = gather_rows(columns(at + core * half, half))
        other = swap_core(mine, nd)
        whole = jnp.zeros((D, size), BF)
        whole = lax.dynamic_update_slice(whole, mine, (0, core * half))
        return lax.dynamic_update_slice(whole, other, (0, (1 - core) * half))

    w_qkv = halves(0, QKVW)
    w_out = halves(QKVW, OUTW)
    gate_cols = columns(gate_at + start * BC, width)
    up_cols = columns(gate_at + FF + start * BC, width)
    down_cols = columns(gate_at + 2 * FF + start * BC, width)
    keep = (jnp.arange(width, dtype=jnp.int32) >= fresh * BC)[None, :]
    down_cols = jnp.where(keep, down_cols, jnp.zeros_like(down_cols))
    w_gate = gather_rows(gate_cols)
    w_up = gather_rows(up_cols)
    w_down = gather_rows(down_cols)

    flat_in = tokens.astype(F32).reshape(count, D)
    normed = rms_gain(flat_in, pre_attn).astype(BF)
    projected = dot_nn(normed, w_qkv)
    queries = projected[:, :OUTW].reshape(count, HEADS, HD)
    keys = projected[:, OUTW : OUTW + HD]
    values = projected[:, OUTW + HD :]
    slots = first + jnp.arange(rows, dtype=jnp.int32)
    _, positions = slot_layout(slots)
    cosine, sine = rope_tables(positions)
    cosine, sine = (jnp.tile(cosine, (micros, 1)), jnp.tile(sine, (micros, 1)))
    rot_queries, rot_keys = prepare_heads(queries, keys, query_gain, key_gain, cosine, sine)
    query_low = rot_queries.astype(BF).reshape(micros, rows, HEADS, HD)
    own_keys = jnp.concatenate([rot_keys.astype(BF), values.astype(BF)], axis=1)
    key_buffer, key_slots = spread_keys(own_keys.reshape(micros, rows, 2 * HD), nf)
    keys_all, values_all = (key_buffer[..., :HD], key_buffer[..., HD:])
    all_probs, all_attended = [], []
    for m in range(micros):
        visible = visibility(slots, key_slots, lengths[m, 0])
        mixed, probs = attend(query_low[m], keys_all[m], values_all[m], visible)
        all_probs.append(probs)
        all_attended.append(mixed.reshape(rows, OUTW).astype(BF))

    half = (nd // 2) * rows
    outputs, saved, gathered_in, gathered_two, hiddens, low_gates, low_ups = [], [], [], [], [], [], []
    grad_resids, gain_terms, low_ones = [], [], []
    for m in range(micros):
        part_in = flat_in[m * rows : (m + 1) * rows]
        branch_one = dot_nt(all_attended[m], w_out)
        resid = part_in + rms_gain(branch_one, post_attn)
        ffw_in = rms_gain(resid, pre_ffw).astype(BF)
        every_in = gather_dp(ffw_in, nd)
        gate = dot_nn(every_in, w_gate)
        up = dot_nn(every_in, w_up)
        hidden = (jax.nn.gelu(gate, approximate=True) * up).astype(BF)
        partial = dot_nt(hidden, w_down)
        branch_two = scatter_sum_dp(partial[:half], partial[half:], nd)
        outputs.append((resid + rms_gain(branch_two, post_ffw)).astype(BF))
        gathered_in.append(every_in)
        hiddens.append(hidden)
        saved.append((branch_one, resid, gate, up, branch_two))
    for m in range(micros):
        branch_one, resid, gate, up, branch_two = saved[m]
        upstream = cotangent[m, 0].astype(F32)
        grad_two, grad_post_ffw = jax.vjp(rms_gain, branch_two, post_ffw)[1](upstream)
        every_two = gather_dp(grad_two.astype(BF), nd)
        grad_hidden = dot_nn(every_two, w_down)
        grad_gate, grad_up = jax.vjp(
            lambda gate_in, up_in: jax.nn.gelu(gate_in, approximate=True) * up_in, gate, up
        )[1](grad_hidden)
        low_gate, low_up = (grad_gate.astype(BF), grad_up.astype(BF))
        partial = dot_nt(low_gate, w_gate) + dot_nt(low_up, w_up)
        grad_ffw_in = scatter_sum_dp(partial[:half], partial[half:], nd)
        grad_resid, grad_pre_ffw = jax.vjp(rms_gain, resid, pre_ffw)[1](grad_ffw_in)
        grad_resid = upstream + grad_resid
        grad_one, grad_post_attn = jax.vjp(rms_gain, branch_one, post_attn)[1](grad_resid)
        gathered_two.append(every_two)
        low_gates.append(low_gate)
        low_ups.append(low_up)
        grad_resids.append(grad_resid)
        low_ones.append(grad_one.astype(BF))
        gain_terms.append((grad_post_attn, grad_pre_ffw, grad_post_ffw))

    def reduce_rows(lefts, rights):
        term = dot_tn(jnp.concatenate(lefts, axis=0), jnp.concatenate(rights, axis=0))
        return lax.psum_scatter(term.astype(BF), "fsdp", scatter_dimension=0, tiled=True)

    def blocks_of(part):
        return part.reshape(band, part.shape[1] // BC, BC).transpose(1, 0, 2)

    ff_bands = [
        reduce_rows(gathered_in, low_gates),
        reduce_rows(gathered_in, low_ups),
        reduce_rows(gathered_two, hiddens),
    ]
    ff_blocks = jnp.concatenate([blocks_of(part) for part in ff_bands], axis=0)

    low_one = jnp.concatenate(low_ones, axis=0)
    attended = jnp.concatenate(all_attended, axis=0)
    low_mixed = dot_nn(low_one, w_out).astype(BF).reshape(micros, rows, HEADS, HD)
    grad_queries, key_terms = [], []
    for m in range(micros):
        for_queries, for_keys, for_values = attend_back(
            query_low[m], keys_all[m], values_all[m], all_probs[m], low_mixed[m]
        )
        grad_queries.append(for_queries)
        key_terms.append(jnp.concatenate([for_keys, for_values], axis=1))
    own_terms = return_key_grads(jnp.stack(key_terms), rows, nf).reshape(count, 2 * HD)
    grad_keys, grad_values = (own_terms[:, :HD], own_terms[:, HD:])

    def heads_only(query_in, key_in, query_scale, key_scale):
        return prepare_heads(query_in, key_in, query_scale, key_scale, cosine, sine)

    pull_heads = jax.vjp(heads_only, queries, keys, query_gain, key_gain)[1]
    grad_query_pre, grad_key_pre, grad_query_gain, grad_key_gain = pull_heads(
        (jnp.concatenate(grad_queries, axis=0), grad_keys)
    )
    low_projected = jnp.concatenate(
        [grad_query_pre.reshape(count, OUTW), grad_key_pre, grad_values], axis=1
    ).astype(BF)
    grad_normed = dot_nt(low_projected, w_qkv)
    grad_in, grad_pre_attn = jax.vjp(rms_gain, flat_in, pre_attn)[1](grad_normed)
    input_grad = (jnp.concatenate(grad_resids, axis=0) + grad_in).astype(BF)

    attn_per = -(-ATTN_BLOCKS // nd)
    attn_width = attn_per * BC
    attn_term = jnp.concatenate([dot_tn(normed, low_projected), dot_tn(low_one, attended)], axis=1)
    attn_term = jnp.pad(attn_term, ((0, 0), (0, nd * attn_width - ATTN_BLOCKS * BC)))

    def owner_columns(index):
        return lax.dynamic_slice(attn_term, (0, index * attn_width), (D, attn_width))

    owners_at = part_owners(nd)
    attn_sum = scatter_sum_dp(
        jnp.concatenate([owner_columns(e) for e in owners_at[: nd // 2]], axis=0),
        jnp.concatenate([owner_columns(e) for e in owners_at[nd // 2 :]], axis=0),
        nd,
    )
    spread = lax.all_to_all(
        attn_sum.astype(BF).reshape(nf, band, attn_width), "fsdp", split_axis=0, concat_axis=0
    )
    attn_band = jnp.sum(spread.astype(F32), axis=0).astype(BF)

    def gather_blocks(part):
        pieces = gather_parts(part, nd)
        out = jnp.zeros((nd,) + part.shape, part.dtype)
        for piece, index in zip(pieces, part_owners(nd)):
            out = lax.dynamic_update_slice(out, piece[None], (index,) + (0,) * part.ndim)
        return out

    ff_all = gather_blocks(ff_blocks)
    attn_all = gather_blocks(blocks_of(attn_band))
    pieces = [attn_all.reshape((nd * attn_per, band, BC))[:ATTN_BLOCKS]]
    for kind in range(3):
        for e in range(nd):
            begin = min(e * per, FF_BLOCKS - per)
            skip = min(e * per - begin, per)
            pieces.append(ff_all[e, kind * per + skip : (kind + 1) * per])
    blocks = jnp.concatenate(pieces, axis=0)

    owners = owner[:, 0]
    index = jnp.arange(NBLK, dtype=jnp.int32)
    before = (owners[:, None] == owners[None, :]) & (index[None, :] < index[:, None])
    ranks = jnp.sum(before.astype(jnp.int32), axis=1)
    slot = owners * capacity + ranks
    my_slots = dp_me * capacity + jnp.arange(capacity, dtype=jnp.int32)
    pick_mine = (slot[None, :] == my_slots[:, None]).astype(BF)
    slot_low = jnp.einsum("sb,brc->src", pick_mine, blocks, preferred_element_type=F32)
    slot_grads = slot_low
    low_slots = slot_low.astype(BF)
    new_left = DECAY * stat_left[0] + (1.0 - DECAY) * jnp.einsum(
        "src,stc->srt", low_slots, low_slots, preferred_element_type=F32
    )
    new_right = DECAY * stat_right[0] + (1.0 - DECAY) * jnp.einsum(
        "src,srd->scd", low_slots, low_slots, preferred_element_type=F32
    )
    every_slot = jnp.arange(nd * capacity, dtype=jnp.int32)
    pick_root = (slot[:, None] == every_slot[None, :]).astype(BF)

    def roots_by_block(root):
        every = gather_blocks(root).reshape((nd * capacity,) + root.shape[1:])
        return jnp.einsum("bs,srt->brt", pick_root, every, preferred_element_type=F32).astype(BF)

    lefts = roots_by_block(root_left[0])
    rights = roots_by_block(root_right[0])
    shaped = jnp.einsum("brt,btc->brc", lefts, blocks, preferred_element_type=F32)
    shaped = jnp.einsum("brc,bcd->brd", shaped.astype(BF), rights, preferred_element_type=F32)
    factor = lax.rsqrt(jnp.mean(shaped * shaped, axis=(1, 2), keepdims=True) + EPSILON)
    changes = -RATE * shaped * factor
    new_master = master + changes.transpose(1, 0, 2).reshape(band, NBLK * BC)
    new_weights = new_master.astype(BF)

    post_attn_sum = sum(entry[0] for entry in gain_terms)
    pre_ffw_sum = sum(entry[1] for entry in gain_terms)
    post_ffw_sum = sum(entry[2] for entry in gain_terms)
    gain_sum = jnp.concatenate(
        [grad_pre_attn, post_attn_sum, pre_ffw_sum, post_ffw_sum, grad_query_gain, grad_key_gain]
    )
    gain_grad = sum_everywhere(gain_sum, nd, nf)
    new_gain_stats = DECAY * gain_stats + (1.0 - DECAY) * gain_grad * gain_grad
    gain_change = -GAIN_RATE * gain_grad * lax.rsqrt(new_gain_stats)
    return (
        jnp.stack(outputs)[:, None],
        input_grad.reshape(micros, 1, rows, D),
        slot_grads[None],
        gain_grad,
        new_left[None],
        new_right[None],
        new_master,
        new_weights,
        new_gain_stats,
        gain_change,
    )


def solution(mesh):
    in_specs = (
        P(None, "dp", "fsdp", None),
        P(None, "dp", "fsdp", None),
        P(None, "dp", None),
        P("fsdp", None),
        P(),
        P(),
        P("fsdp", None),
        P("fsdp", "dp", None, None),
        P("fsdp", "dp", None, None),
        P("fsdp", "dp", None, None),
        P("fsdp", "dp", None, None),
    )
    out_specs = (
        P(None, "dp", "fsdp", None),
        P(None, "dp", "fsdp", None),
        P("fsdp", "dp", None, None),
        P(),
        P("fsdp", "dp", None, None),
        P("fsdp", "dp", None, None),
        P("fsdp", None),
        P("fsdp", None),
        P(),
        P(),
    )
    return jax.shard_map(local, mesh=mesh, in_specs=in_specs, out_specs=out_specs, check_vma=False)
```

time: 3240 us -> 1130 us (0.35)
  waiting for transfers between devices: 2400 us -> 411 us
  starting transfers between devices: 24.4 us -> 88 us
  other arithmetic: 155 us -> 93.9 us
  local copies, waits for them, and re-layouts: 300 us -> 242 us
  blocking collectives: 40.3 us -> 0 us
    all_gather x10 -> x5, waiting for transfers between devices: 1690 us -> 225 us  [gather_rows(): return lax.all_gather(part, 'fsdp', axis=0, tiled=True)]
    all_to_all x5 -> x1, waiting for transfers between devices: 430 us -> 0.01 us  [local(): lax.all_to_all(attn_sum.astype(BF).reshape(nf, band, attn_width), 'fsdp',...]
    reduce_scatter x5 -> x3, waiting for transfers between devices: 279 us -> 0.04 us  [reduce_rows(): lax.psum_scatter(term.astype(BF), 'fsdp', scatter_dimension=0, tiled=True)]
    ppermute x0 -> x57, waiting for transfers between devices: none -> 185 us  [the longest x13 162 us: shift_x(): return lax.ppermute(value, 'dp', pairs)]
    all_to_all x7 -> x0, local copies, waits for them, and re-layouts: 84.7 us -> none  [column_band(): lax.all_to_all(shortened(rights), 'fsdp', split_axis=1, concat_axis=0, ti...]
    concatenate x4 -> x5, local copies, waits for them, and re-layouts: 22.6 us -> 87.5 us  [the longest x1 84.7 us: local(): blocks = jnp.concatenate(pieces, axis=0)]
    ppermute x0 -> x57, starting transfers between devices: none -> 51.3 us  [the longest x13 16.6 us: shift_x(): return lax.ppermute(value, 'dp', pairs)]
    dot_general x4 -> x0, local copies, waits for them, and re-layouts: 51 us -> none  [column_band(): lax.dot_general(left, right, (((0,), (0,)), ((), ())), preferred_element_...]
  transfers between devices with their start and end apart: 20 -> 66, of which waited for: 16 -> 24; matrix products, arithmetic and copies ran while one was open for 9% -> 34% of each run, Pallas kernels for 0% -> 0%
where the time goes in v1:
time: 1130 us; the launch traced here: 1120 us
  waiting for transfers between devices  411 us (36%)
  matrix products  263 us (23%)
  local copies, waits for them, and re-layouts  242 us (21%)
  other arithmetic  93.9 us (8%)
  starting transfers between devices  88 us (8%)
  between operations  20 us (2%)
    all_gather x5, waiting for transfers between devices, gather_rows(): return lax.all_gather(part, 'fsdp', axis=0, tiled=True)  225 us
    ppermute x13, waiting for transfers between devices, shift_x(): return lax.ppermute(value, 'dp', pairs)  162 us
    concatenate x1, local copies, waits for them, and re-layouts, local(): blocks = jnp.concatenate(pieces, axis=0)  84.7 us
    dot_general x8, matrix products, dot_nn(): return jnp.dot(left, right, preferred_element_type=F32)  80.7 us
    dot_general x9, matrix products, dot_nt(): lax.dot_general(left, right, (((1,), (1,)), ((), ())), preferred_element_...  52 us
    dot_general x5, matrix products, dot_tn(): lax.dot_general(left, right, (((0,), (0,)), ((), ())), preferred_element_...  42.6 us
    all_to_all x1, starting transfers between devices, local(): lax.all_to_all(attn_sum.astype(BF).reshape(nf, band, attn_width), 'fsdp',...  36.2 us
    dynamic_update_slice x15, local copies, waits for them, and re-layouts, gather_blocks(): lax.dynamic_update_slice(out, piece[None], (index,) + (0,) * part.ndim)  34.3 us
  transfers between devices with their start and end apart: 66, of which 24 were waited for; matrix products, arithmetic and copies ran while one was open for 34% of the time, Pallas kernels for 0%

profile of v1, /device:TPU:0, one launch (start us, length us, event | category | flops | bytes accessed | tf_op | source)
XLA Modules:
  0.0 1118.3 jit_solution(1695692490103576081)
XLA Ops:
  21.6 37.6 %all-gather.6.cloned.1.call-done = bf16[1152,768]{1,0:T(8,128)(2,1)} async-done(((bf16[144,768]{1,0:T(8,128)(2,1)}), bf16[1152,768]{1,0:T(8,128)(2,1)}) %all-gather.6.cloned.1.call-update) | async-done | bytes 1769488 | tf_op jit(solution)/shard_map/all_gather | solution.py:284
  59.5 42.5 %all-gather.8.cloned.1.call-done = bf16[1152,512]{1,0:T(8,128)(2,1)} async-done(((bf16[144,512]{1,0:T(8,128)(2,1)}), bf16[1152,512]{1,0:T(8,128)(2,1)}) %all-gather.8.cloned.1.call-update) | async-done | bytes 1179664 | tf_op jit(solution)/shard_map/all_gather | solution.py:284
  157.5 13.4 %collective-permute-done.10 = bf16[256,1152]{1,0:T(8,128)(2,1)S(1)} collective-permute-done((bf16[256,1152]{1,0:T(8,128)(2,1)S(1)}, bf16[256,1152]{1,0:T(8,128)(2,1)S(1)}, u32[]{:S(2)}, u32[]{:S(2)}) %collective-permute-start.10) | collective-permute-done | bytes 589856 | tf_op jit(solution)/shard_map/ppermute | solution.py:111
  176.6 13.9 %collective-permute-done.15 = bf16[256,1152]{1,0:T(8,128)(2,1)S(1)} collective-permute-done((bf16[256,1152]{1,0:T(8,128)(2,1)}, bf16[256,1152]{1,0:T(8,128)(2,1)S(1)}, u32[]{:S(2)}, u32[]{:S(2)}) %collective-permute-start.15) | collective-permute-done | bytes 589856 | tf_op jit(solution)/shard_map/ppermute | solution.py:111
  201.9 84.9 %all-gather.12.cloned.1.call-done = bf16[1152,1792]{1,0:T(8,128)(2,1)} async-done(((bf16[144,1792]{1,0:T(8,128)(2,1)}), bf16[1152,1792]{1,0:T(8,128)(2,1)}) %all-gather.12.cloned.1.call-update) | async-done | bytes 4128784 | tf_op jit(solution)/shard_map/all_gather | solution.py:284
  286.9 12.9 %multiply_convert_fusion.3 = (bf16[1024,1792]{1,0:T(8,128)(2,1)}, f32[1024,1792]{1,0:T(8,128)}) fusion(f32[1024,1792]{1,0:T(8,128)} %fusion.122, bf16[1152,1792]{1,0:T(8,128)(2,1)} %all-gather.12.cloned.1.call-done, bf16[256,1152]{1,0:T(8,128)(2,1)} %copy-done.69, bf16[256,1152]{1,0:T(8,128)(2,1)} %copy-done.68, bf16[256,1152]{1,0:T(8,128)(2,1)} %copy-done.67, ...), kind=kOutput, calls=%fused_computation.51 | convolution fusion | flops 4255645696 | bytes 24838144 | tf_op jit(solution)/shard_map/dot_general | solution.py:93
  299.8 60.0 %all-gather.14.cloned.1.call-done = bf16[1152,1792]{1,0:T(8,128)(2,1)} async-done(((bf16[144,1792]{1,0:T(8,128)(2,1)}), bf16[1152,1792]{1,0:T(8,128)(2,1)}) %all-gather.14.cloned.1.call-update) | async-done | bytes 4128784 | tf_op jit(solution)/shard_map/all_gather | solution.py:284
  378.0 12.0 %multiply_convert_fusion.2 = (bf16[1024,1792]{1,0:T(8,128)(2,1)}, f32[1024,1792]{1,0:T(8,128)}) fusion(f32[1024,1792]{1,0:T(8,128)} %fusion.120, bf16[1152,1792]{1,0:T(8,128)(2,1)S(1)} %copy-done.142, bf16[256,1152]{1,0:T(8,128)(2,1)} %collective-permute-done.17, bf16[256,1152]{1,0:T(8,128)(2,1)S(1)} %collective-permute-done.16, ...), kind=kOutput, calls=%fused_computation.50 | convolution fusion | flops 4255645696 | bytes 24838144 | tf_op jit(solution)/shard_map/dot_general | solution.py:93
  401.8 12.2 %collective-permute-done.14 = bf16[256,1152]{1,0:T(8,128)(2,1)S(1)} collective-permute-done((bf16[256,1152]{1,0:T(8,128)(2,1)S(1)}, bf16[256,1152]{1,0:T(8,128)(2,1)S(1)}, u32[]{:S(2)}, u32[]{:S(2)}) %collective-permute-start.14) | collective-permute-done | bytes 589856 | tf_op jit(solution)/shard_map/ppermute | solution.py:111
  430.7 13.0 %collective-permute-done.20 = bf16[256,1152]{1,0:T(8,128)(2,1)S(1)} collective-permute-done((bf16[256,1152]{1,0:T(8,128)(2,1)S(1)}, bf16[256,1152]{1,0:T(8,128)(2,1)S(1)}, u32[]{:S(2)}, u32[]{:S(2)}) %collective-permute-start.20) | collective-permute-done | bytes 589856 | tf_op jit(solution)/shard_map/ppermute | solution.py:111
  449.2 12.5 %collective-permute-done.25 = bf16[256,1152]{1,0:T(8,128)(2,1)S(1)} collective-permute-done((bf16[256,1152]{1,0:T(8,128)(2,1)S(1)}, bf16[256,1152]{1,0:T(8,128)(2,1)S(1)}, u32[]{:S(2)}, u32[]{:S(2)}) %collective-permute-start.25) | collective-permute-done | bytes 589856 | tf_op jit(solution)/shard_map/ppermute | solution.py:111
  461.7 15.8 %multiply_convert_fusion.1 = (bf16[1024,1792]{1,0:T(8,128)(2,1)}, bf16[1024,1792]{1,0:T(8,128)(2,1)}) fusion(f32[1024,1792]{1,0:T(8,128)} %fusion.122, f32[1024,1792]{1,0:T(8,128)} %get-tuple-element.195, bf16[1152,1792]{1,0:T(8,128)(2,1)S(1)} %copy-done.144, bf16[256,1152]{1,0:T(8,128)(2,1)S(1)} %collective-permute-done.22, ...), kind=kOutput, calls=%fused_computation.49 | convolution fusion | flops 4281335808 | bytes 28508160 | tf_op jit(solution)/shard_map/dot_general | solution.py:93
  477.5 15.4 %multiply_convert_fusion = (bf16[1024,1792]{1,0:T(8,128)(2,1)}, bf16[1024,1792]{1,0:T(8,128)(2,1)}) fusion(f32[1024,1792]{1,0:T(8,128)} %fusion.120, f32[1024,1792]{1,0:T(8,128)} %get-tuple-element.197, bf16[1152,1792]{1,0:T(8,128)(2,1)S(1)} %copy-done.144, bf16[256,1152]{1,0:T(8,128)(2,1)S(1)} %collective-permute-done.27, ...), kind=kOutput, calls=%fused_computation.48 | convolution fusion | flops 4281335808 | bytes 28508160 | tf_op jit(solution)/shard_map/dot_general | solution.py:93
  492.9 13.8 %convolution_convert_fusion.2 = bf16[1152,1792]{1,0:T(8,128)(2,1)} fusion(bf16[2048,1152]{1,0:T(8,128)(2,1)S(1)} %constant_dynamic-update-slice_fusion, bf16[1024,1792]{1,0:T(8,128)(2,1)} %get-tuple-element.127, bf16[1024,1792]{1,0:T(8,128)(2,1)} %get-tuple-element.125), kind=kOutput, calls=%fused_computation.24 | convolution fusion | flops 8472461312 | bytes 16187392 | tf_op jit(solution)/shard_map/dot_general | solution.py:101
  685.4 61.9 %collective-permute-done.51 = bf16[57,144,144]{2,1,0:T(8,128)(2,1)} collective-permute-done((bf16[57,144,144]{2,1,0:T(8,128)(2,1)}, bf16[57,144,144]{2,1,0:T(8,128)(2,1)}, u32[]{:S(2)}, u32[]{:S(2)}) %collective-permute-start.51) | collective-permute-done | bytes 2363936 | tf_op jit(solution)/shard_map/ppermute | solution.py:111
  758.9 18.9 %fusion.35 = bf16[182,128,128]{2,0,1:T(8,128)(2,1)} fusion(bf16[228,128,128]{2,1,0:T(8,128)(2,1)S(1)} %bitcast.280, s32[182]{0:T(256)S(1)} %bitcast.338), kind=kOutput, calls=%fused_computation.72 | convolution fusion | flops 1362764288 | bytes 13435608 | tf_op jit(solution)/shard_map/bs,srt->brt/dot_general | solution.py:465
  800.1 20.8 %copy.277 = bf16[228,144,144]{0,2,1:T(8,128)(2,1)} copy(bf16[228,144,144]{2,1,0:T(8,128)(2,1)} %bitcast.77) | data formatting | bytes 18911232 | tf_op jit(solution)/shard_map/reshape | solution.py:464
  827.4 36.2 %all-to-all-start = ((bf16[8,144,640]{2,1,0:T(8,128)(2,1)}), bf16[8,144,640]{2,1,0:T(8,128)(2,1)S(1)}, u32[]{:S(2)}, u32[]{:S(2)}) async-start(bf16[8,144,640]{2,1,0:T(8,128)(2,1)} %bitcast.294), calls=%async_computation | async-start | bytes 2949120 | tf_op jit(solution)/shard_map/all_to_all | solution.py:422
  875.0 14.1 %fusion.132 = f32[182,20736]{0,1} fusion(bf16[228,20736]{0,1:T(8,128)(2,1)} %bitcast.284, s32[182]{0:T(256)S(1)} %bitcast.339), kind=kOutput, calls=%fused_computation.323 | convolution fusion | flops 1720963584 | bytes 24552152
  889.1 12.1 %convert_element_type.278 = bf16[182,144,144]{0,2,1:T(8,128)(2,1)} convert(f32[182,144,144]{0,2,1:T(8,128)} %bitcast.277) | non-fusion elementwise | flops 3773952 | bytes 22643712 | tf_op jit(solution)/shard_map/convert_element_type | solution.py:465
  901.2 19.6 %copy.278 = bf16[182,144,144]{2,1,0:T(8,128)(2,1)} copy(bf16[182,144,144]{0,2,1:T(8,128)(2,1)} %convert_element_type.278) | data formatting | bytes 15095808 | tf_op jit(solution)/shard_map/convert_element_type | solution.py:465
  969.3 84.7 %concatenate.158 = bf16[182,144,128]{2,0,1:T(8,128)(2,1)} concatenate(bf16[20,144,128]{2,0,1:T(8,128)(2,1)S(1)} %copy.275, bf16[14,144,128]{2,0,1:T(8,128)(2,1)} %get-tuple-element.146, bf16[14,144,128]{2,0,1:T(8,128)(2,1)} %get-tuple-element.145, bf16[14,144,128]{2,0,1:T(8,128)(2,1)} %get-tuple-element.144, bf16[12,144,128]{2,0,1:T(8,128)(2,1)S(1)} %get-tuple-element.137, ...), dimensions={0} | concatenate | bytes 13418496 | tf_op jit(solution)/shard_map/concatenate | solution.py:442
  1054.0 16.4 %multiply_reduce_fusion = (f32[182]{0:T(256)S(1)}, f32[182,144,128]{2,1,0:T(8,128)}) fusion(bf16[182,128,128]{2,0,1:T(8,128)(2,1)} %fusion.35, bf16[182,144,144]{2,1,0:T(8,128)(2,1)} %copy.278, bf16[182,144,128]{2,0,1:T(8,128)(2,1)} %concatenate.158), kind=kOutput, calls=%fused_computation.12 | convolution fusion | flops 1834979200 | bytes 33640152 | tf_op jit(solution)/shard_map/brc,bcd->brd/dot_general | solution.py:470
  1074.9 12.3 %fusion.3 = f32[1,57,144,144]{3,2,1,0:T(8,128)} fusion(f32[1,57,144,144]{3,2,1,0:T(8,128)} %param.20, f32[57,144,128]{2,0,1:T(8,128)S(1)} %fusion.137), kind=kOutput, calls=%fused_computation.19 | convolution fusion | flops 304943616 | bytes 13658112 | tf_op jit(solution)/shard_map/src,stc->srt/dot_general | solution.py:454
  (688 shorter events, 441.4 us)
Async XLA Ops:
  7.2 52.0 %all-gather.6.cloned.1.call-start = ((), (), s32[]{:S(2)}) async-start(), calls=%async_computation.4 | async-start | bytes 1990656 | tf_op jit(solution)/shard_map/all_gather | solution.py:284
  9.0 93.0 %all-gather.8.cloned.1.call-start = ((), (), s32[]{:S(2)}) async-start(), calls=%async_computation.5 | async-start | bytes 1327104 | tf_op jit(solution)/shard_map/all_gather | solution.py:284
  10.9 179.7 %all-gather.10.cloned.1.call-start = ((), (), s32[]{:S(2)}) async-start(), calls=%async_computation.6 | async-start | bytes 4644864 | tf_op jit(solution)/shard_map/all_gather | solution.py:284
  14.0 272.9 %all-gather.12.cloned.1.call-start = ((), (), s32[]{:S(2)}) async-start(), calls=%async_computation.7 | async-start | bytes 4644864 | tf_op jit(solution)/shard_map/all_gather | solution.py:284
  14.6 345.3 %all-gather.14.cloned.1.call-start = ((), (), s32[]{:S(2)}) async-start(), calls=%async_computation.8 | async-start | bytes 4644864 | tf_op jit(solution)/shard_map/all_gather | solution.py:284
  15.1 848.5 %reduce-scatter.4.cloned.1.call-start = ((), (), s32[]{:S(2)}) async-start(), calls=%async_computation.9 | async-start | bytes 4644864 | tf_op jit(solution)/shard_map/reduce_scatter | solution.py:369
  59.2 48.8 %collective-permute-start = (bf16[1152,768]{1,0:T(8,128)(2,1)}, bf16[1152,768]{1,0:T(8,128)(2,1)}, u32[]{:S(2)}, u32[]{:S(2)}) collective-permute-start(bf16[1152,768]{1,0:T(8,128)(2,1)} %all-gather.6.cloned.1.call-done), channel_id=1, source_target_pairs={{0,8},{8,0},{16,24},{24,16},{1,9},{9,1},{17,25},{25,17},{2,10},{10... | collective-permute-start | bytes 5308424 | tf_op jit(solution)/shard_map/ppermute | solution.py:105
  176.6 191.8 %collective-permute-start.16 = (bf16[256,1152]{1,0:T(8,128)(2,1)}, bf16[256,1152]{1,0:T(8,128)(2,1)S(1)}, u32[]{:S(2)}, u32[]{:S(2)}) collective-permute-start(bf16[256,1152]{1,0:T(8,128)(2,1)} %get-tuple-element.108), channel_id=1, source_target_pairs={{0,8},{8,0},{16,24},{24,16},{1,9},{9,1},{17,25},{25,17},{2,10},{10... | collective-permute-start | bytes 1769480 | tf_op jit(solution)/shard_map/ppermute | solution.py:105
  190.5 177.9 %collective-permute-start.17 = (bf16[256,1152]{1,0:T(8,128)(2,1)S(1)}, bf16[256,1152]{1,0:T(8,128)(2,1)}, u32[]{:S(2)}, u32[]{:S(2)}) collective-permute-start(bf16[256,1152]{1,0:T(8,128)(2,1)S(1)} %collective-permute-done.15), channel_id=1, source_target_pairs={{0,8},{8,0},{16,24},{24,16},{1,9},{9,1},{17,25},{25,17},{2,10},{10... | collective-permute-start | bytes 1769480 | tf_op jit(solution)/shard_map/ppermute | solution.py:105
  368.3 29.2 %collective-permute-start.13 = (bf16[512,1152]{1,0:T(8,128)(2,1)S(1)}, bf16[512,1152]{1,0:T(8,128)(2,1)S(1)}, u32[]{:S(2)}, u32[]{:S(2)}) collective-permute-start(bf16[512,1152]{1,0:T(8,128)(2,1)S(1)} %slice.479), channel_id=1, source_target_pairs={{0,8},{8,0},{16,24},{24,16},{1,9},{9,1},{17,25},{25,17},{2,10},{10... | collective-permute-start | bytes 3538952 | tf_op jit(solution)/shard_map/ppermute | solution.py:105
  449.1 28.4 %collective-permute-start.26 = (bf16[256,1152]{1,0:T(8,128)(2,1)S(1)}, bf16[256,1152]{1,0:T(8,128)(2,1)S(1)}, u32[]{:S(2)}, u32[]{:S(2)}) collective-permute-start(bf16[256,1152]{1,0:T(8,128)(2,1)S(1)} %get-tuple-element.112), channel_id=1, source_target_pairs={{0,8},{8,0},{16,24},{24,16},{1,9},{9,1},{17,25},{25,17},{2,10},{10... | collective-permute-start | bytes 1769480 | tf_op jit(solution)/shard_map/ppermute | solution.py:105
  506.7 358.4 %reduce-scatter.6.cloned.1.call-start = ((), (), s32[]{:S(2)}) async-start(), calls=%async_computation.10 | async-start | bytes 4644864 | tf_op jit(solution)/shard_map/reduce_scatter | solution.py:369
  506.8 128.9 %collective-permute-start.54 = (bf16[57,128,128]{2,1,0:T(8,128)(2,1)}, bf16[57,128,128]{2,1,0:T(8,128)(2,1)}, u32[]{:S(2)}, u32[]{:S(2)}) collective-permute-start(bf16[57,128,128]{2,1,0:T(8,128)(2,1)} %bitcast.81), channel_id=1, source_target_pairs={{0,16},{8,24},{16,0},{24,8},{1,17},{9,25},{17,1},{25,9},{2,18},{10... | collective-permute-start | bytes 5603336 | tf_op jit(solution)/shard_map/ppermute | solution.py:111
  536.2 331.1 %reduce-scatter.8.cloned.1.call-start = ((), (), s32[]{:S(2)}) async-start(), calls=%async_computation.11 | async-start | bytes 4644864 | tf_op jit(solution)/shard_map/reduce_scatter | solution.py:369
  635.7 25.9 %collective-permute-start.34 = (bf16[2,256,512]{1,2,0:T(8,128)(2,1)}, bf16[2,256,512]{1,2,0:T(8,128)(2,1)}, u32[]{:S(2)}, u32[]{:S(2)}) collective-permute-start(bf16[2,256,512]{1,2,0:T(8,128)(2,1)} %get-tuple-element.156), channel_id=1, source_target_pairs={{2,0},{3,1},{4,2},{10,8},{11,9},{12,10},{18,16},{19,17},{20,18},{2... | collective-permute-start | bytes 1572872 | tf_op jit(solution)/shard_map/ppermute | solution.py:222
  656.6 90.7 %collective-permute-start.51 = (bf16[57,144,144]{2,1,0:T(8,128)(2,1)}, bf16[57,144,144]{2,1,0:T(8,128)(2,1)}, u32[]{:S(2)}, u32[]{:S(2)}) collective-permute-start(bf16[57,144,144]{2,1,0:T(8,128)(2,1)} %bitcast.301), channel_id=1, source_target_pairs={{0,16},{8,24},{16,0},{24,8},{1,17},{9,25},{17,1},{25,9},{2,18},{10... | collective-permute-start | bytes 7091720 | tf_op jit(solution)/shard_map/ppermute | solution.py:111
  661.6 90.4 %collective-permute-start.52 = (bf16[57,144,144]{2,1,0:T(8,128)(2,1)}, bf16[57,144,144]{2,1,0:T(8,128)(2,1)}, u32[]{:S(2)}, u32[]{:S(2)}) collective-permute-start(bf16[57,144,144]{2,1,0:T(8,128)(2,1)} %bitcast.302), channel_id=1, source_target_pairs={{0,8},{8,0},{16,24},{24,16},{1,9},{9,1},{17,25},{25,17},{2,10},{10... | collective-permute-start | bytes 7091720 | tf_op jit(solution)/shard_map/ppermute | solution.py:105
  662.1 94.7 %collective-permute-start.56 = (bf16[57,128,128]{2,1,0:T(8,128)(2,1)}, bf16[57,128,128]{2,1,0:T(8,128)(2,1)}, u32[]{:S(2)}, u32[]{:S(2)}) collective-permute-start(bf16[57,128,128]{2,1,0:T(8,128)(2,1)} %collective-permute-done.54), channel_id=1, source_target_pairs={{0,8},{8,0},{16,24},{24,16},{1,9},{9,1},{17,25},{25,17},{2,10},{10... | collective-permute-start | bytes 5603336 | tf_op jit(solution)/shard_map/ppermute | solution.py:105
  678.5 103.4 %collective-permute-start.38 = (bf16[2304,640]{1,0:T(8,128)(2,1)}, bf16[2304,640]{1,0:T(8,128)(2,1)S(1)}, u32[]{:S(2)}, u32[]{:S(2)}) collective-permute-start(bf16[2304,640]{1,0:T(8,128)(2,1)} %pad_maximum_fusion.1), channel_id=1, source_target_pairs={{0,8},{8,0},{16,24},{24,16},{1,9},{9,1},{17,25},{25,17},{2,10},{10... | collective-permute-start | bytes 8847368 | tf_op jit(solution)/shard_map/ppermute | solution.py:105
  747.3 48.4 %collective-permute-start.53 = (bf16[57,144,144]{2,1,0:T(8,128)(2,1)}, bf16[57,144,144]{2,1,0:T(8,128)(2,1)}, u32[]{:S(2)}, u32[]{:S(2)}) collective-permute-start(bf16[57,144,144]{2,1,0:T(8,128)(2,1)} %collective-permute-done.51), channel_id=1, source_target_pairs={{0,8},{8,0},{16,24},{24,16},{1,9},{9,1},{17,25},{25,17},{2,10},{10... | collective-permute-start | bytes 7091720 | tf_op jit(solution)/shard_map/ppermute | solution.py:105
  789.2 35.0 %collective-permute-start.39 = (bf16[1152,640]{1,0:T(8,128)(2,1)}, bf16[1152,640]{1,0:T(8,128)(2,1)S(1)}, u32[]{:S(2)}, u32[]{:S(2)}) collective-permute-start(bf16[1152,640]{1,0:T(8,128)(2,1)} %slice.475), channel_id=1, source_target_pairs={{0,16},{8,24},{16,0},{24,8},{1,17},{9,25},{17,1},{25,9},{2,18},{10... | collective-permute-start | bytes 4423688 | tf_op jit(solution)/shard_map/ppermute | solution.py:111
  821.0 99.8 %collective-permute-start.47 = (f32[5120]{0:T(1024)S(1)}, f32[5120]{0:T(1024)S(1)}, u32[]{:S(2)}, u32[]{:S(2)}) collective-permute-start(f32[5120]{0:T(1024)S(1)} %add.742), channel_id=1, source_target_pairs={{0,16},{8,24},{16,0},{24,8},{1,17},{9,25},{17,1},{25,9},{2,18},{10... | collective-permute-start | bytes 61448 | tf_op jit(solution)/shard_map/ppermute | solution.py:150
  827.4 114.0 %all-to-all-start = ((bf16[8,144,640]{2,1,0:T(8,128)(2,1)}), bf16[8,144,640]{2,1,0:T(8,128)(2,1)S(1)}, u32[]{:S(2)}, u32[]{:S(2)}) async-start(bf16[8,144,640]{2,1,0:T(8,128)(2,1)} %bitcast.294), calls=%async_computation | async-start | bytes 2949120 | tf_op jit(solution)/shard_map/all_to_all | solution.py:422
  873.1 69.4 %collective-permute-start.43 = (bf16[42,144,128]{2,1,0:T(8,128)(2,1)}, bf16[42,144,128]{2,1,0:T(8,128)(2,1)}, u32[]{:S(2)}, u32[]{:S(2)}) collective-permute-start(bf16[42,144,128]{2,1,0:T(8,128)(2,1)} %copy.270), channel_id=1, source_target_pairs={{0,16},{8,24},{16,0},{24,8},{1,17},{9,25},{17,1},{25,9},{2,18},{10... | collective-permute-start | bytes 4644872 | tf_op jit(solution)/shard_map/ppermute | solution.py:111
  (211 other events, 3238.8 us)
Sparse Core Ops, SparseCore 0:
  10.8 48.3 all-gather.5
  62.0 40.0 all-gather.7
  104.8 79.0 all-gather.9
  186.6 100.2 all-gather.11
  288.9 70.8 all-gather.13
  506.8 85.9 reduce-scatter.3
  596.9 111.2 reduce-scatter.5
  712.3 87.3 reduce-scatter.7

commit v2 on v1

--- a/solution.py
+++ b/solution.py
@@ -2,6 +2,8 @@
 import jax.numpy as jnp
 import numpy as np
 from jax import lax
+from jax.experimental import pallas as pl
+from jax.experimental.pallas import tpu as pltpu
 from jax.sharding import PartitionSpec as P
 
 D = 1152
@@ -26,7 +28,9 @@
 GAIN_RATE = 0.05
 DECAY = 0.5
 SCALE = HD ** (-0.5)
-MAX_ROUNDS = 16
+DIRECT_MAX = 8
+LATE = 21
+VMEM_LIMIT = 40 * 1024 * 1024
 BF = jnp.bfloat16
 F32 = jnp.float32
 
@@ -152,33 +156,205 @@
     return value
 
 
-def key_plan(nf):
-    rows = GLEN // nf
-    slots = np.arange(GLEN)
-    seg = np.where(slots < PROMPT, -1, (slots - PROMPT) // CLEN)
-    pos = np.where(slots < PROMPT, slots, PROMPT + (slots - PROMPT) % CLEN)
-    dist = pos[:, None] - pos[None, :]
-    vis = (dist >= 0) & (dist < WIN) & ((seg[None, :] < 0) | (seg[None, :] == seg[:, None]))
-    need = vis.reshape(nf, rows, nf, rows).any(axis=(1, 3))
-    sources = [[u for u in reversed(range(nf)) if need[t, u] and u != t] for t in range(nf)]
-    count = max(len(s) for s in sources)
-    plan, tables = [], []
-    for k in range(count):
-        edges = [(s[k], t) for t, s in enumerate(sources) if len(s) > k]
-        rounds = []
-        while edges:
-            used, now, later = set(), [], []
-            for src, dst in edges:
-                if src in used:
-                    later.append((src, dst))
-                else:
-                    used.add(src)
-                    now.append((src, dst))
-            rounds.append(now)
-            edges = later
-        plan.append(rounds)
-        tables.append([s[k] if len(s) > k else -1 for s in sources])
-    return (plan, tables)
+def after(value, *others):
+    return lax.optimization_barrier((value,) + others)[0]
+
+
+def swap_fsdp(value, flip, nf):
+    return lax.ppermute(value, "fsdp", [(e, e ^ flip) for e in range(nf)])
+
+
+def gather_rows(own, nf):
+    if nf > DIRECT_MAX:
+        return lax.all_gather(own, "fsdp", axis=0, tiled=True)
+    me = lax.axis_index("fsdp")
+    band, width = own.shape
+    straight = [own] + [swap_fsdp(own, flip, nf) for flip in range(2, nf, 2)]
+    crossed = [swap_fsdp(part, 1, nf) for part in straight]
+    whole = jnp.zeros((nf * band, width), own.dtype)
+    for k in range(nf // 2):
+        whole = lax.dynamic_update_slice(whole, straight[k], ((me ^ (2 * k)) * band, 0))
+        whole = lax.dynamic_update_slice(whole, crossed[k], ((me ^ (2 * k + 1)) * band, 0))
+    return whole
+
+
+def add_low(left, right):
+    return (left.astype(F32) + right.astype(F32)).astype(BF)
+
+
+def reduce_rows(terms, nf):
+    if nf > DIRECT_MAX:
+        return lax.psum_scatter(terms, "fsdp", scatter_dimension=0, tiled=True)
+    me = lax.axis_index("fsdp")
+    band, width = (terms.shape[0] // nf, terms.shape[1])
+
+    def part(flip):
+        return lax.dynamic_slice(terms, ((me ^ flip) * band, 0), (band, width))
+
+    sums = []
+    for k in range(nf // 2 - 1, -1, -1):
+        received = swap_fsdp(part(2 * k + 1), 1, nf)
+        if k:
+            sums.append(swap_fsdp(add_low(part(2 * k), received), 2 * k, nf))
+        else:
+            sums.append(received)
+    total = part(0).astype(F32)
+    for piece in sums:
+        total = total + piece.astype(F32)
+    return total.astype(BF)
+
+
+def direct_reduce(terms, nf):
+    band, width = (terms.shape[0] // nf, terms.shape[1])
+    if nf > DIRECT_MAX:
+        spread = lax.all_to_all(
+            terms.reshape(nf, band, width), "fsdp", split_axis=0, concat_axis=0
+        )
+        return jnp.sum(spread.astype(F32), axis=0).astype(BF)
+    me = lax.axis_index("fsdp")
+    total = lax.dynamic_slice(terms, (me * band, 0), (band, width)).astype(F32)
+    for flip in range(1, nf):
+        sent = lax.dynamic_slice(terms, ((me ^ flip) * band, 0), (band, width))
+        total = total + lax.ppermute(sent, "fsdp", [(e, e ^ flip) for e in range(nf)]).astype(F32)
+    return total.astype(BF)
+
+
+def dot_on(left, right, left_dim, right_dim):
+    return lax.dot_general(
+        left, right, (((left_dim,), (right_dim,)), ((), ())), preferred_element_type=F32
+    )
+
+
+def pick_grad(sources, flags, at):
+    if len(sources) == 1:
+        return sources[0][...]
+    return jnp.where(flags[at] > 0, sources[1][...], sources[0][...])
+
+
+def update_body(group, count, flags, refs):
+    grads = refs[: group * count]
+    lefts = refs[group * count : group * (count + 1)]
+    rights = refs[group * (count + 1) : group * (count + 2)]
+    master_ref, new_ref, low_ref = (refs[group * (count + 2)], refs[-2], refs[-1])
+    for j in range(group):
+        grad = pick_grad(grads[j * count : (j + 1) * count], flags, pl.program_id(0) * group + j)
+        shaped = dot_on(lefts[j][...], grad, 1, 0)
+        shaped = dot_on(shaped.astype(BF), rights[j][...], 1, 0)
+        power = jnp.sum(jnp.sum(shaped * shaped, axis=1, keepdims=True), axis=0, keepdims=True)
+        factor = -RATE * lax.rsqrt(power * (1.0 / (shaped.shape[0] * shaped.shape[1])) + EPSILON)
+        at = pl.ds(j * BC, BC)
+        fresh = master_ref[:, at] + shaped * factor
+        new_ref[:, at] = fresh
+        low_ref[:, at] = fresh.astype(BF)
+
+
+def grad_specs(sources, group, skip, band):
+    def spec(j, is_second):
+        def index(i, part, kind, column, flags, *more):
+            at = (i + skip) * group + j
+            own = jnp.where(flags[at] > 0, 1, 0) if len(sources) > 1 else 0
+            fits = own if is_second else 1 - own
+            return (part[at] * fits, kind[at] * fits, 0, column[at] * fits)
+
+        return pl.BlockSpec((None, None, band, BC), index)
+
+    return [spec(j, n > 0) for j in range(group) for n in range(len(sources))]
+
+
+def update_blocks(sources, places, roots, left_roots, right_roots, master, start, count, group, into):
+    band = master.shape[0]
+    skip = start // group
+
+    def root_spec(shape, j):
+        def index(i, part, kind, column, flags, root):
+            return (root[i * group + j], 0, 0)
+
+        return pl.BlockSpec((None,) + shape, index)
+
+    wide = pl.BlockSpec((band, group * BC), lambda i, *tables: (0, i + skip))
+    in_specs = grad_specs(sources, group, 0, band)
+    in_specs += [root_spec(left_roots.shape[1:], j) for j in range(group)]
+    in_specs += [root_spec(right_roots.shape[1:], j) for j in range(group)]
+    in_specs += [wide]
+    operands = list(sources) * group + [left_roots] * group + [right_roots] * group + [master]
+    tables = list(places) + [roots]
+    aliases = {}
+    if into is not None:
+        aliases = {len(tables) + len(operands) + n: n for n in range(2)}
+        in_specs += [pl.BlockSpec(memory_space=pl.ANY)] * 2
+        operands += list(into)
+    return pl.pallas_call(
+        lambda *refs: update_body(group, len(sources), refs[3], refs[5:]),
+        grid_spec=pltpu.PrefetchScalarGridSpec(
+            num_scalar_prefetch=5,
+            grid=(count // group,),
+            in_specs=in_specs,
+            out_specs=[wide, wide],
+        ),
+        out_shape=[
+            jax.ShapeDtypeStruct(master.shape, F32),
+            jax.ShapeDtypeStruct(master.shape, BF),
+        ],
+        input_output_aliases=aliases,
+        compiler_params=pltpu.CompilerParams(vmem_limit_bytes=VMEM_LIMIT),
+        name="update_blocks",
+    )(*tables, *operands)
+
+
+def stats_body(group, count, skip, flags, used, refs):
+    grads, (left_ref, right_ref) = (refs[: group * count], refs[group * count : group * count + 2])
+    grad_out, left_out, right_out = refs[-3:]
+    for j in range(group):
+        at = (pl.program_id(0) + skip) * group + j
+        grad = pick_grad(grads[j * count : (j + 1) * count], flags, at)
+        grad = jnp.where(used[at] > 0, grad, jnp.zeros_like(grad))
+        grad_out[j] = grad.astype(F32)
+        left_out[j] = DECAY * left_ref[j] + (1.0 - DECAY) * dot_on(grad, grad, 1, 1)
+        right_out[j] = DECAY * right_ref[j] + (1.0 - DECAY) * dot_on(grad, grad, 0, 0)
+
+
+def owner_stats(sources, places, used, stat_left, stat_right, start, count, group, into):
+    slots, band = (stat_left.shape[0], sources[0].shape[2])
+    skip = start // group
+
+    def slab(shape):
+        return pl.BlockSpec((group,) + shape, lambda i, *tables: (i + skip, 0, 0))
+
+    shapes = [(band, BC), stat_left.shape[1:], stat_right.shape[1:]]
+    in_specs = grad_specs(sources, group, skip, band) + [slab(shapes[1]), slab(shapes[2])]
+    operands = list(sources) * group + [stat_left, stat_right]
+    tables = list(places) + [used]
+    aliases = {}
+    if into is not None:
+        aliases = {len(tables) + len(operands) + n: n for n in range(3)}
+        in_specs += [pl.BlockSpec(memory_space=pl.ANY)] * 3
+        operands += list(into)
+    return pl.pallas_call(
+        lambda *refs: stats_body(group, len(sources), skip, refs[3], refs[4], refs[5:]),
+        grid_spec=pltpu.PrefetchScalarGridSpec(
+            num_scalar_prefetch=5,
+            grid=(count // group,),
+            in_specs=in_specs,
+            out_specs=[slab(shape) for shape in shapes],
+        ),
+        out_shape=[jax.ShapeDtypeStruct((slots,) + shape, F32) for shape in shapes],
+        input_output_aliases=aliases,
+        compiler_params=pltpu.CompilerParams(vmem_limit_bytes=VMEM_LIMIT),
+        name="owner_stats",
+    )(*tables, *operands)
+
+
+KEY_SHARDS = 8
+TO_SECOND = [(0, 2), (1, 3), (2, 4), (3, 5)]
+TO_NEXT = [(0, 1), (1, 2), (2, 3)]
+ONWARDS = [(4, 6), (5, 7)]
+ACROSS = [(4, 5), (5, 4), (6, 7), (7, 6)]
+FIRST_SOURCE = [-1, -1, 0, 1, 2, 3, 2, 3]
+SECOND_SOURCE = [-1, 0, 1, 2, 3, 2, 3, 2]
+
+
+def backwards(pairs):
+    return [(dst, src) for src, dst in pairs]
 
 
 def pick_static(table, index):
@@ -187,41 +363,40 @@
     return jnp.sum(jnp.where(hit, values, 0))
 
 
-def spread_keys(own, nf):
-    rows = own.shape[1]
+def key_slots_of(rows, nf):
     me = lax.axis_index("fsdp")
     step = jnp.arange(rows, dtype=jnp.int32)
-    plan, tables = key_plan(nf)
-    if sum(len(r) for r in plan) > MAX_ROUNDS:
-        return (
-            lax.all_gather(own, "fsdp", axis=1, tiled=True),
-            jnp.arange(rows * nf, dtype=jnp.int32),
-        )
-    parts, ids = [own], [me * rows + step]
-    for rounds, table in zip(plan, tables):
-        got = [lax.ppermute(own, "fsdp", pairs) for pairs in rounds]
-        total = got[0]
-        for more in got[1:]:
-            total = total + more
+    if nf != KEY_SHARDS:
+        return jnp.arange(rows * nf, dtype=jnp.int32)
+    ids = [me * rows + step]
+    for table in (FIRST_SOURCE, SECOND_SOURCE):
         source = pick_static(table, me)
-        parts.append(total)
         ids.append(jnp.where(source >= 0, source * rows + step, -1))
-    return (jnp.concatenate(parts, axis=1), jnp.concatenate(ids))
+    return jnp.concatenate(ids)
+
+
+def spread_keys(own, nf):
+    if nf != KEY_SHARDS:
+        return lax.all_gather(own, "fsdp", axis=0, tiled=True)
+    second = lax.ppermute(own, "fsdp", TO_SECOND)
+    following = lax.ppermute(own, "fsdp", TO_NEXT)
+    onward = lax.ppermute(second, "fsdp", ONWARDS)
+    crossed = lax.ppermute(second, "fsdp", ACROSS[:2])
+    crossed_on = lax.ppermute(onward, "fsdp", ACROSS[2:])
+    return jnp.concatenate([own, second + onward, following + crossed + crossed_on], axis=0)
 
 
 def return_key_grads(terms, rows, nf):
-    plan, _ = key_plan(nf)
-    if sum(len(r) for r in plan) > MAX_ROUNDS:
+    if nf != KEY_SHARDS:
         return lax.psum_scatter(
-            terms.astype(BF), "fsdp", scatter_dimension=1, tiled=True
+            terms.astype(BF), "fsdp", scatter_dimension=0, tiled=True
         ).astype(F32)
-    total = terms[:, :rows]
-    for k, rounds in enumerate(plan):
-        sent = terms[:, (k + 1) * rows : (k + 2) * rows].astype(BF)
-        for pairs in rounds:
-            back = lax.ppermute(sent, "fsdp", [(dst, src) for src, dst in pairs])
-            total = total + back.astype(F32)
-    return total
+    first = terms[rows : 2 * rows]
+    second = terms[2 * rows :].astype(BF)
+    total = terms[:rows] + lax.ppermute(second, "fsdp", backwards(TO_NEXT)).astype(F32)
+    first = first + lax.ppermute(second, "fsdp", ACROSS).astype(F32)
+    first = first + lax.ppermute(first.astype(BF), "fsdp", backwards(ONWARDS)).astype(F32)
+    return total + lax.ppermute(first.astype(BF), "fsdp", backwards(TO_SECOND)).astype(F32)
 
 
 def attend(query_low, keys, values, visible):
@@ -280,27 +455,24 @@
     def columns(at, size):
         return lax.dynamic_slice(master, (0, at), (band, size)).astype(BF)
 
-    def gather_rows(part):
-        return lax.all_gather(part, "fsdp", axis=0, tiled=True)
-
-    def halves(at, size):
-        half = size // 2
-        mine = gather_rows(columns(at + core * half, half))
-        other = swap_core(mine, nd)
+    def quarters(at, size):
+        part = size // nd
+        mine = gather_rows(columns(at + dp_me * part, part), nf)
         whole = jnp.zeros((D, size), BF)
-        whole = lax.dynamic_update_slice(whole, mine, (0, core * half))
-        return lax.dynamic_update_slice(whole, other, (0, (1 - core) * half))
-
-    w_qkv = halves(0, QKVW)
-    w_out = halves(QKVW, OUTW)
+        for piece, index in zip(gather_parts(mine, nd), part_owners(nd)):
+            whole = lax.dynamic_update_slice(whole, piece, (0, index * part))
+        return whole
+
+    w_qkv = quarters(0, QKVW)
+    w_out = quarters(QKVW, OUTW)
     gate_cols = columns(gate_at + start * BC, width)
     up_cols = columns(gate_at + FF + start * BC, width)
     down_cols = columns(gate_at + 2 * FF + start * BC, width)
     keep = (jnp.arange(width, dtype=jnp.int32) >= fresh * BC)[None, :]
     down_cols = jnp.where(keep, down_cols, jnp.zeros_like(down_cols))
-    w_gate = gather_rows(gate_cols)
-    w_up = gather_rows(up_cols)
-    w_down = gather_rows(down_cols)
+    w_gate = lax.all_gather(gate_cols, "fsdp", axis=0, tiled=True)
+    w_up = lax.all_gather(up_cols, "fsdp", axis=0, tiled=True)
+    w_down = lax.all_gather(down_cols, "fsdp", axis=0, tiled=True)
 
     flat_in = tokens.astype(F32).reshape(count, D)
     normed = rms_gain(flat_in, pre_attn).astype(BF)
@@ -315,8 +487,10 @@
     rot_queries, rot_keys = prepare_heads(queries, keys, query_gain, key_gain, cosine, sine)
     query_low = rot_queries.astype(BF).reshape(micros, rows, HEADS, HD)
     own_keys = jnp.concatenate([rot_keys.astype(BF), values.astype(BF)], axis=1)
-    key_buffer, key_slots = spread_keys(own_keys.reshape(micros, rows, 2 * HD), nf)
-    keys_all, values_all = (key_buffer[..., :HD], key_buffer[..., HD:])
+    key_buffers = [spread_keys(own_keys[m * rows : (m + 1) * rows], nf) for m in range(micros)]
+    key_slots = key_slots_of(rows, nf)
+    keys_all = [buffer[:, :HD] for buffer in key_buffers]
+    values_all = [buffer[:, HD:] for buffer in key_buffers]
     all_probs, all_attended = [], []
     for m in range(micros):
         visible = visibility(slots, key_slots, lengths[m, 0])
@@ -364,19 +538,28 @@
         low_ones.append(grad_one.astype(BF))
         gain_terms.append((grad_post_attn, grad_pre_ffw, grad_post_ffw))
 
-    def reduce_rows(lefts, rights):
+    def weight_term(lefts, rights):
         term = dot_tn(jnp.concatenate(lefts, axis=0), jnp.concatenate(rights, axis=0))
-        return lax.psum_scatter(term.astype(BF), "fsdp", scatter_dimension=0, tiled=True)
-
-    def blocks_of(part):
-        return part.reshape(band, part.shape[1] // BC, BC).transpose(1, 0, 2)
-
+        return term.astype(BF)
+
+    down_term = weight_term(gathered_two, hiddens)
     ff_bands = [
-        reduce_rows(gathered_in, low_gates),
-        reduce_rows(gathered_in, low_ups),
-        reduce_rows(gathered_two, hiddens),
+        reduce_rows(weight_term(gathered_in, low_gates), nf),
+        reduce_rows(weight_term(gathered_in, low_ups), nf),
+        lax.psum_scatter(down_term, "fsdp", scatter_dimension=0, tiled=True),
     ]
-    ff_blocks = jnp.concatenate([blocks_of(part) for part in ff_bands], axis=0)
+
+    def gather_relative(bands):
+        parts = [gather_parts(part, nd) for part in bands]
+        out = jnp.zeros((nd, len(bands)) + bands[0].shape, BF)
+        for kind, pieces in enumerate(parts):
+            for place, piece in enumerate(pieces):
+                out = lax.dynamic_update_slice(
+                    out, piece[None, None], (place, kind) + (0,) * piece.ndim
+                )
+        return out
+
+    ff_all = gather_relative(ff_bands)
 
     low_one = jnp.concatenate(low_ones, axis=0)
     attended = jnp.concatenate(all_attended, axis=0)
@@ -387,8 +570,9 @@
             query_low[m], keys_all[m], values_all[m], all_probs[m], low_mixed[m]
         )
         grad_queries.append(for_queries)
-        key_terms.append(jnp.concatenate([for_keys, for_values], axis=1))
-    own_terms = return_key_grads(jnp.stack(key_terms), rows, nf).reshape(count, 2 * HD)
+        terms = jnp.concatenate([for_keys, for_values], axis=1)
+        key_terms.append(return_key_grads(terms, rows, nf))
+    own_terms = jnp.concatenate(key_terms, axis=0)
     grad_keys, grad_values = (own_terms[:, :HD], own_terms[:, HD:])
 
     def heads_only(query_in, key_in, query_scale, key_scale):
@@ -419,59 +603,60 @@
         jnp.concatenate([owner_columns(e) for e in owners_at[nd // 2 :]], axis=0),
         nd,
     )
-    spread = lax.all_to_all(
-        attn_sum.astype(BF).reshape(nf, band, attn_width), "fsdp", split_axis=0, concat_axis=0
-    )
-    attn_band = jnp.sum(spread.astype(F32), axis=0).astype(BF)
-
-    def gather_blocks(part):
-        pieces = gather_parts(part, nd)
-        out = jnp.zeros((nd,) + part.shape, part.dtype)
-        for piece, index in zip(pieces, part_owners(nd)):
-            out = lax.dynamic_update_slice(out, piece[None], (index,) + (0,) * part.ndim)
-        return out
-
-    ff_all = gather_blocks(ff_blocks)
-    attn_all = gather_blocks(blocks_of(attn_band))
-    pieces = [attn_all.reshape((nd * attn_per, band, BC))[:ATTN_BLOCKS]]
-    for kind in range(3):
-        for e in range(nd):
-            begin = min(e * per, FF_BLOCKS - per)
-            skip = min(e * per - begin, per)
-            pieces.append(ff_all[e, kind * per + skip : (kind + 1) * per])
-    blocks = jnp.concatenate(pieces, axis=0)
+    attn_band = direct_reduce(attn_sum.astype(BF), nf)
+    attn_all = gather_relative([attn_band])
+
+    def relative(index):
+        nx = nd // 2
+        flip = (index % 2) ^ core
+        return flip * nx + (dp_me // 2 + nx - index // 2) % nx
+
+    ff_index = np.arange(3 * FF_BLOCKS)
+    ff_dp = np.minimum(ff_index % FF_BLOCKS // per, nd - 1)
+    ff_column = ff_index % FF_BLOCKS - np.minimum(ff_dp * per, FF_BLOCKS - per)
+    attn_index = np.arange(ATTN_BLOCKS)
+    part_of = relative(
+        jnp.asarray(np.concatenate([attn_index // attn_per, ff_dp]).astype(np.int32))
+    )
+    kind_of = jnp.asarray(
+        np.concatenate([np.zeros(ATTN_BLOCKS), ff_index // FF_BLOCKS]).astype(np.int32)
+    )
+    column_of = jnp.asarray(np.concatenate([attn_index % attn_per, ff_column]).astype(np.int32))
 
     owners = owner[:, 0]
     index = jnp.arange(NBLK, dtype=jnp.int32)
     before = (owners[:, None] == owners[None, :]) & (index[None, :] < index[:, None])
     ranks = jnp.sum(before.astype(jnp.int32), axis=1)
-    slot = owners * capacity + ranks
-    my_slots = dp_me * capacity + jnp.arange(capacity, dtype=jnp.int32)
-    pick_mine = (slot[None, :] == my_slots[:, None]).astype(BF)
-    slot_low = jnp.einsum("sb,brc->src", pick_mine, blocks, preferred_element_type=F32)
-    slot_grads = slot_low
-    low_slots = slot_low.astype(BF)
-    new_left = DECAY * stat_left[0] + (1.0 - DECAY) * jnp.einsum(
-        "src,stc->srt", low_slots, low_slots, preferred_element_type=F32
-    )
-    new_right = DECAY * stat_right[0] + (1.0 - DECAY) * jnp.einsum(
-        "src,srd->scd", low_slots, low_slots, preferred_element_type=F32
-    )
-    every_slot = jnp.arange(nd * capacity, dtype=jnp.int32)
-    pick_root = (slot[:, None] == every_slot[None, :]).astype(BF)
-
-    def roots_by_block(root):
-        every = gather_blocks(root).reshape((nd * capacity,) + root.shape[1:])
-        return jnp.einsum("bs,srt->brt", pick_root, every, preferred_element_type=F32).astype(BF)
-
-    lefts = roots_by_block(root_left[0])
-    rights = roots_by_block(root_right[0])
-    shaped = jnp.einsum("brt,btc->brc", lefts, blocks, preferred_element_type=F32)
-    shaped = jnp.einsum("brc,bcd->brd", shaped.astype(BF), rights, preferred_element_type=F32)
-    factor = lax.rsqrt(jnp.mean(shaped * shaped, axis=(1, 2), keepdims=True) + EPSILON)
-    changes = -RATE * shaped * factor
-    new_master = master + changes.transpose(1, 0, 2).reshape(band, NBLK * BC)
-    new_weights = new_master.astype(BF)
+    my_slots = jnp.arange(capacity, dtype=jnp.int32)
+    mine = (owners[None, :] == dp_me) & (ranks[None, :] == my_slots[:, None])
+    used = jnp.sum(mine.astype(jnp.int32), axis=1)
+
+    def of_slot(values):
+        return jnp.sum(jnp.where(mine, values[None, :], 0), axis=1)
+
+    root_of = relative(owners) * capacity + ranks
+    every_left = gather_relative([after(root_left[0], w_qkv)])
+    every_left = every_left.reshape((nd * capacity,) + root_left.shape[2:])
+    every_right = gather_relative([after(root_right[0], w_qkv)])
+    every_right = every_right.reshape((nd * capacity,) + root_right.shape[2:])
+
+    is_attn = (index < ATTN_BLOCKS).astype(jnp.int32)
+    places = (part_of, kind_of, column_of, is_attn)
+    early = tuple(table[LATE:] for table in places)
+    late = tuple(table[:LATE] for table in places)
+    root_args = (every_left, every_right, master)
+    fresh_arrays = update_blocks(
+        [ff_all], early, root_of[LATE:], *root_args, LATE, NBLK - LATE, 7, None
+    )
+    slot_places = tuple(of_slot(table) for table in places)
+    group = 3 if (capacity - LATE) % 3 == 0 else 1
+    stat_args = (slot_places, used, stat_left[0], stat_right[0])
+    fresh_stats = owner_stats([ff_all], *stat_args, LATE, capacity - LATE, group, None)
+    both = [ff_all, attn_all]
+    new_master, new_weights = update_blocks(
+        both, late, root_of[:LATE], *root_args, 0, LATE, 7, fresh_arrays
+    )
+    slot_grads, new_left, new_right = owner_stats(both, *stat_args, 0, LATE, group, fresh_stats)
 
     post_attn_sum = sum(entry[0] for entry in gain_terms)
     pre_ffw_sum = sum(entry[1] for entry in gain_terms)

time: 1130 us -> 933 us (0.83)
  waiting for transfers between devices: 411 us -> 261 us
  local copies, waits for them, and re-layouts: 242 us -> 101 us
  starting transfers between devices: 88 us -> 219 us
  matrix products: 263 us -> 197 us
  Pallas kernels: 0 us -> 59 us
  other arithmetic: 93.9 us -> 64.4 us
    all_gather x5 -> x3, waiting for transfers between devices: 225 us -> 0.01 us  [the longest x1 0.01 us: local(): w_gate = lax.all_gather(gate_cols, 'fsdp', axis=0, tiled=True)]
    ppermute x16 -> x53, starting transfers between devices: 24.4 us -> 156 us  [the longest x28 101 us: swap_fsdp(): return lax.ppermute(value, 'fsdp', [(e, e ^ flip) for e in range(nf)])]
    concatenate x4 -> x2, local copies, waits for them, and re-layouts: 87.5 us -> 1.2 us  [weight_term(): jnp.concatenate(lefts, axis=0)]
    dot_general x5 -> x0, matrix products: 59.4 us -> none  [the longest x1 18.9 us: roots_by_block(): jnp.einsum('bs,srt->brt', pick_root, every, preferred_element_type=F32)]
    pallas_call x0 -> x4, Pallas kernels: none -> 59 us  [the longest x2 38.6 us: update_blocks(): pl.pallas_call(lambda *refs: update_body(group, len(sources), refs[3], re...]
    ppermute x16 -> x53, waiting for transfers between devices: 15.1 us -> 73.3 us  [the longest x28 61.4 us: swap_fsdp(): return lax.ppermute(value, 'fsdp', [(e, e ^ flip) for e in range(nf)])]
    ppermute x5, waiting for transfers between devices: 2.32 us -> 40 us  [sum_everywhere(): lax.ppermute(value, axis, [(e, e ^ step) for e in range(count)])]
    all_to_all x1 -> x0, starting transfers between devices: 36.2 us -> none  [local(): lax.all_to_all(attn_sum.astype(BF).reshape(nf, band, attn_width), 'fsdp',...]
  transfers between devices with their start and end apart: 66 -> 108, of which waited for: 24 -> 31; matrix products, arithmetic and copies ran while one was open for 34% -> 34% of each run, Pallas kernels for 0% -> 0%
where the time goes in v2:
time: 933 us; the launch traced here: 922 us
  waiting for transfers between devices  261 us (28%)
  starting transfers between devices  219 us (23%)
  matrix products  197 us (21%)
  local copies, waits for them, and re-layouts  101 us (11%)
  other arithmetic  64.4 us (7%)
  Pallas kernels  59 us (6%)
  between operations  19.8 us (2%)
    ppermute x17, waiting for transfers between devices, shift_x(): return lax.ppermute(value, 'dp', pairs)  144 us
    ppermute x28, starting transfers between devices, swap_fsdp(): return lax.ppermute(value, 'fsdp', [(e, e ^ flip) for e in range(nf)])  101 us
    dot_general x8, matrix products, dot_nn(): return jnp.dot(left, right, preferred_element_type=F32)  82.9 us
    ppermute x28, waiting for transfers between devices, swap_fsdp(): return lax.ppermute(value, 'fsdp', [(e, e ^ flip) for e in range(nf)])  61.4 us
    dot_general x9, matrix products, dot_nt(): lax.dot_general(left, right, (((1,), (1,)), ((), ())), preferred_element_...  56.5 us
    dynamic_update_slice x23, local copies, waits for them, and re-layouts, gather_relative(): lax.dynamic_update_slice(out, piece[None, None], (place, kind) + (0,) * p...  52.4 us
    dot_general x5, matrix products, dot_tn(): lax.dot_general(left, right, (((0,), (0,)), ((), ())), preferred_element_...  45 us
    ppermute x5, waiting for transfers between devices, sum_everywhere(): lax.ppermute(value, axis, [(e, e ^ step) for e in range(count)])  40 us
  transfers between devices with their start and end apart: 108, of which 31 were waited for; matrix products, arithmetic and copies ran while one was open for 34% of the time, Pallas kernels for 0%

profile of v2, /device:TPU:0, one launch (start us, length us, event | category | flops | bytes accessed | tf_op | source)
XLA Modules:
  0.0 921.5 jit_solution(9409525190102696060)
XLA Ops:
  73.5 16.3 %collective-permute-done.7 = bf16[1152,384]{1,0:T(8,128)(2,1)} collective-permute-done((bf16[1152,384]{1,0:T(8,128)(2,1)S(1)}, bf16[1152,384]{1,0:T(8,128)(2,1)}, u32[]{:S(2)}, u32[]{:S(2)}) %collective-permute-start.7) | collective-permute-done | bytes 884768 | tf_op jit(solution)/shard_map/ppermute | solution.py:115
  156.2 18.4 %collective-permute-done.25 = bf16[256,1152]{1,0:T(8,128)(2,1)S(1)} collective-permute-done((bf16[256,1152]{1,0:T(8,128)(2,1)}, bf16[256,1152]{1,0:T(8,128)(2,1)S(1)}, u32[]{:S(2)}, u32[]{:S(2)}) %collective-permute-start.25) | collective-permute-done | bytes 589856 | tf_op jit(solution)/shard_map/ppermute | solution.py:115
  178.0 23.8 %collective-permute-start.103 = (bf16[57,128,128]{2,1,0:T(8,128)(2,1)}, bf16[57,128,128]{2,1,0:T(8,128)(2,1)}, u32[]{:S(2)}, u32[]{:S(2)}) collective-permute-start(bf16[57,128,128]{2,1,0:T(8,128)(2,1)} %collective-permute-done.101), channel_id=1, source_target_pairs={{0,8},{8,0},{16,24},{24,16},{1,9},{9,1},{17,25},{25,17},{2,10},{10... | collective-permute-start | bytes 5603336 | tf_op jit(solution)/shard_map/ppermute | solution.py:109
  212.6 52.2 %collective-permute-done.98 = bf16[57,144,144]{2,1,0:T(8,128)(2,1)} collective-permute-done((bf16[57,144,144]{2,1,0:T(8,128)(2,1)}, bf16[57,144,144]{2,1,0:T(8,128)(2,1)}, u32[]{:S(2)}, u32[]{:S(2)}) %collective-permute-start.98) | collective-permute-done | bytes 2363936 | tf_op jit(solution)/shard_map/ppermute | solution.py:115
  264.8 10.9 %collective-permute-done.35 = bf16[256,1152]{1,0:T(8,128)(2,1)} collective-permute-done((bf16[256,1152]{1,0:T(8,128)(2,1)}, bf16[256,1152]{1,0:T(8,128)(2,1)}, u32[]{:S(2)}, u32[]{:S(2)}) %collective-permute-start.35) | collective-permute-done | bytes 589856 | tf_op jit(solution)/shard_map/ppermute | solution.py:115
  275.7 10.7 %fusion.112 = f32[1024,1792]{1,0:T(8,128)} fusion(bf16[1152,1792]{1,0:T(8,128)(2,1)} %all-gather.4.cloned.1.call-done, bf16[256,1152]{1,0:T(8,128)(2,1)} %copy-done.67, bf16[256,1152]{1,0:T(8,128)(2,1)} %collective-permute-done.26, bf16[256,1152]{1,0:T(8,128)(2,1)S(1)} %collective-permute-done.25, bf16[256,1152]{1,0:T(8,128)(2,1)} %get-tuple-element.133), kind=kOutput, calls=%fused_computation.300 | convolution fusion | flops 4237295616 | bytes 13828096 | tf_op jit(solution)/shard_map/dot_general | solution.py:97
  286.4 12.8 %multiply_convert_fusion.3 = (bf16[1024,1792]{1,0:T(8,128)(2,1)}, f32[1024,1792]{1,0:T(8,128)}) fusion(f32[1024,1792]{1,0:T(8,128)} %fusion.112, bf16[1152,1792]{1,0:T(8,128)(2,1)} %all-gather.6.cloned.1.call-done, bf16[256,1152]{1,0:T(8,128)(2,1)} %copy-done.67, bf16[256,1152]{1,0:T(8,128)(2,1)} %collective-permute-done.26, ...), kind=kOutput, calls=%fused_computation.43 | convolution fusion | flops 4255645696 | bytes 24838144 | tf_op jit(solution)/shard_map/dot_general | solution.py:97
  308.3 9.8 %fusion.110 = f32[1024,1792]{1,0:T(8,128)} fusion(bf16[1152,1792]{1,0:T(8,128)(2,1)S(1)} %copy-done.133, bf16[256,1152]{1,0:T(8,128)(2,1)} %collective-permute-done.37, bf16[256,1152]{1,0:T(8,128)(2,1)} %collective-permute-done.36, bf16[256,1152]{1,0:T(8,128)(2,1)} %collective-permute-done.35, bf16[256,1152]{1,0:T(8,128)(2,1)} %get-tuple-element.131), kind=kOutput, calls=%fused_computation.298 | convolution fusion | flops 4237295616 | bytes 13828096 | tf_op jit(solution)/shard_map/dot_general | solution.py:97
  318.1 12.0 %multiply_convert_fusion.2 = (bf16[1024,1792]{1,0:T(8,128)(2,1)}, f32[1024,1792]{1,0:T(8,128)}) fusion(f32[1024,1792]{1,0:T(8,128)} %fusion.110, bf16[1152,1792]{1,0:T(8,128)(2,1)S(1)} %copy-done.134, bf16[256,1152]{1,0:T(8,128)(2,1)} %collective-permute-done.37, bf16[256,1152]{1,0:T(8,128)(2,1)} %collective-permute-done.36, ...), kind=kOutput, calls=%fused_computation.42 | convolution fusion | flops 4255645696 | bytes 24838144 | tf_op jit(solution)/shard_map/dot_general | solution.py:97
  350.4 12.6 %collective-permute-done.29 = bf16[256,1152]{1,0:T(8,128)(2,1)S(1)} collective-permute-done((bf16[256,1152]{1,0:T(8,128)(2,1)S(1)}, bf16[256,1152]{1,0:T(8,128)(2,1)S(1)}, u32[]{:S(2)}, u32[]{:S(2)}) %collective-permute-start.29) | collective-permute-done | bytes 589856 | tf_op jit(solution)/shard_map/ppermute | solution.py:115
  363.3 12.0 %collective-permute-done.39 = bf16[256,1152]{1,0:T(8,128)(2,1)S(1)} collective-permute-done((bf16[256,1152]{1,0:T(8,128)(2,1)S(1)}, bf16[256,1152]{1,0:T(8,128)(2,1)S(1)}, u32[]{:S(2)}, u32[]{:S(2)}) %collective-permute-start.39) | collective-permute-done | bytes 589856 | tf_op jit(solution)/shard_map/ppermute | solution.py:115
  398.7 16.8 %multiply_convert_fusion.1 = (bf16[1024,1792]{1,0:T(8,128)(2,1)}, bf16[1024,1792]{1,0:T(8,128)(2,1)}) fusion(f32[1024,1792]{1,0:T(8,128)} %fusion.112, f32[1024,1792]{1,0:T(8,128)} %get-tuple-element.231, bf16[1152,1792]{1,0:T(8,128)(2,1)} %all-gather.8.cloned.1.call-done, bf16[256,1152]{1,0:T(8,128)(2,1)S(1)} %collective-permute-done.42, ...), kind=kOutput, calls=%fused_computation.41 | convolution fusion | flops 4281335808 | bytes 28508160 | tf_op jit(solution)/shard_map/dot_general | solution.py:97
  440.0 17.0 %multiply_convert_fusion = (bf16[1024,1792]{1,0:T(8,128)(2,1)}, bf16[1024,1792]{1,0:T(8,128)(2,1)}) fusion(f32[1024,1792]{1,0:T(8,128)} %fusion.110, f32[1024,1792]{1,0:T(8,128)} %get-tuple-element.233, bf16[1152,1792]{1,0:T(8,128)(2,1)} %all-gather.8.cloned.1.call-done, bf16[256,1152]{1,0:T(8,128)(2,1)S(1)} %collective-permute-done.47, ...), kind=kOutput, calls=%fused_computation.40 | convolution fusion | flops 4281335808 | bytes 28508160 | tf_op jit(solution)/shard_map/dot_general | solution.py:97
  457.1 12.4 %convolution_convert_fusion.2 = bf16[1152,1792]{1,0:T(8,128)(2,1)S(1)} fusion(bf16[2048,1152]{1,0:T(8,128)(2,1)S(1)} %constant_dynamic-update-slice_fusion, bf16[1024,1792]{1,0:T(8,128)(2,1)} %get-tuple-element.154, bf16[1024,1792]{1,0:T(8,128)(2,1)} %get-tuple-element.152), kind=kOutput, calls=%fused_computation.16 | convolution fusion | flops 8472461312 | bytes 16187392 | tf_op jit(solution)/shard_map/dot_general | solution.py:105
  480.9 12.6 %convolution_convert_fusion.1 = bf16[1152,1792]{1,0:T(8,128)(2,1)} fusion(bf16[2048,1152]{1,0:T(8,128)(2,1)S(1)} %constant_dynamic-update-slice_fusion, bf16[1024,1792]{1,0:T(8,128)(2,1)} %get-tuple-element.153, bf16[1024,1792]{1,0:T(8,128)(2,1)S(1)} %copy-done.138), kind=kOutput, calls=%fused_computation.15 | convolution fusion | flops 8472461312 | bytes 16187392 | tf_op jit(solution)/shard_map/dot_general | solution.py:105
  518.9 9.9 %collective-permute-start.61 = (bf16[144,1792]{1,0:T(8,128)(2,1)}, bf16[144,1792]{1,0:T(8,128)(2,1)}, u32[]{:S(2)}, u32[]{:S(2)}) collective-permute-start(bf16[144,1792]{1,0:T(8,128)(2,1)} %get-tuple-element.171), channel_id=1, source_target_pairs={{0,4},{1,5},{2,6},{3,7},{4,0},{5,1},{6,2},{7,3},{8,12},{9,13},{10,... | collective-permute-start | bytes 1548296 | tf_op jit(solution)/shard_map/ppermute | solution.py:164
  528.9 12.9 %convolution_convert_fusion = bf16[1152,1792]{1,0:T(8,128)(2,1)} fusion(bf16[2048,1152]{1,0:T(8,128)(2,1)S(1)} %constant_dynamic-update-slice_fusion.8, bf16[1024,1792]{1,0:T(8,128)(2,1)} %get-tuple-element.232, bf16[1024,1792]{1,0:T(8,128)(2,1)S(1)} %copy-done.139), kind=kOutput, calls=%fused_computation.14 | convolution fusion | flops 8472461312 | bytes 16187392 | tf_op jit(solution)/shard_map/dot_general | solution.py:105
  546.0 15.2 %collective-permute-done.61 = bf16[144,1792]{1,0:T(8,128)(2,1)} collective-permute-done((bf16[144,1792]{1,0:T(8,128)(2,1)}, bf16[144,1792]{1,0:T(8,128)(2,1)}, u32[]{:S(2)}, u32[]{:S(2)}) %collective-permute-start.61) | collective-permute-done | bytes 516128 | tf_op jit(solution)/shard_map/ppermute | solution.py:164
  656.5 34.9 %collective-permute-start.73 = (bf16[144,1792]{1,0:T(8,128)(2,1)}, bf16[144,1792]{1,0:T(8,128)(2,1)}, u32[]{:S(2)}, u32[]{:S(2)}) collective-permute-start(bf16[144,1792]{1,0:T(8,128)(2,1)} %get-tuple-element.163), channel_id=1, source_target_pairs={{0,2},{1,3},{2,0},{3,1},{4,6},{5,7},{6,4},{7,5},{8,10},{9,11},{10,... | collective-permute-start | bytes 1548296 | tf_op jit(solution)/shard_map/ppermute | solution.py:164
  736.4 37.6 %collective-permute-done.94 = f32[5120]{0:T(1024)S(1)} collective-permute-done((f32[5120]{0:T(1024)S(1)}, f32[5120]{0:T(1024)S(1)}, u32[]{:S(2)}, u32[]{:S(2)}) %collective-permute-start.94) | collective-permute-done | bytes 20512 | tf_op jit(solution)/shard_map/ppermute | solution.py:154
  801.5 15.3 %collective-permute-start.85 = (bf16[144,640]{1,0:T(8,128)(2,1)S(1)}, bf16[144,640]{1,0:T(8,128)(2,1)S(1)}, u32[]{:S(2)}, u32[]{:S(2)}) collective-permute-start(bf16[144,640]{1,0:T(8,128)(2,1)S(1)} %get-tuple-element.189), channel_id=1, source_target_pairs={{0,3},{1,2},{2,1},{3,0},{4,7},{5,6},{6,5},{7,4},{8,11},{9,10},{10,... | collective-permute-start | bytes 552968 | tf_op jit(solution)/shard_map/ppermute | solution.py:218
  842.2 10.7 %collective-permute-done.78 = bf16[144,1792]{1,0:T(8,128)(2,1)S(1)} collective-permute-done((bf16[144,1792]{1,0:T(8,128)(2,1)}, bf16[144,1792]{1,0:T(8,128)(2,1)S(1)}, u32[]{:S(2)}, u32[]{:S(2)}) %collective-permute-start.78) | collective-permute-done | bytes 516128 | tf_op jit(solution)/shard_map/ppermute | solution.py:115
  855.7 12.3 %owner_stats.2 = (f32[57,144,128]{2,1,0:T(8,128)}, f32[57,144,144]{2,1,0:T(8,128)}, f32[57,128,128]{2,1,0:T(8,128)}) custom-call(s32[57]{0:T(128)S(1)} %get-tuple-element.120.refs_0_, s32[57]{0:T(128)S(1)} %get-tuple-element.119.refs_1_, s32[57]{0:T(128)S(1)} %get-tuple-element.118.refs_2_, s32[57]{0:T(128)S(1)} %get-tuple-element.117.refs_3_, ...), custom_call_target="tpu_custom_call" | custom-call | tf_op jit(solution)/shard_map/owner_stats/pallas_call | solution.py:332
  876.1 31.5 %update_blocks.2 = (f32[144,23296]{1,0:T(8,128)}, bf16[144,23296]{1,0:T(8,128)(2,1)}) custom-call(s32[161]{0:T(256)S(1)} %slice.281.refs_0_, s32[161]{0:T(256)S(1)} %copy-done.1, s32[161]{0:T(256)S(1)} %copy-done.2, s32[161]{0:T(256)S(1)} %slice.284.refs_3_, s32[161]{0:T(256)S(1)} %slice.285.refs_4_, ...), custom_call_target="tpu_custom_call" | custom-call | tf_op jit(solution)/shard_map/update_blocks/pallas_call | solution.py:286
  (742 shorter events, 471.0 us)
Async XLA Ops:
  7.2 268.5 %all-gather.4.cloned.1.call-start = ((), (), s32[]{:S(2)}) async-start(), calls=%async_computation.1 | async-start | bytes 4644864 | tf_op jit(solution)/shard_map/all_gather | solution.py:473
  10.5 275.9 %all-gather.6.cloned.1.call-start = ((), (), s32[]{:S(2)}) async-start(), calls=%async_computation.2 | async-start | bytes 4644864 | tf_op jit(solution)/shard_map/all_gather | solution.py:474
  11.2 288.0 %all-gather.8.cloned.1.call-start = ((), (), s32[]{:S(2)}) async-start(), calls=%async_computation.3 | async-start | bytes 4644864 | tf_op jit(solution)/shard_map/all_gather | solution.py:475
  21.1 817.4 %reduce-scatter.2.cloned.1.call-start = ((), (), s32[]{:S(2)}) async-start(), calls=%async_computation.4 | async-start | bytes 4644864 | tf_op jit(solution)/shard_map/reduce_scatter | solution.py:549
  118.1 59.9 %collective-permute-start.101 = (bf16[57,128,128]{2,1,0:T(8,128)(2,1)}, bf16[57,128,128]{2,1,0:T(8,128)(2,1)}, u32[]{:S(2)}, u32[]{:S(2)}) collective-permute-start(bf16[57,128,128]{2,1,0:T(8,128)(2,1)} %bitcast.58), channel_id=1, source_target_pairs={{0,16},{8,24},{16,0},{24,8},{1,17},{9,25},{17,1},{25,9},{2,18},{10... | collective-permute-start | bytes 5603336 | tf_op jit(solution)/shard_map/ppermute | solution.py:115
  139.4 125.4 %collective-permute-start.98 = (bf16[57,144,144]{2,1,0:T(8,128)(2,1)}, bf16[57,144,144]{2,1,0:T(8,128)(2,1)}, u32[]{:S(2)}, u32[]{:S(2)}) collective-permute-start(bf16[57,144,144]{2,1,0:T(8,128)(2,1)} %bitcast.52), channel_id=1, source_target_pairs={{0,16},{8,24},{16,0},{24,8},{1,17},{9,25},{17,1},{25,9},{2,18},{10... | collective-permute-start | bytes 7091720 | tf_op jit(solution)/shard_map/ppermute | solution.py:115
  141.0 68.6 %collective-permute-start.102 = (bf16[57,128,128]{2,1,0:T(8,128)(2,1)}, bf16[57,128,128]{2,1,0:T(8,128)(2,1)}, u32[]{:S(2)}, u32[]{:S(2)}) collective-permute-start(bf16[57,128,128]{2,1,0:T(8,128)(2,1)} %bitcast.58), channel_id=1, source_target_pairs={{0,8},{8,0},{16,24},{24,16},{1,9},{9,1},{17,25},{25,17},{2,10},{10... | collective-permute-start | bytes 5603336 | tf_op jit(solution)/shard_map/ppermute | solution.py:109
  175.5 166.4 %collective-permute-start.99 = (bf16[57,144,144]{2,1,0:T(8,128)(2,1)}, bf16[57,144,144]{2,1,0:T(8,128)(2,1)}, u32[]{:S(2)}, u32[]{:S(2)}) collective-permute-start(bf16[57,144,144]{2,1,0:T(8,128)(2,1)} %bitcast.52), channel_id=1, source_target_pairs={{0,8},{8,0},{16,24},{24,16},{1,9},{9,1},{17,25},{25,17},{2,10},{10... | collective-permute-start | bytes 7091720 | tf_op jit(solution)/shard_map/ppermute | solution.py:109
  178.0 203.6 %collective-permute-start.103 = (bf16[57,128,128]{2,1,0:T(8,128)(2,1)}, bf16[57,128,128]{2,1,0:T(8,128)(2,1)}, u32[]{:S(2)}, u32[]{:S(2)}) collective-permute-start(bf16[57,128,128]{2,1,0:T(8,128)(2,1)} %collective-permute-done.101), channel_id=1, source_target_pairs={{0,8},{8,0},{16,24},{24,16},{1,9},{9,1},{17,25},{25,17},{2,10},{10... | collective-permute-start | bytes 5603336 | tf_op jit(solution)/shard_map/ppermute | solution.py:109
  204.6 71.1 %collective-permute-start.35 = (bf16[256,1152]{1,0:T(8,128)(2,1)}, bf16[256,1152]{1,0:T(8,128)(2,1)}, u32[]{:S(2)}, u32[]{:S(2)}) collective-permute-start(bf16[256,1152]{1,0:T(8,128)(2,1)} %get-tuple-element.131), channel_id=1, source_target_pairs={{0,16},{8,24},{16,0},{24,8},{1,17},{9,25},{17,1},{25,9},{2,18},{10... | collective-permute-start | bytes 1769480 | tf_op jit(solution)/shard_map/ppermute | solution.py:115
  212.6 95.1 %collective-permute-start.36 = (bf16[256,1152]{1,0:T(8,128)(2,1)}, bf16[256,1152]{1,0:T(8,128)(2,1)}, u32[]{:S(2)}, u32[]{:S(2)}) collective-permute-start(bf16[256,1152]{1,0:T(8,128)(2,1)} %get-tuple-element.131), channel_id=1, source_target_pairs={{0,8},{8,0},{16,24},{24,16},{1,9},{9,1},{17,25},{25,17},{2,10},{10... | collective-permute-start | bytes 1769480 | tf_op jit(solution)/shard_map/ppermute | solution.py:109
  264.8 167.6 %collective-permute-start.100 = (bf16[57,144,144]{2,1,0:T(8,128)(2,1)}, bf16[57,144,144]{2,1,0:T(8,128)(2,1)}, u32[]{:S(2)}, u32[]{:S(2)}) collective-permute-start(bf16[57,144,144]{2,1,0:T(8,128)(2,1)} %collective-permute-done.98), channel_id=1, source_target_pairs={{0,8},{8,0},{16,24},{24,16},{1,9},{9,1},{17,25},{25,17},{2,10},{10... | collective-permute-start | bytes 7091720 | tf_op jit(solution)/shard_map/ppermute | solution.py:109
  470.5 44.5 %collective-permute-start.58 = (bf16[144,1792]{1,0:T(8,128)(2,1)S(1)}, bf16[144,1792]{1,0:T(8,128)(2,1)S(1)}, u32[]{:S(2)}, u32[]{:S(2)}) collective-permute-start(bf16[144,1792]{1,0:T(8,128)(2,1)S(1)} %get-tuple-element.172), channel_id=1, source_target_pairs={{0,1},{1,0},{2,3},{3,2},{4,5},{5,4},{6,7},{7,6},{8,9},{9,8},{10,11... | collective-permute-start | bytes 1548296 | tf_op jit(solution)/shard_map/ppermute | solution.py:164
  513.7 61.4 %collective-permute-start.48 = (bf16[512,1152]{1,0:T(8,128)(2,1)}, bf16[512,1152]{1,0:T(8,128)(2,1)}, u32[]{:S(2)}, u32[]{:S(2)}) collective-permute-start(bf16[512,1152]{1,0:T(8,128)(2,1)} %slice.472), channel_id=1, source_target_pairs={{0,8},{8,0},{16,24},{24,16},{1,9},{9,1},{17,25},{25,17},{2,10},{10... | collective-permute-start | bytes 3538952 | tf_op jit(solution)/shard_map/ppermute | solution.py:109
  528.8 44.0 %collective-permute-start.59 = (bf16[144,1792]{1,0:T(8,128)(2,1)}, bf16[144,1792]{1,0:T(8,128)(2,1)}, u32[]{:S(2)}, u32[]{:S(2)}) collective-permute-start(bf16[144,1792]{1,0:T(8,128)(2,1)} %get-tuple-element.169), channel_id=1, source_target_pairs={{0,6},{1,7},{2,4},{3,5},{4,2},{5,3},{6,0},{7,1},{8,14},{9,15},{10,... | collective-permute-start | bytes 1548296 | tf_op jit(solution)/shard_map/ppermute | solution.py:164
  544.3 64.7 %collective-permute-start.44 = (bf16[256,1152]{1,0:T(8,128)(2,1)S(1)}, bf16[256,1152]{1,0:T(8,128)(2,1)S(1)}, u32[]{:S(2)}, u32[]{:S(2)}) collective-permute-start(bf16[256,1152]{1,0:T(8,128)(2,1)S(1)} %slice.477), channel_id=1, source_target_pairs={{0,16},{8,24},{16,0},{24,8},{1,17},{9,25},{17,1},{25,9},{2,18},{10... | collective-permute-start | bytes 1769480 | tf_op jit(solution)/shard_map/ppermute | solution.py:115
  544.8 183.0 %collective-permute-start.74 = (bf16[144,1792]{1,0:T(8,128)(2,1)}, bf16[144,1792]{1,0:T(8,128)(2,1)}, u32[]{:S(2)}, u32[]{:S(2)}) collective-permute-start(bf16[144,1792]{1,0:T(8,128)(2,1)} %get-tuple-element.166), channel_id=1, source_target_pairs={{0,1},{1,0},{2,3},{3,2},{4,5},{5,4},{6,7},{7,6},{8,9},{9,8},{10,11... | collective-permute-start | bytes 1548296 | tf_op jit(solution)/shard_map/ppermute | solution.py:164
  637.4 63.7 %collective-permute-start.50 = (bf16[256,512]{1,0:T(8,128)(2,1)}, bf16[256,512]{1,0:T(8,128)(2,1)S(1)}, u32[]{:S(2)}, u32[]{:S(2)}) collective-permute-start(bf16[256,512]{1,0:T(8,128)(2,1)} %fusion.101), channel_id=1, source_target_pairs={{1,0},{2,1},{3,2},{9,8},{10,9},{11,10},{17,16},{18,17},{19,18},{25... | collective-permute-start | bytes 786440 | tf_op jit(solution)/shard_map/ppermute | solution.py:396
  647.0 44.4 %collective-permute-start.57 = (bf16[256,512]{1,0:T(8,128)(2,1)}, bf16[256,512]{1,0:T(8,128)(2,1)}, u32[]{:S(2)}, u32[]{:S(2)}) collective-permute-start(bf16[256,512]{1,0:T(8,128)(2,1)} %add_convert_fusion.11), channel_id=1, source_target_pairs={{2,0},{3,1},{4,2},{5,3},{10,8},{11,9},{12,10},{13,11},{18,16},{19,... | collective-permute-start | bytes 786440 | tf_op jit(solution)/shard_map/ppermute | solution.py:399
  649.0 52.1 %collective-permute-start.53 = (bf16[256,512]{1,0:T(8,128)(2,1)}, bf16[256,512]{1,0:T(8,128)(2,1)}, u32[]{:S(2)}, u32[]{:S(2)}) collective-permute-start(bf16[256,512]{1,0:T(8,128)(2,1)} %add_convert_fusion.12), channel_id=1, source_target_pairs={{2,0},{3,1},{4,2},{5,3},{10,8},{11,9},{12,10},{13,11},{18,16},{19,... | collective-permute-start | bytes 786440 | tf_op jit(solution)/shard_map/ppermute | solution.py:399
  656.5 72.1 %collective-permute-start.73 = (bf16[144,1792]{1,0:T(8,128)(2,1)}, bf16[144,1792]{1,0:T(8,128)(2,1)}, u32[]{:S(2)}, u32[]{:S(2)}) collective-permute-start(bf16[144,1792]{1,0:T(8,128)(2,1)} %get-tuple-element.163), channel_id=1, source_target_pairs={{0,2},{1,3},{2,0},{3,1},{4,6},{5,7},{6,4},{7,5},{8,10},{9,11},{10,... | collective-permute-start | bytes 1548296 | tf_op jit(solution)/shard_map/ppermute | solution.py:164
  727.8 61.4 %collective-permute-start.82 = (bf16[1152,640]{1,0:T(8,128)(2,1)S(1)}, bf16[1152,640]{1,0:T(8,128)(2,1)S(1)}, u32[]{:S(2)}, u32[]{:S(2)}) collective-permute-start(bf16[1152,640]{1,0:T(8,128)(2,1)S(1)} %slice.471), channel_id=1, source_target_pairs={{0,16},{8,24},{16,0},{24,8},{1,17},{9,25},{17,1},{25,9},{2,18},{10... | collective-permute-start | bytes 4423688 | tf_op jit(solution)/shard_map/ppermute | solution.py:115
  735.1 60.0 %collective-permute-start.76 = (bf16[144,1792]{1,0:T(8,128)(2,1)S(1)}, bf16[144,1792]{1,0:T(8,128)(2,1)S(1)}, u32[]{:S(2)}, u32[]{:S(2)}) collective-permute-start(bf16[144,1792]{1,0:T(8,128)(2,1)S(1)} %get-tuple-element.129), channel_id=1, source_target_pairs={{0,8},{8,0},{16,24},{24,16},{1,9},{9,1},{17,25},{25,17},{2,10},{10... | collective-permute-start | bytes 1548296 | tf_op jit(solution)/shard_map/ppermute | solution.py:109
  776.4 57.9 %collective-permute-start.77 = (bf16[144,1792]{1,0:T(8,128)(2,1)S(1)}, bf16[144,1792]{1,0:T(8,128)(2,1)S(1)}, u32[]{:S(2)}, u32[]{:S(2)}) collective-permute-start(bf16[144,1792]{1,0:T(8,128)(2,1)S(1)} %collective-permute-done.75), channel_id=1, source_target_pairs={{0,8},{8,0},{16,24},{24,16},{1,9},{9,1},{17,25},{25,17},{2,10},{10... | collective-permute-start | bytes 1548296 | tf_op jit(solution)/shard_map/ppermute | solution.py:109
  (230 other events, 3505.0 us)
Sparse Core Ops, SparseCore 0:
  10.8 89.8 all-gather.3
  103.4 81.0 all-gather.5
  186.8 70.8 all-gather.7
  541.9 119.4 reduce-scatter.1

commit v3 on v2

--- a/solution.py
+++ b/solution.py
@@ -164,13 +164,14 @@
     return lax.ppermute(value, "fsdp", [(e, e ^ flip) for e in range(nf)])
 
 
-def gather_rows(own, nf):
+def gather_rows(own, nf, ties=()):
     if nf > DIRECT_MAX:
         return lax.all_gather(own, "fsdp", axis=0, tiled=True)
     me = lax.axis_index("fsdp")
     band, width = own.shape
     straight = [own] + [swap_fsdp(own, flip, nf) for flip in range(2, nf, 2)]
-    crossed = [swap_fsdp(part, 1, nf) for part in straight]
+    passed = [own] + [after(part, *ties) if ties else part for part in straight[1:]]
+    crossed = [swap_fsdp(part, 1, nf) for part in passed]
     whole = jnp.zeros((nf * band, width), own.dtype)
     for k in range(nf // 2):
         whole = lax.dynamic_update_slice(whole, straight[k], ((me ^ (2 * k)) * band, 0))
@@ -178,45 +179,10 @@
     return whole
 
 
-def add_low(left, right):
-    return (left.astype(F32) + right.astype(F32)).astype(BF)
-
-
-def reduce_rows(terms, nf):
-    if nf > DIRECT_MAX:
-        return lax.psum_scatter(terms, "fsdp", scatter_dimension=0, tiled=True)
-    me = lax.axis_index("fsdp")
-    band, width = (terms.shape[0] // nf, terms.shape[1])
-
-    def part(flip):
-        return lax.dynamic_slice(terms, ((me ^ flip) * band, 0), (band, width))
-
-    sums = []
-    for k in range(nf // 2 - 1, -1, -1):
-        received = swap_fsdp(part(2 * k + 1), 1, nf)
-        if k:
-            sums.append(swap_fsdp(add_low(part(2 * k), received), 2 * k, nf))
-        else:
-            sums.append(received)
-    total = part(0).astype(F32)
-    for piece in sums:
-        total = total + piece.astype(F32)
-    return total.astype(BF)
-
-
 def direct_reduce(terms, nf):
     band, width = (terms.shape[0] // nf, terms.shape[1])
-    if nf > DIRECT_MAX:
-        spread = lax.all_to_all(
-            terms.reshape(nf, band, width), "fsdp", split_axis=0, concat_axis=0
-        )
-        return jnp.sum(spread.astype(F32), axis=0).astype(BF)
-    me = lax.axis_index("fsdp")
-    total = lax.dynamic_slice(terms, (me * band, 0), (band, width)).astype(F32)
-    for flip in range(1, nf):
-        sent = lax.dynamic_slice(terms, ((me ^ flip) * band, 0), (band, width))
-        total = total + lax.ppermute(sent, "fsdp", [(e, e ^ flip) for e in range(nf)]).astype(F32)
-    return total.astype(BF)
+    spread = lax.all_to_all(terms.reshape(nf, band, width), "fsdp", split_axis=0, concat_axis=0)
+    return jnp.sum(spread.astype(F32), axis=0).astype(BF)
 
 
 def dot_on(left, right, left_dim, right_dim):
@@ -231,19 +197,26 @@
     return jnp.where(flags[at] > 0, sources[1][...], sources[0][...])
 
 
-def update_body(group, count, flags, refs):
+def update_body(group, count, pieces, flags, refs):
     grads = refs[: group * count]
-    lefts = refs[group * count : group * (count + 1)]
-    rights = refs[group * (count + 1) : group * (count + 2)]
-    master_ref, new_ref, low_ref = (refs[group * (count + 2)], refs[-2], refs[-1])
+    lefts = refs[group * count : group * (count + pieces)]
+    rights = refs[group * (count + pieces) : group * (count + pieces + 1)]
+    master_ref, new_ref, low_ref = (refs[group * (count + pieces + 1)], refs[-2], refs[-1])
+    base = pl.program_id(0) * group
+    shaped = []
     for j in range(group):
-        grad = pick_grad(grads[j * count : (j + 1) * count], flags, pl.program_id(0) * group + j)
-        shaped = dot_on(lefts[j][...], grad, 1, 0)
-        shaped = dot_on(shaped.astype(BF), rights[j][...], 1, 0)
-        power = jnp.sum(jnp.sum(shaped * shaped, axis=1, keepdims=True), axis=0, keepdims=True)
-        factor = -RATE * lax.rsqrt(power * (1.0 / (shaped.shape[0] * shaped.shape[1])) + EPSILON)
+        grad = pick_grad(grads[j * count : (j + 1) * count], flags, base + j)
+        product = dot_on(lefts[j][...], grad[: lefts[j].shape[1]], 1, 0)
+        if pieces > 1:
+            product = product + dot_on(lefts[group + j][...], grad[lefts[j].shape[1] :], 0, 0)
+        shaped.append(product.astype(BF))
+    shaped = [dot_on(shaped[j], rights[j][...], 1, 0) for j in range(group)]
+    scale = 1.0 / (shaped[0].shape[0] * shaped[0].shape[1])
+    powers = [jnp.sum(jnp.sum(s * s, axis=0, keepdims=True), axis=1, keepdims=True) for s in shaped]
+    factors = [-RATE * lax.rsqrt(power * scale + EPSILON) for power in powers]
+    for j in range(group):
         at = pl.ds(j * BC, BC)
-        fresh = master_ref[:, at] + shaped * factor
+        fresh = master_ref[:, at] + shaped[j] * factors[j]
         new_ref[:, at] = fresh
         low_ref[:, at] = fresh.astype(BF)
 
@@ -273,10 +246,11 @@
 
     wide = pl.BlockSpec((band, group * BC), lambda i, *tables: (0, i + skip))
     in_specs = grad_specs(sources, group, 0, band)
-    in_specs += [root_spec(left_roots.shape[1:], j) for j in range(group)]
+    in_specs += [root_spec(left.shape[1:], j) for left in left_roots for j in range(group)]
     in_specs += [root_spec(right_roots.shape[1:], j) for j in range(group)]
     in_specs += [wide]
-    operands = list(sources) * group + [left_roots] * group + [right_roots] * group + [master]
+    operands = list(sources) * group + [left for left in left_roots for _ in range(group)]
+    operands += [right_roots] * group + [master]
     tables = list(places) + [roots]
     aliases = {}
     if into is not None:
@@ -284,7 +258,7 @@
         in_specs += [pl.BlockSpec(memory_space=pl.ANY)] * 2
         operands += list(into)
     return pl.pallas_call(
-        lambda *refs: update_body(group, len(sources), refs[3], refs[5:]),
+        lambda *refs: update_body(group, len(sources), len(left_roots), refs[3], refs[5:]),
         grid_spec=pltpu.PrefetchScalarGridSpec(
             num_scalar_prefetch=5,
             grid=(count // group,),
@@ -455,23 +429,44 @@
     def columns(at, size):
         return lax.dynamic_slice(master, (0, at), (band, size)).astype(BF)
 
-    def quarters(at, size):
-        part = size // nd
-        mine = gather_rows(columns(at + dp_me * part, part), nf)
+    def gather_relative(bands, *ties):
+        parts = [gather_parts(part, nd) for part in bands]
+        if ties:
+            parts = [[after(piece, *ties) for piece in pieces] for pieces in parts]
+        out = jnp.zeros((nd, len(bands)) + bands[0].shape, BF)
+        for kind, pieces in enumerate(parts):
+            for place, piece in enumerate(pieces):
+                out = lax.dynamic_update_slice(
+                    out, piece[None, None], (place, kind) + (0,) * piece.ndim
+                )
+        return out
+
+    def gather_columns(bands):
+        out = jnp.zeros((nd, 1, band, sum(part.shape[1] for part in bands)), BF)
+        at = 0
+        for part in bands:
+            for place, piece in enumerate(gather_parts(part, nd)):
+                out = lax.dynamic_update_slice(out, piece[None, None], (place, 0, 0, at))
+            at += part.shape[1]
+        return out
+
+    def halves(at, size, first_ties, next_ties):
+        part = size // 2
+        cols = columns(at + core * part, part)
+        mine = gather_rows(after(cols, *first_ties) if first_ties else cols, nf, next_ties)
         whole = jnp.zeros((D, size), BF)
-        for piece, index in zip(gather_parts(mine, nd), part_owners(nd)):
-            whole = lax.dynamic_update_slice(whole, piece, (0, index * part))
-        return whole
-
-    w_qkv = quarters(0, QKVW)
-    w_out = quarters(QKVW, OUTW)
+        whole = lax.dynamic_update_slice(whole, mine, (0, core * part))
+        return lax.dynamic_update_slice(whole, swap_core(mine, nd), (0, (1 - core) * part))
+
+    w_qkv = halves(0, QKVW, (), ())
     gate_cols = columns(gate_at + start * BC, width)
     up_cols = columns(gate_at + FF + start * BC, width)
     down_cols = columns(gate_at + 2 * FF + start * BC, width)
     keep = (jnp.arange(width, dtype=jnp.int32) >= fresh * BC)[None, :]
     down_cols = jnp.where(keep, down_cols, jnp.zeros_like(down_cols))
-    w_gate = lax.all_gather(gate_cols, "fsdp", axis=0, tiled=True)
-    w_up = lax.all_gather(up_cols, "fsdp", axis=0, tiled=True)
+    both_cols = jnp.concatenate([gate_cols, up_cols], axis=1)
+    w_both = lax.all_gather(both_cols, "fsdp", axis=0, tiled=True)
+    w_gate, w_up = (w_both[:, :width], w_both[:, width:])
     w_down = lax.all_gather(down_cols, "fsdp", axis=0, tiled=True)
 
     flat_in = tokens.astype(F32).reshape(count, D)
@@ -489,6 +484,7 @@
     own_keys = jnp.concatenate([rot_keys.astype(BF), values.astype(BF)], axis=1)
     key_buffers = [spread_keys(own_keys[m * rows : (m + 1) * rows], nf) for m in range(micros)]
     key_slots = key_slots_of(rows, nf)
+    w_out = halves(QKVW, OUTW, (projected,), (key_buffers[0],))
     keys_all = [buffer[:, :HD] for buffer in key_buffers]
     values_all = [buffer[:, HD:] for buffer in key_buffers]
     all_probs, all_attended = [], []
@@ -506,64 +502,78 @@
         branch_one = dot_nt(all_attended[m], w_out)
         resid = part_in + rms_gain(branch_one, post_attn)
         ffw_in = rms_gain(resid, pre_ffw).astype(BF)
-        every_in = gather_dp(ffw_in, nd)
+        gathered_in.append(gather_dp(ffw_in, nd))
+        saved.append([branch_one, resid])
+    partials = []
+    for m in range(micros):
+        every_in = gathered_in[m]
+        if m:
+            every_in = after(every_in, hiddens[-1])
         gate = dot_nn(every_in, w_gate)
         up = dot_nn(every_in, w_up)
         hidden = (jax.nn.gelu(gate, approximate=True) * up).astype(BF)
-        partial = dot_nt(hidden, w_down)
-        branch_two = scatter_sum_dp(partial[:half], partial[half:], nd)
+        hiddens.append(hidden)
+        saved[m] += [gate, up]
+    for m in range(micros):
+        hidden = after(hiddens[m], partials[-1] if m else hiddens[-1])
+        partials.append(dot_nt(hidden, w_down))
+    last = partials[-1]
+    for m in range(micros):
+        branch_one, resid, gate, up = saved[m]
+        branch_two = scatter_sum_dp(partials[m][:half], partials[m][half:], nd)
         outputs.append((resid + rms_gain(branch_two, post_ffw)).astype(BF))
-        gathered_in.append(every_in)
-        hiddens.append(hidden)
-        saved.append((branch_one, resid, gate, up, branch_two))
-    for m in range(micros):
-        branch_one, resid, gate, up, branch_two = saved[m]
         upstream = cotangent[m, 0].astype(F32)
         grad_two, grad_post_ffw = jax.vjp(rms_gain, branch_two, post_ffw)[1](upstream)
-        every_two = gather_dp(grad_two.astype(BF), nd)
-        grad_hidden = dot_nn(every_two, w_down)
+        gathered_two.append(gather_dp(grad_two.astype(BF), nd))
+        saved[m] += [upstream, grad_post_ffw]
+    for m in range(micros):
+        branch_one, resid, gate, up, upstream, grad_post_ffw = saved[m]
+        grad_hidden = dot_nn(after(gathered_two[m], last), w_down)
         grad_gate, grad_up = jax.vjp(
             lambda gate_in, up_in: jax.nn.gelu(gate_in, approximate=True) * up_in, gate, up
         )[1](grad_hidden)
-        low_gate, low_up = (grad_gate.astype(BF), grad_up.astype(BF))
-        partial = dot_nt(low_gate, w_gate) + dot_nt(low_up, w_up)
+        low_gates.append(grad_gate.astype(BF))
+        low_ups.append(grad_up.astype(BF))
+        last = low_ups[-1]
+
+    def weight_term(lefts, rights, follow):
+        left = jnp.concatenate(lefts, axis=0)
+        term = dot_tn(after(left, *follow), jnp.concatenate(rights, axis=0))
+        return term.astype(BF)
+
+    def from_x(root, *ties):
+        root = after(root, *ties)
+        return [root] + [shift_x(root, nd, k) for k in range(1, nd // 2)]
+
+    right_mine = from_x(root_right[0], *gathered_two)
+    down_term = weight_term(gathered_two, hiddens, (last,))
+    def sum_rows(term):
+        return lax.psum_scatter(term, "fsdp", scatter_dimension=0, tiled=True)
+
+    down_band = sum_rows(down_term)
+    last = down_term
+    for m in range(micros):
+        branch_one, resid, gate, up, upstream, grad_post_ffw = saved[m]
+        ties = [last] if m else [last] + right_mine[1:]
+        partial = dot_nt(after(low_gates[m], *ties), w_gate) + dot_nt(low_ups[m], w_up)
+        last = partial
         grad_ffw_in = scatter_sum_dp(partial[:half], partial[half:], nd)
         grad_resid, grad_pre_ffw = jax.vjp(rms_gain, resid, pre_ffw)[1](grad_ffw_in)
         grad_resid = upstream + grad_resid
         grad_one, grad_post_attn = jax.vjp(rms_gain, branch_one, post_attn)[1](grad_resid)
-        gathered_two.append(every_two)
-        low_gates.append(low_gate)
-        low_ups.append(low_up)
         grad_resids.append(grad_resid)
         low_ones.append(grad_one.astype(BF))
         gain_terms.append((grad_post_attn, grad_pre_ffw, grad_post_ffw))
-
-    def weight_term(lefts, rights):
-        term = dot_tn(jnp.concatenate(lefts, axis=0), jnp.concatenate(rights, axis=0))
-        return term.astype(BF)
-
-    down_term = weight_term(gathered_two, hiddens)
-    ff_bands = [
-        reduce_rows(weight_term(gathered_in, low_gates), nf),
-        reduce_rows(weight_term(gathered_in, low_ups), nf),
-        lax.psum_scatter(down_term, "fsdp", scatter_dimension=0, tiled=True),
-    ]
-
-    def gather_relative(bands):
-        parts = [gather_parts(part, nd) for part in bands]
-        out = jnp.zeros((nd, len(bands)) + bands[0].shape, BF)
-        for kind, pieces in enumerate(parts):
-            for place, piece in enumerate(pieces):
-                out = lax.dynamic_update_slice(
-                    out, piece[None, None], (place, kind) + (0,) * piece.ndim
-                )
-        return out
-
-    ff_all = gather_relative(ff_bands)
+    gate_term = weight_term(gathered_in, low_gates, (last,))
+    up_term = weight_term(gathered_in, low_ups, (gate_term,))
+    both_band = sum_rows(jnp.concatenate([gate_term, up_term], axis=1))
 
     low_one = jnp.concatenate(low_ones, axis=0)
     attended = jnp.concatenate(all_attended, axis=0)
-    low_mixed = dot_nn(low_one, w_out).astype(BF).reshape(micros, rows, HEADS, HD)
+    left_mine = [from_x(root_left[0, :, :, :BC], low_one)]
+    if band > BC:
+        left_mine.append(from_x(root_left[0, :, :, BC:].transpose(0, 2, 1), left_mine[0][-1]))
+    low_mixed = dot_nn(after(low_one, up_term), w_out).astype(BF).reshape(micros, rows, HEADS, HD)
     grad_queries, key_terms = [], []
     for m in range(micros):
         for_queries, for_keys, for_values = attend_back(
@@ -572,7 +582,9 @@
         grad_queries.append(for_queries)
         terms = jnp.concatenate([for_keys, for_values], axis=1)
         key_terms.append(return_key_grads(terms, rows, nf))
+        last = terms
     own_terms = jnp.concatenate(key_terms, axis=0)
+    out_term = dot_tn(after(low_one, last), attended)
     grad_keys, grad_values = (own_terms[:, :HD], own_terms[:, HD:])
 
     def heads_only(query_in, key_in, query_scale, key_scale):
@@ -591,20 +603,32 @@
 
     attn_per = -(-ATTN_BLOCKS // nd)
     attn_width = attn_per * BC
-    attn_term = jnp.concatenate([dot_tn(normed, low_projected), dot_tn(low_one, attended)], axis=1)
+    attn_term = jnp.concatenate([dot_tn(normed, low_projected), out_term], axis=1)
     attn_term = jnp.pad(attn_term, ((0, 0), (0, nd * attn_width - ATTN_BLOCKS * BC)))
 
     def owner_columns(index):
         return lax.dynamic_slice(attn_term, (0, index * attn_width), (D, attn_width))
 
+    attn_term = after(attn_term, *left_mine[-1])
     owners_at = part_owners(nd)
     attn_sum = scatter_sum_dp(
         jnp.concatenate([owner_columns(e) for e in owners_at[: nd // 2]], axis=0),
         jnp.concatenate([owner_columns(e) for e in owners_at[nd // 2 :]], axis=0),
         nd,
     )
-    attn_band = direct_reduce(attn_sum.astype(BF), nf)
+    ff_all = gather_columns([both_band, down_band])
+    attn_band = direct_reduce(after(attn_sum, both_band).astype(BF), nf)
     attn_all = gather_relative([attn_band])
+
+    def all_parts(mine):
+        parts = [after(piece, attn_sum) for piece in mine + [swap_core(piece, nd) for piece in mine]]
+        out = jnp.zeros((nd,) + parts[0].shape, BF)
+        for place, piece in enumerate(parts):
+            out = lax.dynamic_update_slice(out, piece[None], (place,) + (0,) * piece.ndim)
+        return out.reshape((nd * capacity,) + out.shape[2:])
+
+    left_roots = [all_parts(mine) for mine in left_mine]
+    right_roots = all_parts(right_mine)
 
     def relative(index):
         nx = nd // 2
@@ -614,12 +638,13 @@
     ff_index = np.arange(3 * FF_BLOCKS)
     ff_dp = np.minimum(ff_index % FF_BLOCKS // per, nd - 1)
     ff_column = ff_index % FF_BLOCKS - np.minimum(ff_dp * per, FF_BLOCKS - per)
+    ff_column = ff_column + ff_index // FF_BLOCKS * per
     attn_index = np.arange(ATTN_BLOCKS)
     part_of = relative(
         jnp.asarray(np.concatenate([attn_index // attn_per, ff_dp]).astype(np.int32))
     )
     kind_of = jnp.asarray(
-        np.concatenate([np.zeros(ATTN_BLOCKS), ff_index // FF_BLOCKS]).astype(np.int32)
+        np.zeros(NBLK).astype(np.int32)
     )
     column_of = jnp.asarray(np.concatenate([attn_index % attn_per, ff_column]).astype(np.int32))
 
@@ -634,17 +659,12 @@
     def of_slot(values):
         return jnp.sum(jnp.where(mine, values[None, :], 0), axis=1)
 
-    root_of = relative(owners) * capacity + ranks
-    every_left = gather_relative([after(root_left[0], w_qkv)])
-    every_left = every_left.reshape((nd * capacity,) + root_left.shape[2:])
-    every_right = gather_relative([after(root_right[0], w_qkv)])
-    every_right = every_right.reshape((nd * capacity,) + root_right.shape[2:])
-
     is_attn = (index < ATTN_BLOCKS).astype(jnp.int32)
     places = (part_of, kind_of, column_of, is_attn)
     early = tuple(table[LATE:] for table in places)
     late = tuple(table[:LATE] for table in places)
-    root_args = (every_left, every_right, master)
+    root_of = relative(owners) * capacity + ranks
+    root_args = (left_roots, right_roots, master)
     fresh_arrays = update_blocks(
         [ff_all], early, root_of[LATE:], *root_args, LATE, NBLK - LATE, 7, None
     )
@@ -664,7 +684,7 @@
     gain_sum = jnp.concatenate(
         [grad_pre_attn, post_attn_sum, pre_ffw_sum, post_ffw_sum, grad_query_gain, grad_key_gain]
     )
-    gain_grad = sum_everywhere(gain_sum, nd, nf)
+    gain_grad = sum_everywhere(after(gain_sum, attn_band), nd, nf)
     new_gain_stats = DECAY * gain_stats + (1.0 - DECAY) * gain_grad * gain_grad
     gain_change = -GAIN_RATE * gain_grad * lax.rsqrt(new_gain_stats)
     return (

time: 933 us -> 806 us (0.86)
  starting transfers between devices: 219 us -> 104 us
  other arithmetic: 64.4 us -> 82.7 us
  matrix products: 197 us -> 180 us
  waiting for transfers between devices: 261 us -> 246 us
    ppermute x28 -> x14, starting transfers between devices: 101 us -> 37.9 us  [swap_fsdp(): return lax.ppermute(value, 'fsdp', [(e, e ^ flip) for e in range(nf)])]
    dynamic_update_slice x23 -> x4, local copies, waits for them, and re-layouts: 52.4 us -> 0.13 us  [gather_relative(): lax.dynamic_update_slice(out, piece[None, None], (place, kind) + (0,) * p...]
    dynamic_update_slice x8 -> x24, local copies, waits for them, and re-layouts: 2.3 us -> 46.7 us  [the longest x12 29.6 us: all_parts(): lax.dynamic_update_slice(out, piece[None], (place,) + (0,) * piece.ndim)]
    ppermute x5, waiting for transfers between devices: 40 us -> 2.45 us  [sum_everywhere(): lax.ppermute(value, axis, [(e, e ^ step) for e in range(count)])]
    ppermute x2, waiting for transfers between devices: 0.01 us -> 36.9 us  [return_key_grads(): lax.ppermute(first.astype(BF), 'fsdp', backwards(TO_SECOND)).astype(F32)]
    ppermute x7 -> x0, starting transfers between devices: 29.5 us -> none  [direct_reduce(): lax.ppermute(sent, 'fsdp', [(e, e ^ flip) for e in range(nf)]).astype(F32)]
    ppermute x29 -> x27, starting transfers between devices: 27.7 us -> 3.74 us  [swap_core(): return lax.ppermute(value, 'dp', [(e, e ^ 1) for e in range(nd)])]
    concatenate x1 -> x7, other arithmetic: 1.51 us -> 20.3 us  [the longest x1 9.85 us: local(): jnp.concatenate([dot_tn(normed, low_projected), out_term], axis=1)]
  transfers between devices with their start and end apart: 108 -> 84, of which waited for: 31 -> 31; matrix products, arithmetic and copies ran while one was open for 34% -> 42% of each run, Pallas kernels for 0% -> 5%
where the time goes in v3:
time: 806 us; the launch traced here: 796 us
  waiting for transfers between devices  246 us (31%)
  matrix products  180 us (22%)
  local copies, waits for them, and re-layouts  105 us (13%)
  starting transfers between devices  104 us (13%)
  other arithmetic  82.7 us (10%)
  Pallas kernels  58.1 us (7%)
  between operations  19.8 us (2%)
    ppermute x15, waiting for transfers between devices, shift_x(): return lax.ppermute(value, 'dp', pairs)  138 us
    dot_general x8, matrix products, dot_nn(): return jnp.dot(left, right, preferred_element_type=F32)  64.5 us
    dot_general x9, matrix products, dot_nt(): lax.dot_general(left, right, (((1,), (1,)), ((), ())), preferred_element_...  55.3 us
    dot_general x5, matrix products, dot_tn(): lax.dot_general(left, right, (((0,), (0,)), ((), ())), preferred_element_...  48 us
    ppermute x14, waiting for transfers between devices, swap_fsdp(): return lax.ppermute(value, 'fsdp', [(e, e ^ flip) for e in range(nf)])  42.9 us
    ppermute x14, starting transfers between devices, swap_fsdp(): return lax.ppermute(value, 'fsdp', [(e, e ^ flip) for e in range(nf)])  37.9 us
    pallas_call x2, Pallas kernels, update_blocks(): pl.pallas_call(lambda *refs: update_body(group, len(sources), len(left_ro...  37.3 us
    ppermute x2, waiting for transfers between devices, return_key_grads(): lax.ppermute(first.astype(BF), 'fsdp', backwards(TO_SECOND)).astype(F32)  36.9 us
  transfers between devices with their start and end apart: 84, of which 31 were waited for; matrix products, arithmetic and copies ran while one was open for 42% of the time, Pallas kernels for 5%

profile of v3, /device:TPU:0, one launch (start us, length us, event | category | flops | bytes accessed | tf_op | source)
XLA Modules:
  0.0 796.0 jit_solution(214588512959749710)
XLA Ops:
  90.5 12.6 %collective-permute-start.26 = (bf16[256,512]{1,0:T(8,128)(2,1)S(1)}, bf16[256,512]{1,0:T(8,128)(2,1)S(1)}, u32[]{:S(2)}, u32[]{:S(2)}) collective-permute-start(bf16[256,512]{1,0:T(8,128)(2,1)S(1)} %get-tuple-element.241), channel_id=1, source_target_pairs={{0,1},{1,2},{2,3},{8,9},{9,10},{10,11},{16,17},{17,18},{18,19},{24... | collective-permute-start | bytes 786440 | tf_op jit(solution)/shard_map/ppermute | solution.py:356
  104.1 18.0 %collective-permute-start.18 = (bf16[144,512]{1,0:T(8,128)(2,1)S(1)}, bf16[144,512]{1,0:T(8,128)(2,1)S(1)}, u32[]{:S(2)}, u32[]{:S(2)}) collective-permute-start(bf16[144,512]{1,0:T(8,128)(2,1)S(1)} %dynamic-slice_convert_fusion.6), channel_id=1, source_target_pairs={{0,6},{1,7},{2,4},{3,5},{4,2},{5,3},{6,0},{7,1},{8,14},{9,15},{10,... | collective-permute-start | bytes 442376 | tf_op jit(solution)/shard_map/ppermute | solution.py:164
  131.8 14.8 %collective-permute-done.16 = bf16[144,512]{1,0:T(8,128)(2,1)S(1)} collective-permute-done((bf16[144,512]{1,0:T(8,128)(2,1)S(1)}, bf16[144,512]{1,0:T(8,128)(2,1)S(1)}, u32[]{:S(2)}, u32[]{:S(2)}) %collective-permute-start.16) | collective-permute-done | bytes 147488 | tf_op jit(solution)/shard_map/ppermute | solution.py:164
  172.3 14.0 %collective-permute-done.21 = bf16[256,1152]{1,0:T(8,128)(2,1)S(1)} collective-permute-done((bf16[256,1152]{1,0:T(8,128)(2,1)}, bf16[256,1152]{1,0:T(8,128)(2,1)S(1)}, u32[]{:S(2)}, u32[]{:S(2)}) %collective-permute-start.21) | collective-permute-done | bytes 589856 | tf_op jit(solution)/shard_map/ppermute | solution.py:115
  192.4 14.1 %collective-permute-done.29 = bf16[256,1152]{1,0:T(8,128)(2,1)S(1)} collective-permute-done((bf16[256,1152]{1,0:T(8,128)(2,1)S(1)}, bf16[256,1152]{1,0:T(8,128)(2,1)S(1)}, u32[]{:S(2)}, u32[]{:S(2)}) %collective-permute-start.29) | collective-permute-done | bytes 589856 | tf_op jit(solution)/shard_map/ppermute | solution.py:115
  218.6 11.6 %multiply_convert_fusion.3 = (bf16[1024,1792]{1,0:T(8,128)(2,1)}, f32[1024,1792]{1,0:T(8,128)}) fusion(f32[1024,1792]{1,0:T(8,128)S(1)} %fusion.37, bf16[1152,3584]{1,0:T(8,128)(2,1)S(1)} %copy-done.137, bf16[256,1152]{1,0:T(8,128)(2,1)S(1)} %copy-done.75, bf16[256,1152]{1,0:T(8,128)(2,1)S(1)} %collective-permute-done.22, ...), kind=kOutput, calls=%fused_computation.37 | convolution fusion | flops 4255645696 | bytes 24838144 | tf_op jit(solution)/shard_map/dot_general | solution.py:97
  285.3 12.0 %collective-permute-done.33 = bf16[256,1152]{1,0:T(8,128)(2,1)S(1)} collective-permute-done((bf16[256,1152]{1,0:T(8,128)(2,1)S(1)}, bf16[256,1152]{1,0:T(8,128)(2,1)S(1)}, u32[]{:S(2)}, u32[]{:S(2)}) %collective-permute-start.33) | collective-permute-done | bytes 589856 | tf_op jit(solution)/shard_map/ppermute | solution.py:115
  304.7 10.9 %collective-permute-done.36 = bf16[256,1152]{1,0:T(8,128)(2,1)S(1)} collective-permute-done((bf16[256,1152]{1,0:T(8,128)(2,1)S(1)}, bf16[256,1152]{1,0:T(8,128)(2,1)S(1)}, u32[]{:S(2)}, u32[]{:S(2)}) %collective-permute-start.36) | collective-permute-done | bytes 589856 | tf_op jit(solution)/shard_map/ppermute | solution.py:115
  319.8 14.6 %fusion.8 = (bf16[1024,1792]{1,0:T(8,128)(2,1)}, bf16[1024,1792]{1,0:T(8,128)(2,1)}) fusion(f32[1024,1792]{1,0:T(8,128)} %copy-done.141, f32[1024,1792]{1,0:T(8,128)} %get-tuple-element.267, bf16[1024,1152]{1,0:T(8,128)(2,1)S(1)} %pad_maximum_fusion.6, bf16[1152,1792]{1,0:T(8,128)(2,1)} %all-gather.5.cloned.1.call-done), kind=kOutput, calls=%fused_computation.17 | convolution fusion | flops 4271898624 | bytes 28508160 | tf_op jit(solution)/shard_map/dot_general | solution.py:97
  335.0 9.2 %fusion.26 = f32[1024,1152]{1,0:T(8,128)} fusion(bf16[1024,1792]{1,0:T(8,128)(2,1)} %get-tuple-element.211, bf16[1152,3584]{1,0:T(8,128)(2,1)S(1)} %bitcast.302), kind=kOutput, calls=%fused_computation.59 | convolution fusion | flops 4227858432 | bytes 12517376 | tf_op jit(solution)/shard_map/dot_general | solution.py:101
  346.4 13.4 %multiply_convert_fusion = (bf16[1024,1792]{1,0:T(8,128)(2,1)}, bf16[1024,1792]{1,0:T(8,128)(2,1)}) fusion(f32[1024,1792]{1,0:T(8,128)} %copy-done.140, f32[1024,1792]{1,0:T(8,128)} %get-tuple-element.269, bf16[1024,1152]{1,0:T(8,128)(2,1)S(1)} %pad_maximum_fusion.7, bf16[1152,1792]{1,0:T(8,128)(2,1)S(1)} %copy-done.139), kind=kOutput, calls=%fused_computation.34 | convolution fusion | flops 4271898624 | bytes 28508160 | tf_op jit(solution)/shard_map/dot_general | solution.py:97
  359.9 12.6 %convolution_convert_fusion.2 = bf16[1152,1792]{1,0:T(8,128)(2,1)} fusion(bf16[2048,1152]{1,0:T(8,128)(2,1)S(1)} %constant_dynamic-update-slice_fusion, bf16[1024,1792]{1,0:T(8,128)(2,1)S(1)} %copy-done.143, bf16[1024,1792]{1,0:T(8,128)(2,1)} %get-tuple-element.59), kind=kOutput, calls=%fused_computation.10 | convolution fusion | flops 8472461312 | bytes 16187392 | tf_op jit(solution)/shard_map/dot_general | solution.py:105
  372.8 14.8 %collective-permute-done.42 = bf16[57,128,128]{2,1,0:T(8,128)(2,1)} collective-permute-done((bf16[57,128,128]{2,1,0:T(8,128)(2,1)}, bf16[57,128,128]{2,1,0:T(8,128)(2,1)}, u32[]{:S(2)}, u32[]{:S(2)}) %collective-permute-start.42) | collective-permute-done | bytes 1867808 | tf_op jit(solution)/shard_map/ppermute | solution.py:115
  387.5 9.9 %convolution_add_fusion.1 = f32[1024,1152]{1,0:T(8,128)S(1)} fusion(f32[1024,1152]{1,0:T(8,128)} %fusion.26, bf16[1024,1792]{1,0:T(8,128)(2,1)} %get-tuple-element.65, bf16[1152,3584]{1,0:T(8,128)(2,1)} %all-gather.3.cloned.1.call-done), kind=kOutput, calls=%fused_computation.42 | convolution fusion | flops 4229038080 | bytes 17235968 | tf_op jit(solution)/shard_map/dot_general | solution.py:101
  413.5 14.3 %convolution_convert_fusion.1 = bf16[1152,1792]{1,0:T(8,128)(2,1)} fusion(bf16[2048,1152]{1,0:T(8,128)(2,1)S(1)} %bitcast.295, bf16[1024,1792]{1,0:T(8,128)(2,1)} %get-tuple-element.66, bf16[1024,1792]{1,0:T(8,128)(2,1)} %get-tuple-element.65), kind=kOutput, calls=%fused_computation.9 | convolution fusion | flops 8472461312 | bytes 16187392 | tf_op jit(solution)/shard_map/dot_general | solution.py:105
  428.3 12.4 %convolution_convert_fusion = bf16[1152,1792]{1,0:T(8,128)(2,1)} fusion(bf16[2048,1152]{1,0:T(8,128)(2,1)S(1)} %bitcast.295, bf16[1024,1792]{1,0:T(8,128)(2,1)S(1)} %copy-done.144, bf16[1024,1792]{1,0:T(8,128)(2,1)} %get-tuple-element.211), kind=kOutput, calls=%fused_computation.8 | convolution fusion | flops 8472461312 | bytes 16187392 | tf_op jit(solution)/shard_map/dot_general | solution.py:105
  458.4 11.7 %collective-permute-done.44 = bf16[256,1152]{1,0:T(8,128)(2,1)} collective-permute-done((bf16[256,1152]{1,0:T(8,128)(2,1)}, bf16[256,1152]{1,0:T(8,128)(2,1)}, u32[]{:S(2)}, u32[]{:S(2)}) %collective-permute-start.44) | collective-permute-done | bytes 589856 | tf_op jit(solution)/shard_map/ppermute | solution.py:115
  523.7 29.8 %collective-permute-done.50 = bf16[256,512]{1,0:T(8,128)(2,1)} collective-permute-done((bf16[256,512]{1,0:T(8,128)(2,1)}, bf16[256,512]{1,0:T(8,128)(2,1)}, u32[]{:S(2)}, u32[]{:S(2)}) %collective-permute-start.50) | collective-permute-done | bytes 262176 | tf_op jit(solution)/shard_map/ppermute | solution.py:373
  573.8 9.9 %pad_maximum_fusion = f32[1152,2560]{1,0:T(8,128)} fusion(f32[1152,1024]{1,0:T(8,128)} %fusion.70, f32[1152,1536]{1,0:T(8,128)} %fusion.80), kind=kLoop, calls=%fused_computation.2 | loop fusion | flops 2949120 | bytes 23592960 | tf_op jit(solution)/shard_map/concatenate | solution.py:606
  607.5 30.7 %collective-permute-done.64 = bf16[1152,640]{1,0:T(8,128)(2,1)S(1)} collective-permute-done((bf16[1152,640]{1,0:T(8,128)(2,1)S(1)}, bf16[1152,640]{1,0:T(8,128)(2,1)S(1)}, u32[]{:S(2)}, u32[]{:S(2)}) %collective-permute-start.64) | collective-permute-done | bytes 1474592 | tf_op jit(solution)/shard_map/ppermute | solution.py:115
  679.2 10.9 %collective-permute-done.55 = bf16[144,3584]{1,0:T(8,128)(2,1)} collective-permute-done((bf16[144,3584]{1,0:T(8,128)(2,1)}, bf16[144,3584]{1,0:T(8,128)(2,1)}, u32[]{:S(2)}, u32[]{:S(2)}) %collective-permute-start.55) | collective-permute-done | bytes 1032224 | tf_op jit(solution)/shard_map/ppermute | solution.py:115
  693.5 12.6 %all-to-all-done = bf16[8,144,640]{2,1,0:T(8,128)(2,1)S(1)} async-done(((bf16[8,144,640]{2,1,0:T(8,128)(2,1)}), bf16[8,144,640]{2,1,0:T(8,128)(2,1)S(1)}, u32[]{:S(2)}, u32[]{:S(2)}) %all-to-all-start) | async-done | bytes 1474592 | tf_op jit(solution)/shard_map/all_to_all | solution.py:184
  723.8 12.7 %owner_stats.2 = (f32[57,144,128]{2,1,0:T(8,128)}, f32[57,144,144]{2,1,0:T(8,128)}, f32[57,128,128]{2,1,0:T(8,128)}) custom-call(s32[57]{0:T(128)S(1)} %get-tuple-element.183.refs_0_, s32[57]{0:T(128)S(1)} %broadcast.987.refs_1_, s32[57]{0:T(128)S(1)} %get-tuple-element.182.refs_2_, s32[57]{0:T(128)S(1)} %get-tuple-element.181.refs_3_, ...), custom_call_target="tpu_custom_call" | custom-call | tf_op jit(solution)/shard_map/owner_stats/pallas_call | solution.py:306
  736.5 30.5 %update_blocks.2 = (f32[144,23296]{1,0:T(8,128)}, bf16[144,23296]{1,0:T(8,128)(2,1)}) custom-call(s32[161]{0:T(256)S(1)} %slice.297.refs_0_, s32[161]{0:T(256)S(1)} %broadcast.985.refs_1_, s32[161]{0:T(256)S(1)} %copy-done.1, s32[161]{0:T(256)S(1)} %slice.300.refs_3_, s32[161]{0:T(256)S(1)} %slice.301.refs_4_, ...), custom_call_target="tpu_custom_call" | custom-call | tf_op jit(solution)/shard_map/update_blocks/pallas_call | solution.py:260
  (704 shorter events, 418.4 us)
Async XLA Ops:
  7.2 203.8 %all-gather.3.cloned.1.call-start = ((), (), s32[]{:S(2)}) async-start(), calls=%async_computation.3 | async-start | bytes 9289728 | tf_op jit(solution)/shard_map/all_gather | solution.py:468
  20.5 224.2 %all-gather.5.cloned.1.call-start = ((), (), s32[]{:S(2)}) async-start(), calls=%async_computation.4 | async-start | bytes 4644864 | tf_op jit(solution)/shard_map/all_gather | solution.py:470
  65.8 57.3 %collective-permute-start.10 = (bf16[256,512]{1,0:T(8,128)(2,1)S(1)}, bf16[256,512]{1,0:T(8,128)(2,1)}, u32[]{:S(2)}, u32[]{:S(2)}) collective-permute-start(bf16[256,512]{1,0:T(8,128)(2,1)S(1)} %get-tuple-element.240), channel_id=1, source_target_pairs={{0,1},{1,2},{2,3},{8,9},{9,10},{10,11},{16,17},{17,18},{18,19},{24... | collective-permute-start | bytes 786440 | tf_op jit(solution)/shard_map/ppermute | solution.py:356
  81.3 41.9 %collective-permute-start.11 = (bf16[256,512]{1,0:T(8,128)(2,1)}, bf16[256,512]{1,0:T(8,128)(2,1)S(1)}, u32[]{:S(2)}, u32[]{:S(2)}) collective-permute-start(bf16[256,512]{1,0:T(8,128)(2,1)} %collective-permute-done.8), channel_id=1, source_target_pairs={{4,5},{5,4},{12,13},{13,12},{20,21},{21,20},{28,29},{29,28}} | collective-permute-start | bytes 786440 | tf_op jit(solution)/shard_map/ppermute | solution.py:358
  88.7 35.2 %collective-permute-start.12 = (bf16[256,512]{1,0:T(8,128)(2,1)S(1)}, bf16[256,512]{1,0:T(8,128)(2,1)S(1)}, u32[]{:S(2)}, u32[]{:S(2)}) collective-permute-start(bf16[256,512]{1,0:T(8,128)(2,1)S(1)} %collective-permute-done.9), channel_id=1, source_target_pairs={{6,7},{7,6},{14,15},{15,14},{22,23},{23,22},{30,31},{31,30}} | collective-permute-start | bytes 786440 | tf_op jit(solution)/shard_map/ppermute | solution.py:359
  90.5 62.4 %collective-permute-start.26 = (bf16[256,512]{1,0:T(8,128)(2,1)S(1)}, bf16[256,512]{1,0:T(8,128)(2,1)S(1)}, u32[]{:S(2)}, u32[]{:S(2)}) collective-permute-start(bf16[256,512]{1,0:T(8,128)(2,1)S(1)} %get-tuple-element.241), channel_id=1, source_target_pairs={{0,1},{1,2},{2,3},{8,9},{9,10},{10,11},{16,17},{17,18},{18,19},{24... | collective-permute-start | bytes 786440 | tf_op jit(solution)/shard_map/ppermute | solution.py:356
  172.1 468.1 %reduce-scatter.5.cloned.1.call-start = ((), (), s32[]{:S(2)}) async-start(), calls=%async_computation.6 | async-start | bytes 4644864 | tf_op jit(solution)/shard_map/reduce_scatter | solution.py:551
  344.5 43.0 %collective-permute-start.42 = (bf16[57,128,128]{2,1,0:T(8,128)(2,1)}, bf16[57,128,128]{2,1,0:T(8,128)(2,1)}, u32[]{:S(2)}, u32[]{:S(2)}) collective-permute-start(bf16[57,128,128]{2,1,0:T(8,128)(2,1)} %bitcast.20), channel_id=1, source_target_pairs={{0,16},{8,24},{16,0},{24,8},{1,17},{9,25},{17,1},{25,9},{2,18},{10... | collective-permute-start | bytes 5603336 | tf_op jit(solution)/shard_map/ppermute | solution.py:115
  372.5 292.7 %reduce-scatter.3.cloned.1.call-start = ((), (), s32[]{:S(2)}) async-start(), calls=%async_computation.5 | async-start | bytes 9289728 | tf_op jit(solution)/shard_map/reduce_scatter | solution.py:551
  504.3 50.3 %collective-permute-start.51 = (bf16[256,512]{1,0:T(8,128)(2,1)}, bf16[256,512]{1,0:T(8,128)(2,1)}, u32[]{:S(2)}, u32[]{:S(2)}) collective-permute-start(bf16[256,512]{1,0:T(8,128)(2,1)} %fusion.95), channel_id=1, source_target_pairs={{1,0},{2,1},{3,2},{9,8},{10,9},{11,10},{17,16},{18,17},{19,18},{25... | collective-permute-start | bytes 786440 | tf_op jit(solution)/shard_map/ppermute | solution.py:370
  515.4 56.9 %collective-permute-start.61 = (bf16[57,144,128]{2,1,0:T(8,128)(2,1)}, bf16[57,144,128]{2,1,0:T(8,128)(2,1)}, u32[]{:S(2)}, u32[]{:S(2)}) collective-permute-start(bf16[57,144,128]{2,1,0:T(8,128)(2,1)} %slice_bitcast_fusion), channel_id=1, source_target_pairs={{0,16},{8,24},{16,0},{24,8},{1,17},{9,25},{17,1},{25,9},{2,18},{10... | collective-permute-start | bytes 6303752 | tf_op jit(solution)/shard_map/ppermute | solution.py:115
  516.3 37.2 %collective-permute-start.50 = (bf16[256,512]{1,0:T(8,128)(2,1)}, bf16[256,512]{1,0:T(8,128)(2,1)}, u32[]{:S(2)}, u32[]{:S(2)}) collective-permute-start(bf16[256,512]{1,0:T(8,128)(2,1)} %add_convert_fusion.4), channel_id=1, source_target_pairs={{2,0},{3,1},{4,2},{5,3},{10,8},{11,9},{12,10},{13,11},{18,16},{19,... | collective-permute-start | bytes 786440 | tf_op jit(solution)/shard_map/ppermute | solution.py:373
  518.4 43.3 %collective-permute-start.54 = (bf16[256,512]{1,0:T(8,128)(2,1)}, bf16[256,512]{1,0:T(8,128)(2,1)}, u32[]{:S(2)}, u32[]{:S(2)}) collective-permute-start(bf16[256,512]{1,0:T(8,128)(2,1)} %add_convert_fusion.3), channel_id=1, source_target_pairs={{2,0},{3,1},{4,2},{5,3},{10,8},{11,9},{12,10},{13,11},{18,16},{19,... | collective-permute-start | bytes 786440 | tf_op jit(solution)/shard_map/ppermute | solution.py:373
  591.7 48.4 %collective-permute-start.77 = (bf16[57,128,128]{2,1,0:T(8,128)(2,1)}, bf16[57,128,128]{2,1,0:T(8,128)(2,1)}, u32[]{:S(2)}, u32[]{:S(2)}) collective-permute-start(bf16[57,128,128]{2,1,0:T(8,128)(2,1)} %bitcast.20), channel_id=1, source_target_pairs={{0,8},{8,0},{16,24},{24,16},{1,9},{9,1},{17,25},{25,17},{2,10},{10... | collective-permute-start | bytes 5603336 | tf_op jit(solution)/shard_map/ppermute | solution.py:109
  592.3 47.4 %collective-permute-start.78 = (bf16[57,128,128]{2,1,0:T(8,128)(2,1)}, bf16[57,128,128]{2,1,0:T(8,128)(2,1)}, u32[]{:S(2)}, u32[]{:S(2)}) collective-permute-start(bf16[57,128,128]{2,1,0:T(8,128)(2,1)} %collective-permute-done.42), channel_id=1, source_target_pairs={{0,8},{8,0},{16,24},{24,16},{1,9},{9,1},{17,25},{25,17},{2,10},{10... | collective-permute-start | bytes 5603336 | tf_op jit(solution)/shard_map/ppermute | solution.py:109
  592.3 56.2 %collective-permute-start.73 = (bf16[57,144,128]{2,1,0:T(8,128)(2,1)}, bf16[57,144,128]{2,1,0:T(8,128)(2,1)S(1)}, u32[]{:S(2)}, u32[]{:S(2)}) collective-permute-start(bf16[57,144,128]{2,1,0:T(8,128)(2,1)} %slice_bitcast_fusion), channel_id=1, source_target_pairs={{0,8},{8,0},{16,24},{24,16},{1,9},{9,1},{17,25},{25,17},{2,10},{10... | collective-permute-start | bytes 6303752 | tf_op jit(solution)/shard_map/ppermute | solution.py:109
  603.9 34.3 %collective-permute-start.64 = (bf16[1152,640]{1,0:T(8,128)(2,1)S(1)}, bf16[1152,640]{1,0:T(8,128)(2,1)S(1)}, u32[]{:S(2)}, u32[]{:S(2)}) collective-permute-start(bf16[1152,640]{1,0:T(8,128)(2,1)S(1)} %slice.522), channel_id=1, source_target_pairs={{0,16},{8,24},{16,0},{24,8},{1,17},{9,25},{17,1},{25,9},{2,18},{10... | collective-permute-start | bytes 4423688 | tf_op jit(solution)/shard_map/ppermute | solution.py:115
  607.5 59.1 %collective-permute-start.75 = (bf16[57,16,144]{2,1,0:T(8,128)(2,1)}, bf16[57,16,144]{2,1,0:T(8,128)(2,1)}, u32[]{:S(2)}, u32[]{:S(2)}) collective-permute-start(bf16[57,16,144]{2,1,0:T(8,128)(2,1)} %bitcast.41), channel_id=1, source_target_pairs={{0,8},{8,0},{16,24},{24,16},{1,9},{9,1},{17,25},{25,17},{2,10},{10... | collective-permute-start | bytes 787976 | tf_op jit(solution)/shard_map/ppermute | solution.py:109
  638.2 33.7 %collective-permute-start.74 = (bf16[57,144,128]{2,1,0:T(8,128)(2,1)}, bf16[57,144,128]{2,1,0:T(8,128)(2,1)}, u32[]{:S(2)}, u32[]{:S(2)}) collective-permute-start(bf16[57,144,128]{2,1,0:T(8,128)(2,1)} %collective-permute-done.61), channel_id=1, source_target_pairs={{0,8},{8,0},{16,24},{24,16},{1,9},{9,1},{17,25},{25,17},{2,10},{10... | collective-permute-start | bytes 6303752 | tf_op jit(solution)/shard_map/ppermute | solution.py:109
  639.7 32.3 %collective-permute-start.76 = (bf16[57,16,144]{2,1,0:T(8,128)(2,1)}, bf16[57,16,144]{2,1,0:T(8,128)(2,1)}, u32[]{:S(2)}, u32[]{:S(2)}) collective-permute-start(bf16[57,16,144]{2,1,0:T(8,128)(2,1)} %collective-permute-done.62), channel_id=1, source_target_pairs={{0,8},{8,0},{16,24},{24,16},{1,9},{9,1},{17,25},{25,17},{2,10},{10... | collective-permute-start | bytes 787976 | tf_op jit(solution)/shard_map/ppermute | solution.py:109
  666.6 50.5 %collective-permute-start.59 = (bf16[144,1792]{1,0:T(8,128)(2,1)}, bf16[144,1792]{1,0:T(8,128)(2,1)}, u32[]{:S(2)}, u32[]{:S(2)}) collective-permute-start(bf16[144,1792]{1,0:T(8,128)(2,1)} %reduce-scatter.5.cloned.1.call-done), channel_id=1, source_target_pairs={{0,8},{8,0},{16,24},{24,16},{1,9},{9,1},{17,25},{25,17},{2,10},{10... | collective-permute-start | bytes 1548296 | tf_op jit(solution)/shard_map/ppermute | solution.py:109
  666.7 55.2 %collective-permute-start.60 = (bf16[144,1792]{1,0:T(8,128)(2,1)}, bf16[144,1792]{1,0:T(8,128)(2,1)}, u32[]{:S(2)}, u32[]{:S(2)}) collective-permute-start(bf16[144,1792]{1,0:T(8,128)(2,1)} %collective-permute-done.58), channel_id=1, source_target_pairs={{0,8},{8,0},{16,24},{24,16},{1,9},{9,1},{17,25},{25,17},{2,10},{10... | collective-permute-start | bytes 1548296 | tf_op jit(solution)/shard_map/ppermute | solution.py:109
  667.2 38.9 %all-to-all-start = ((bf16[8,144,640]{2,1,0:T(8,128)(2,1)}), bf16[8,144,640]{2,1,0:T(8,128)(2,1)S(1)}, u32[]{:S(2)}, u32[]{:S(2)}) async-start(bf16[8,144,640]{2,1,0:T(8,128)(2,1)} %bitcast.43), calls=%async_computation.2 | async-start | bytes 2949120 | tf_op jit(solution)/shard_map/all_to_all | solution.py:184
  720.9 47.2 %collective-permute-start.72 = (f32[5120]{0:T(1024)S(1)}, f32[5120]{0:T(1024)S(1)}, u32[]{:S(2)}, u32[]{:S(2)}) collective-permute-start(f32[5120]{0:T(1024)S(1)} %add.704), channel_id=1, source_target_pairs={{0,4},{1,5},{2,6},{3,7},{4,0},{5,1},{6,2},{7,3},{8,12},{9,13},{10,... | collective-permute-start | bytes 61448 | tf_op jit(solution)/shard_map/ppermute | solution.py:154
  (210 other events, 2417.8 us)
Sparse Core Ops, SparseCore 0:
  20.6 139.6 all-gather.2
  172.2 72.3 all-gather.4
  372.6 86.5 reduce-scatter.4
  463.8 161.8 reduce-scatter.2

commit v4 on v3

--- a/solution.py
+++ b/solution.py
@@ -219,6 +219,33 @@
         fresh = master_ref[:, at] + shaped[j] * factors[j]
         new_ref[:, at] = fresh
         low_ref[:, at] = fresh.astype(BF)
+
+
+def pack_roots(roots):
+    slots, rows = roots.shape[:2]
+    group = 3 if slots % 3 == 0 else 1
+    rest = rows - BC
+
+    def body(root_ref, first_ref, rest_ref):
+        for j in range(group):
+            first_ref[j] = root_ref[j, :, :BC]
+            rest_ref[j] = root_ref[j, :, BC:].astype(F32).T.astype(BF)
+
+    def slab(shape):
+        return pl.BlockSpec((group,) + shape, lambda i: (i, 0, 0))
+
+    return pl.pallas_call(
+        body,
+        grid=(slots // group,),
+        in_specs=[slab((rows, rows))],
+        out_specs=[slab((rows, BC)), slab((rest, rows))],
+        out_shape=[
+            jax.ShapeDtypeStruct((slots, rows, BC), BF),
+            jax.ShapeDtypeStruct((slots, rest, rows), BF),
+        ],
+        compiler_params=pltpu.CompilerParams(vmem_limit_bytes=VMEM_LIMIT),
+        name="pack_roots",
+    )(roots)
 
 
 def grad_specs(sources, group, skip, band):
@@ -515,19 +542,30 @@
         hiddens.append(hidden)
         saved[m] += [gate, up]
     for m in range(micros):
-        hidden = after(hiddens[m], partials[-1] if m else hiddens[-1])
-        partials.append(dot_nt(hidden, w_down))
-    last = partials[-1]
+        hidden = after(hiddens[m], *(partials[-1] if m else hiddens[-1:]))
+        away = dot_nt(hidden[half:], w_down).astype(BF)
+        partials.append((away, dot_nt(after(hidden[:half], away), w_down)))
+    last = partials[-1][1]
     for m in range(micros):
         branch_one, resid, gate, up = saved[m]
-        branch_two = scatter_sum_dp(partials[m][:half], partials[m][half:], nd)
+        branch_two = scatter_sum_dp(partials[m][1], partials[m][0], nd)
         outputs.append((resid + rms_gain(branch_two, post_ffw)).astype(BF))
         upstream = cotangent[m, 0].astype(F32)
         grad_two, grad_post_ffw = jax.vjp(rms_gain, branch_two, post_ffw)[1](upstream)
         gathered_two.append(gather_dp(grad_two.astype(BF), nd))
         saved[m] += [upstream, grad_post_ffw]
+    def weight_term(lefts, rights, follow):
+        left = jnp.concatenate(lefts, axis=0)
+        term = dot_tn(after(left, *follow), jnp.concatenate(rights, axis=0))
+        return term.astype(BF)
+
+    def sum_rows(term):
+        return lax.psum_scatter(term, "fsdp", scatter_dimension=0, tiled=True)
+
     for m in range(micros):
-        branch_one, resid, gate, up, upstream, grad_post_ffw = saved[m]
+        gate, up = saved[m][2:4]
+        if m == micros - 1:
+            last = down_term = weight_term(gathered_two, hiddens, (last,))
         grad_hidden = dot_nn(after(gathered_two[m], last), w_down)
         grad_gate, grad_up = jax.vjp(
             lambda gate_in, up_in: jax.nn.gelu(gate_in, approximate=True) * up_in, gate, up
@@ -536,44 +574,54 @@
         low_ups.append(grad_up.astype(BF))
         last = low_ups[-1]
 
-    def weight_term(lefts, rights, follow):
-        left = jnp.concatenate(lefts, axis=0)
-        term = dot_tn(after(left, *follow), jnp.concatenate(rights, axis=0))
-        return term.astype(BF)
-
     def from_x(root, *ties):
-        root = after(root, *ties)
+        root = after(root, *ties) if ties else root
         return [root] + [shift_x(root, nd, k) for k in range(1, nd // 2)]
 
     right_mine = from_x(root_right[0], *gathered_two)
-    down_term = weight_term(gathered_two, hiddens, (last,))
-    def sum_rows(term):
-        return lax.psum_scatter(term, "fsdp", scatter_dimension=0, tiled=True)
-
     down_band = sum_rows(down_term)
-    last = down_term
+    gate_term = weight_term(gathered_in, low_gates, (last,))
+    up_term = weight_term(gathered_in, low_ups, (gate_term,))
+    both_term = jnp.concatenate([gate_term, up_term], axis=1)
+    both_band = sum_rows(both_term)
+    last = both_term
     for m in range(micros):
-        branch_one, resid, gate, up, upstream, grad_post_ffw = saved[m]
-        ties = [last] if m else [last] + right_mine[1:]
-        partial = dot_nt(after(low_gates[m], *ties), w_gate) + dot_nt(low_ups[m], w_up)
-        last = partial
-        grad_ffw_in = scatter_sum_dp(partial[:half], partial[half:], nd)
+        branch_one, resid, _, _, upstream, grad_post_ffw = saved[m]
+        gate_in, up_in = (after(low_gates[m], last, *right_mine[1:]), low_ups[m])
+        away = dot_nt(gate_in[half:], w_gate) + dot_nt(up_in[half:], w_up)
+        gate_in = after(gate_in, away)
+        last = dot_nt(gate_in[:half], w_gate) + dot_nt(up_in[:half], w_up)
+        grad_ffw_in = scatter_sum_dp(last, away, nd)
         grad_resid, grad_pre_ffw = jax.vjp(rms_gain, resid, pre_ffw)[1](grad_ffw_in)
         grad_resid = upstream + grad_resid
         grad_one, grad_post_attn = jax.vjp(rms_gain, branch_one, post_attn)[1](grad_resid)
         grad_resids.append(grad_resid)
         low_ones.append(grad_one.astype(BF))
         gain_terms.append((grad_post_attn, grad_pre_ffw, grad_post_ffw))
-    gate_term = weight_term(gathered_in, low_gates, (last,))
-    up_term = weight_term(gathered_in, low_ups, (gate_term,))
-    both_band = sum_rows(jnp.concatenate([gate_term, up_term], axis=1))
 
     low_one = jnp.concatenate(low_ones, axis=0)
     attended = jnp.concatenate(all_attended, axis=0)
-    left_mine = [from_x(root_left[0, :, :, :BC], low_one)]
-    if band > BC:
-        left_mine.append(from_x(root_left[0, :, :, BC:].transpose(0, 2, 1), left_mine[0][-1]))
-    low_mixed = dot_nn(after(low_one, up_term), w_out).astype(BF).reshape(micros, rows, HEADS, HD)
+    owners_at = part_owners(nd)
+    qkv_per, out_per = (-(-QKVW // (BC * nd)), -(-OUTW // (BC * nd)))
+
+    def term_over_dp(left, right, per_index):
+        size = per_index * BC
+        right = jnp.pad(right, ((0, 0), (0, nd * size - right.shape[1])))
+        terms = [
+            dot_tn(left, lax.dynamic_slice(right, (0, index * size), (count, size)))
+            for index in owners_at
+        ]
+        mine, away = (terms[: nd // 2], terms[nd // 2 :])
+        away = jnp.concatenate(away, axis=0).astype(BF)
+        return (scatter_sum_dp(jnp.concatenate(mine, axis=0), away, nd), away)
+
+    out_sum, _ = term_over_dp(low_one, attended, out_per)
+    left_root = after(root_left[0], low_one)
+    left_pieces = pack_roots(left_root) if band > BC else [left_root]
+    left_mine = [from_x(left) for left in left_pieces]
+    left_here = [piece for mine in left_mine for piece in mine[1:]]
+
+    low_mixed = dot_nn(after(low_one, down_band, *left_pieces), w_out).astype(BF).reshape(micros, rows, HEADS, HD)
     grad_queries, key_terms = [], []
     for m in range(micros):
         for_queries, for_keys, for_values = attend_back(
@@ -583,8 +631,7 @@
         terms = jnp.concatenate([for_keys, for_values], axis=1)
         key_terms.append(return_key_grads(terms, rows, nf))
         last = terms
-    own_terms = jnp.concatenate(key_terms, axis=0)
-    out_term = dot_tn(after(low_one, last), attended)
+    own_terms = after(jnp.concatenate(key_terms, axis=0), *left_here)
     grad_keys, grad_values = (own_terms[:, :HD], own_terms[:, HD:])
 
     def heads_only(query_in, key_in, query_scale, key_scale):
@@ -601,34 +648,22 @@
     grad_in, grad_pre_attn = jax.vjp(rms_gain, flat_in, pre_attn)[1](grad_normed)
     input_grad = (jnp.concatenate(grad_resids, axis=0) + grad_in).astype(BF)
 
-    attn_per = -(-ATTN_BLOCKS // nd)
-    attn_width = attn_per * BC
-    attn_term = jnp.concatenate([dot_tn(normed, low_projected), out_term], axis=1)
-    attn_term = jnp.pad(attn_term, ((0, 0), (0, nd * attn_width - ATTN_BLOCKS * BC)))
-
-    def owner_columns(index):
-        return lax.dynamic_slice(attn_term, (0, index * attn_width), (D, attn_width))
-
-    attn_term = after(attn_term, *left_mine[-1])
-    owners_at = part_owners(nd)
-    attn_sum = scatter_sum_dp(
-        jnp.concatenate([owner_columns(e) for e in owners_at[: nd // 2]], axis=0),
-        jnp.concatenate([owner_columns(e) for e in owners_at[nd // 2 :]], axis=0),
-        nd,
-    )
+    qkv_sum, qkv_away = term_over_dp(after(normed, both_band), low_projected, qkv_per)
+    attn_sum = jnp.concatenate([qkv_sum, out_sum], axis=1).astype(BF)
     ff_all = gather_columns([both_band, down_band])
-    attn_band = direct_reduce(after(attn_sum, both_band).astype(BF), nf)
+    attn_band = direct_reduce(after(attn_sum, both_band), nf)
     attn_all = gather_relative([attn_band])
 
-    def all_parts(mine):
-        parts = [after(piece, attn_sum) for piece in mine + [swap_core(piece, nd) for piece in mine]]
+    def all_parts(mine, *ties):
+        parts = mine + [swap_core(piece, nd) for piece in mine]
+        parts = [after(piece, *ties) for piece in parts]
         out = jnp.zeros((nd,) + parts[0].shape, BF)
         for place, piece in enumerate(parts):
             out = lax.dynamic_update_slice(out, piece[None], (place,) + (0,) * piece.ndim)
         return out.reshape((nd * capacity,) + out.shape[2:])
 
-    left_roots = [all_parts(mine) for mine in left_mine]
-    right_roots = all_parts(right_mine)
+    right_roots = all_parts(right_mine, qkv_away)
+    left_roots = [all_parts(mine, qkv_away) for mine in left_mine]
 
     def relative(index):
         nx = nd // 2
@@ -639,14 +674,16 @@
     ff_dp = np.minimum(ff_index % FF_BLOCKS // per, nd - 1)
     ff_column = ff_index % FF_BLOCKS - np.minimum(ff_dp * per, FF_BLOCKS - per)
     ff_column = ff_column + ff_index // FF_BLOCKS * per
-    attn_index = np.arange(ATTN_BLOCKS)
+    qkv_index, out_index = (np.arange(QKVW // BC), np.arange(OUTW // BC))
+    attn_dp = np.concatenate([qkv_index // qkv_per, out_index // out_per])
+    attn_column = np.concatenate([qkv_index % qkv_per, qkv_per + out_index % out_per])
     part_of = relative(
-        jnp.asarray(np.concatenate([attn_index // attn_per, ff_dp]).astype(np.int32))
+        jnp.asarray(np.concatenate([attn_dp, ff_dp]).astype(np.int32))
     )
     kind_of = jnp.asarray(
         np.zeros(NBLK).astype(np.int32)
     )
-    column_of = jnp.asarray(np.concatenate([attn_index % attn_per, ff_column]).astype(np.int32))
+    column_of = jnp.asarray(np.concatenate([attn_column, ff_column]).astype(np.int32))
 
     owners = owner[:, 0]
     index = jnp.arange(NBLK, dtype=jnp.int32)

time: 806 us -> 772 us (0.958)
  waiting for transfers between devices: 246 us -> 226 us
  local copies, waits for them, and re-layouts: 105 us -> 91.1 us
    ppermute x2, waiting for transfers between devices: 36.9 us -> 7.65 us  [return_key_grads(): lax.ppermute(first.astype(BF), 'fsdp', backwards(TO_SECOND)).astype(F32)]
    ppermute x14, waiting for transfers between devices: 42.9 us -> 22.2 us  [swap_fsdp(): return lax.ppermute(value, 'fsdp', [(e, e ^ flip) for e in range(nf)])]
    reduce_scatter x2, waiting for transfers between devices: 0.02 us -> 13.1 us  [sum_rows(): return lax.psum_scatter(term, 'fsdp', scatter_dimension=0, tiled=True)]
    all_gather x1, waiting for transfers between devices: 0.84 us -> 12.7 us  [local(): w_down = lax.all_gather(down_cols, 'fsdp', axis=0, tiled=True)]
    ppermute x14, starting transfers between devices: 37.9 us -> 47 us  [swap_fsdp(): return lax.ppermute(value, 'fsdp', [(e, e ^ flip) for e in range(nf)])]
    concatenate x3 -> x6, other arithmetic: 19.1 us -> 11.3 us  [the longest x1 7.41 us: local(): both_term = jnp.concatenate([gate_term, up_term], axis=1)]
    dot_general x5 -> x11, matrix products: 48 us -> 42.3 us  [dot_tn(): lax.dot_general(left, right, (((0,), (0,)), ((), ())), preferred_element_...]
    ppermute x15 -> x16, waiting for transfers between devices: 138 us -> 134 us  [shift_x(): return lax.ppermute(value, 'dp', pairs)]
  transfers between devices with their start and end apart: 84 -> 86, of which waited for: 31 -> 33; matrix products, arithmetic and copies ran while one was open for 42% -> 39% of each run, Pallas kernels for 5% -> 6%
where the time goes in v4:
time: 772 us; the launch traced here: 762 us
  waiting for transfers between devices  226 us (29%)
  matrix products  177 us (23%)
  starting transfers between devices  110 us (14%)
  local copies, waits for them, and re-layouts  91.1 us (12%)
  other arithmetic  76.8 us (10%)
  Pallas kernels  60.4 us (8%)
  between operations  19.8 us (3%)
    ppermute x16, waiting for transfers between devices, shift_x(): return lax.ppermute(value, 'dp', pairs)  134 us
    dot_general x8, matrix products, dot_nn(): return jnp.dot(left, right, preferred_element_type=F32)  66.1 us
    dot_general x15, matrix products, dot_nt(): lax.dot_general(left, right, (((1,), (1,)), ((), ())), preferred_element_...  55.4 us
    ppermute x14, starting transfers between devices, swap_fsdp(): return lax.ppermute(value, 'fsdp', [(e, e ^ flip) for e in range(nf)])  47 us
    dot_general x11, matrix products, dot_tn(): lax.dot_general(left, right, (((0,), (0,)), ((), ())), preferred_element_...  42.3 us
    pallas_call x2, Pallas kernels, update_blocks(): pl.pallas_call(lambda *refs: update_body(group, len(sources), len(left_ro...  37.3 us
    dynamic_update_slice x12, local copies, waits for them, and re-layouts, all_parts(): lax.dynamic_update_slice(out, piece[None], (place,) + (0,) * piece.ndim)  26.3 us
    unnamed x343, local copies, waits for them, and re-layouts  23.1 us
  transfers between devices with their start and end apart: 86, of which 33 were waited for; matrix products, arithmetic and copies ran while one was open for 39% of the time, Pallas kernels for 6%

profile of v4, /device:TPU:0, one launch (start us, length us, event | category | flops | bytes accessed | tf_op | source)
XLA Modules:
  0.0 762.0 jit_solution(14678608081979749309)
XLA Ops:
  35.0 15.3 %collective-permute-done.2 = bf16[144,768]{1,0:T(8,128)(2,1)S(1)} collective-permute-done((bf16[144,768]{1,0:T(8,128)(2,1)}, bf16[144,768]{1,0:T(8,128)(2,1)S(1)}, u32[]{:S(2)}, u32[]{:S(2)}) %collective-permute-start.2) | collective-permute-done | bytes 221216 | tf_op jit(solution)/shard_map/ppermute | solution.py:164
  88.6 23.3 %collective-permute-start.18 = (bf16[144,512]{1,0:T(8,128)(2,1)S(1)}, bf16[144,512]{1,0:T(8,128)(2,1)S(1)}, u32[]{:S(2)}, u32[]{:S(2)}) collective-permute-start(bf16[144,512]{1,0:T(8,128)(2,1)S(1)} %dynamic-slice_convert_fusion.4), channel_id=1, source_target_pairs={{0,6},{1,7},{2,4},{3,5},{4,2},{5,3},{6,0},{7,1},{8,14},{9,15},{10,... | collective-permute-start | bytes 442376 | tf_op jit(solution)/shard_map/ppermute | solution.py:164
  155.4 14.1 %collective-permute-done.21 = bf16[256,1152]{1,0:T(8,128)(2,1)S(1)} collective-permute-done((bf16[256,1152]{1,0:T(8,128)(2,1)}, bf16[256,1152]{1,0:T(8,128)(2,1)S(1)}, u32[]{:S(2)}, u32[]{:S(2)}) %collective-permute-start.21) | collective-permute-done | bytes 589856 | tf_op jit(solution)/shard_map/ppermute | solution.py:115
  175.5 14.2 %collective-permute-done.29 = bf16[256,1152]{1,0:T(8,128)(2,1)S(1)} collective-permute-done((bf16[256,1152]{1,0:T(8,128)(2,1)S(1)}, bf16[256,1152]{1,0:T(8,128)(2,1)S(1)}, u32[]{:S(2)}, u32[]{:S(2)}) %collective-permute-start.29) | collective-permute-done | bytes 589856 | tf_op jit(solution)/shard_map/ppermute | solution.py:115
  201.8 11.6 %multiply_convert_fusion.3 = (bf16[1024,1792]{1,0:T(8,128)(2,1)}, f32[1024,1792]{1,0:T(8,128)}) fusion(f32[1024,1792]{1,0:T(8,128)S(1)} %fusion.64, bf16[1152,3584]{1,0:T(8,128)(2,1)S(1)} %copy-done.147, bf16[256,1152]{1,0:T(8,128)(2,1)S(1)} %copy-done.83, bf16[256,1152]{1,0:T(8,128)(2,1)S(1)} %collective-permute-done.22, ...), kind=kOutput, calls=%fused_computation.36 | convolution fusion | flops 4255645696 | bytes 24838144 | tf_op jit(solution)/shard_map/dot_general | solution.py:97
  218.3 8.5 %multiply_convert_fusion.2 = (bf16[1024,1792]{1,0:T(8,128)(2,1)}, f32[1024,1792]{1,0:T(8,128)}) fusion(f32[1024,1792]{1,0:T(8,128)S(1)} %fusion.62, bf16[1024,1152]{1,0:T(8,128)(2,1)S(1)} %copy-done.72, bf16[1152,3584]{1,0:T(8,128)(2,1)S(1)} %copy-done.147), kind=kOutput, calls=%fused_computation.35 | convolution fusion | flops 4246208512 | bytes 24838144 | tf_op jit(solution)/shard_map/dot_general | solution.py:97
  226.8 12.7 %all-gather.5.cloned.1.call-done = bf16[1152,1792]{1,0:T(8,128)(2,1)} async-done(((bf16[144,1792]{1,0:T(8,128)(2,1)}), bf16[1152,1792]{1,0:T(8,128)(2,1)}) %all-gather.5.cloned.1.call-update) | async-done | bytes 4128784 | tf_op jit(solution)/shard_map/all_gather | solution.py:497
  260.1 9.5 %collective-permute-done.33 = bf16[256,1152]{1,0:T(8,128)(2,1)S(1)} collective-permute-done((bf16[256,1152]{1,0:T(8,128)(2,1)S(1)}, bf16[256,1152]{1,0:T(8,128)(2,1)S(1)}, u32[]{:S(2)}, u32[]{:S(2)}) %collective-permute-start.33) | collective-permute-done | bytes 589856 | tf_op jit(solution)/shard_map/ppermute | solution.py:115
  269.9 11.8 %collective-permute-done.35 = bf16[256,1152]{1,0:T(8,128)(2,1)S(1)} collective-permute-done((bf16[256,1152]{1,0:T(8,128)(2,1)S(1)}, bf16[256,1152]{1,0:T(8,128)(2,1)S(1)}, u32[]{:S(2)}, u32[]{:S(2)}) %collective-permute-start.35) | collective-permute-done | bytes 589856 | tf_op jit(solution)/shard_map/ppermute | solution.py:115
  289.3 10.7 %collective-permute-done.36 = bf16[256,1152]{1,0:T(8,128)(2,1)S(1)} collective-permute-done((bf16[256,1152]{1,0:T(8,128)(2,1)S(1)}, bf16[256,1152]{1,0:T(8,128)(2,1)S(1)}, u32[]{:S(2)}, u32[]{:S(2)}) %collective-permute-start.36) | collective-permute-done | bytes 589856 | tf_op jit(solution)/shard_map/ppermute | solution.py:115
  304.4 13.6 %fusion.8 = (bf16[1024,1792]{1,0:T(8,128)(2,1)}, bf16[1024,1792]{1,0:T(8,128)(2,1)}) fusion(f32[1024,1792]{1,0:T(8,128)} %copy-done.158, f32[1024,1792]{1,0:T(8,128)} %get-tuple-element.275, bf16[1024,1152]{1,0:T(8,128)(2,1)S(1)} %pad_maximum_fusion.3, bf16[1152,1792]{1,0:T(8,128)(2,1)S(1)} %copy-done.148), kind=kOutput, calls=%fused_computation.16 | convolution fusion | flops 4271898624 | bytes 28508160 | tf_op jit(solution)/shard_map/dot_general | solution.py:97
  327.1 10.7 %convolution_convert_fusion.2 = bf16[1152,1792]{1,0:T(8,128)(2,1)} fusion(bf16[2048,1152]{1,0:T(8,128)(2,1)S(1)} %constant_dynamic-update-slice_fusion.8, bf16[1024,1792]{1,0:T(8,128)(2,1)S(1)} %copy-done.81, bf16[1024,1792]{1,0:T(8,128)(2,1)S(1)} %copy-done.80), kind=kOutput, calls=%fused_computation.9 | convolution fusion | flops 8472461312 | bytes 16187392 | tf_op jit(solution)/shard_map/dot_general | solution.py:105
  339.9 14.2 %fusion.15 = (bf16[1024,1792]{1,0:T(8,128)(2,1)}, bf16[1024,1792]{1,0:T(8,128)(2,1)S(1)}) fusion(f32[1024,1792]{1,0:T(8,128)} %copy-done.157, f32[1024,1792]{1,0:T(8,128)} %get-tuple-element.277, bf16[1024,1152]{1,0:T(8,128)(2,1)S(1)} %pad_maximum_fusion.4, bf16[1152,1792]{1,0:T(8,128)(2,1)} %all-gather.5.cloned.1.call-done), kind=kOutput, calls=%fused_computation.23 | convolution fusion | flops 4271898624 | bytes 28508160 | tf_op jit(solution)/shard_map/dot_general | solution.py:97
  355.3 12.8 %convolution_convert_fusion.1 = bf16[1152,1792]{1,0:T(8,128)(2,1)} fusion(bf16[2048,1152]{1,0:T(8,128)(2,1)S(1)} %bitcast.287, bf16[1024,1792]{1,0:T(8,128)(2,1)} %get-tuple-element.77, bf16[1024,1792]{1,0:T(8,128)(2,1)S(1)} %copy-done.153), kind=kOutput, calls=%fused_computation.8 | convolution fusion | flops 8472461312 | bytes 16187392 | tf_op jit(solution)/shard_map/dot_general | solution.py:105
  368.1 11.0 %convolution_convert_fusion = bf16[1152,1792]{1,0:T(8,128)(2,1)} fusion(bf16[2048,1152]{1,0:T(8,128)(2,1)S(1)} %bitcast.287, bf16[1024,1792]{1,0:T(8,128)(2,1)S(1)} %get-tuple-element.223, bf16[1024,1792]{1,0:T(8,128)(2,1)S(1)} %copy-done.151), kind=kOutput, calls=%fused_computation.7 | convolution fusion | flops 8472461312 | bytes 16187392 | tf_op jit(solution)/shard_map/dot_general | solution.py:105
  427.7 11.8 %collective-permute-done.46 = bf16[256,1152]{1,0:T(8,128)(2,1)} collective-permute-done((bf16[256,1152]{1,0:T(8,128)(2,1)}, bf16[256,1152]{1,0:T(8,128)(2,1)}, u32[]{:S(2)}, u32[]{:S(2)}) %collective-permute-start.46) | collective-permute-done | bytes 589856 | tf_op jit(solution)/shard_map/ppermute | solution.py:115
  439.5 11.8 %collective-permute-done.44 = bf16[256,1152]{1,0:T(8,128)(2,1)} collective-permute-done((bf16[256,1152]{1,0:T(8,128)(2,1)}, bf16[256,1152]{1,0:T(8,128)(2,1)}, u32[]{:S(2)}, u32[]{:S(2)}) %collective-permute-start.44) | collective-permute-done | bytes 589856 | tf_op jit(solution)/shard_map/ppermute | solution.py:115
  542.0 8.9 %collective-permute-done.56 = bf16[57,16,144]{2,1,0:T(8,128)(2,1)} collective-permute-done((bf16[57,16,144]{2,1,0:T(8,128)(2,1)S(1)}, bf16[57,16,144]{2,1,0:T(8,128)(2,1)}, u32[]{:S(2)}, u32[]{:S(2)}) %collective-permute-start.56) | collective-permute-done | bytes 262688 | tf_op jit(solution)/shard_map/ppermute | solution.py:115
  569.3 13.1 %reduce-scatter.5.cloned.1.call-done = bf16[144,3584]{1,0:T(8,128)(2,1)} async-done(((bf16[1152,3584]{1,0:T(8,128)(2,1)}), bf16[144,3584]{1,0:T(8,128)(2,1)}) %reduce-scatter.5.cloned.1.call-update) | async-done | bytes 1032208 | tf_op jit(solution)/shard_map/reduce_scatter | solution.py:563
  615.8 13.1 %collective-permute-done.64 = bf16[1152,384]{1,0:T(8,128)(2,1)S(1)} collective-permute-done((bf16[1152,384]{1,0:T(8,128)(2,1)S(1)}, bf16[1152,384]{1,0:T(8,128)(2,1)S(1)}, u32[]{:S(2)}, u32[]{:S(2)}) %collective-permute-start.64) | collective-permute-done | bytes 884768 | tf_op jit(solution)/shard_map/ppermute | solution.py:115
  644.4 9.0 %collective-permute-done.57 = bf16[144,3584]{1,0:T(8,128)(2,1)} collective-permute-done((bf16[144,3584]{1,0:T(8,128)(2,1)S(1)}, bf16[144,3584]{1,0:T(8,128)(2,1)}, u32[]{:S(2)}, u32[]{:S(2)}) %collective-permute-start.57) | collective-permute-done | bytes 1032224 | tf_op jit(solution)/shard_map/ppermute | solution.py:115
  656.8 14.1 %all-to-all-done = bf16[8,144,640]{2,1,0:T(8,128)(2,1)} async-done(((bf16[8,144,640]{2,1,0:T(8,128)(2,1)}), bf16[8,144,640]{2,1,0:T(8,128)(2,1)}, u32[]{:S(2)}, u32[]{:S(2)}) %all-to-all-start) | async-done | bytes 1474592 | tf_op jit(solution)/shard_map/all_to_all | solution.py:184
  688.6 12.7 %owner_stats.2 = (f32[57,144,128]{2,1,0:T(8,128)}, f32[57,144,144]{2,1,0:T(8,128)}, f32[57,128,128]{2,1,0:T(8,128)}) custom-call(s32[57]{0:T(128)S(1)} %get-tuple-element.193.refs_0_, s32[57]{0:T(128)S(1)} %broadcast.987.refs_1_, s32[57]{0:T(128)S(1)} %get-tuple-element.192.refs_2_, s32[57]{0:T(128)S(1)} %get-tuple-element.191.refs_3_, ...), custom_call_target="tpu_custom_call" | custom-call | tf_op jit(solution)/shard_map/owner_stats/pallas_call | solution.py:333
  701.3 30.5 %update_blocks.2 = (f32[144,23296]{1,0:T(8,128)}, bf16[144,23296]{1,0:T(8,128)(2,1)}) custom-call(s32[161]{0:T(256)S(1)} %slice.310.refs_0_, s32[161]{0:T(256)S(1)} %broadcast.985.refs_1_, s32[161]{0:T(256)S(1)} %copy-done.4, s32[161]{0:T(256)S(1)} %slice.313.refs_3_, s32[161]{0:T(256)S(1)} %slice.314.refs_4_, ...), custom_call_target="tpu_custom_call" | custom-call | tf_op jit(solution)/shard_map/update_blocks/pallas_call | solution.py:287
  (748 shorter events, 423.2 us)
Async XLA Ops:
  7.2 187.0 %all-gather.3.cloned.1.call-start = ((), (), s32[]{:S(2)}) async-start(), calls=%async_computation.3 | async-start | bytes 9289728 | tf_op jit(solution)/shard_map/all_gather | solution.py:495
  20.3 219.2 %all-gather.5.cloned.1.call-start = ((), (), s32[]{:S(2)}) async-start(), calls=%async_computation.4 | async-start | bytes 4644864 | tf_op jit(solution)/shard_map/all_gather | solution.py:497
  60.4 28.3 %collective-permute-start.14 = (bf16[144,512]{1,0:T(8,128)(2,1)S(1)}, bf16[144,512]{1,0:T(8,128)(2,1)S(1)}, u32[]{:S(2)}, u32[]{:S(2)}) collective-permute-start(bf16[144,512]{1,0:T(8,128)(2,1)S(1)} %dynamic-slice_convert_fusion.4), channel_id=1, source_target_pairs={{0,2},{1,3},{2,0},{3,1},{4,6},{5,7},{6,4},{7,5},{8,10},{9,11},{10,... | collective-permute-start | bytes 442376 | tf_op jit(solution)/shard_map/ppermute | solution.py:164
  62.1 55.2 %collective-permute-start.10 = (bf16[256,512]{1,0:T(8,128)(2,1)S(1)}, bf16[256,512]{1,0:T(8,128)(2,1)}, u32[]{:S(2)}, u32[]{:S(2)}) collective-permute-start(bf16[256,512]{1,0:T(8,128)(2,1)S(1)} %get-tuple-element.248), channel_id=1, source_target_pairs={{0,1},{1,2},{2,3},{8,9},{9,10},{10,11},{16,17},{17,18},{18,19},{24... | collective-permute-start | bytes 786440 | tf_op jit(solution)/shard_map/ppermute | solution.py:383
  78.1 47.4 %collective-permute-start.11 = (bf16[256,512]{1,0:T(8,128)(2,1)}, bf16[256,512]{1,0:T(8,128)(2,1)S(1)}, u32[]{:S(2)}, u32[]{:S(2)}) collective-permute-start(bf16[256,512]{1,0:T(8,128)(2,1)} %collective-permute-done.8), channel_id=1, source_target_pairs={{4,5},{5,4},{12,13},{13,12},{20,21},{21,20},{28,29},{29,28}} | collective-permute-start | bytes 786440 | tf_op jit(solution)/shard_map/ppermute | solution.py:385
  86.2 26.8 %collective-permute-start.25 = (bf16[256,512]{1,0:T(8,128)(2,1)}, bf16[256,512]{1,0:T(8,128)(2,1)S(1)}, u32[]{:S(2)}, u32[]{:S(2)}) collective-permute-start(bf16[256,512]{1,0:T(8,128)(2,1)} %collective-permute-done.24), channel_id=1, source_target_pairs={{4,6},{5,7},{12,14},{13,15},{20,22},{21,23},{28,30},{29,31}} | collective-permute-start | bytes 786440 | tf_op jit(solution)/shard_map/ppermute | solution.py:384
  86.9 39.3 %collective-permute-start.12 = (bf16[256,512]{1,0:T(8,128)(2,1)S(1)}, bf16[256,512]{1,0:T(8,128)(2,1)S(1)}, u32[]{:S(2)}, u32[]{:S(2)}) collective-permute-start(bf16[256,512]{1,0:T(8,128)(2,1)S(1)} %collective-permute-done.9), channel_id=1, source_target_pairs={{6,7},{7,6},{14,15},{15,14},{22,23},{23,22},{30,31},{31,30}} | collective-permute-start | bytes 786440 | tf_op jit(solution)/shard_map/ppermute | solution.py:386
  88.6 39.8 %collective-permute-start.18 = (bf16[144,512]{1,0:T(8,128)(2,1)S(1)}, bf16[144,512]{1,0:T(8,128)(2,1)S(1)}, u32[]{:S(2)}, u32[]{:S(2)}) collective-permute-start(bf16[144,512]{1,0:T(8,128)(2,1)S(1)} %dynamic-slice_convert_fusion.4), channel_id=1, source_target_pairs={{0,6},{1,7},{2,4},{3,5},{4,2},{5,3},{6,0},{7,1},{8,14},{9,15},{10,... | collective-permute-start | bytes 442376 | tf_op jit(solution)/shard_map/ppermute | solution.py:164
  155.2 330.6 %reduce-scatter.3.cloned.1.call-start = ((), (), s32[]{:S(2)}) async-start(), calls=%async_computation.5 | async-start | bytes 4644864 | tf_op jit(solution)/shard_map/reduce_scatter | solution.py:563
  337.9 244.5 %reduce-scatter.5.cloned.1.call-start = ((), (), s32[]{:S(2)}) async-start(), calls=%async_computation.6 | async-start | bytes 9289728 | tf_op jit(solution)/shard_map/reduce_scatter | solution.py:563
  354.1 43.2 %collective-permute-start.42 = (bf16[57,128,128]{2,1,0:T(8,128)(2,1)}, bf16[57,128,128]{2,1,0:T(8,128)(2,1)}, u32[]{:S(2)}, u32[]{:S(2)}) collective-permute-start(bf16[57,128,128]{2,1,0:T(8,128)(2,1)} %bitcast.20), channel_id=1, source_target_pairs={{0,16},{8,24},{16,0},{24,8},{1,17},{9,25},{17,1},{25,9},{2,18},{10... | collective-permute-start | bytes 5603336 | tf_op jit(solution)/shard_map/ppermute | solution.py:115
  476.4 74.5 %collective-permute-start.55 = (bf16[57,144,128]{2,1,0:T(8,128)(2,1)S(1)}, bf16[57,144,128]{2,1,0:T(8,128)(2,1)}, u32[]{:S(2)}, u32[]{:S(2)}) collective-permute-start(bf16[57,144,128]{2,1,0:T(8,128)(2,1)S(1)} %get-tuple-element.92), channel_id=1, source_target_pairs={{0,16},{8,24},{16,0},{24,8},{1,17},{9,25},{17,1},{25,9},{2,18},{10... | collective-permute-start | bytes 6303752 | tf_op jit(solution)/shard_map/ppermute | solution.py:115
  501.0 28.7 %collective-permute-start.47 = (bf16[256,512]{1,0:T(8,128)(2,1)}, bf16[256,512]{1,0:T(8,128)(2,1)}, u32[]{:S(2)}, u32[]{:S(2)}) collective-permute-start(bf16[256,512]{1,0:T(8,128)(2,1)} %fusion.106), channel_id=1, source_target_pairs={{1,0},{2,1},{3,2},{9,8},{10,9},{11,10},{17,16},{18,17},{19,18},{25... | collective-permute-start | bytes 786440 | tf_op jit(solution)/shard_map/ppermute | solution.py:397
  529.8 57.1 %collective-permute-start.79 = (bf16[57,128,128]{2,1,0:T(8,128)(2,1)}, bf16[57,128,128]{2,1,0:T(8,128)(2,1)}, u32[]{:S(2)}, u32[]{:S(2)}) collective-permute-start(bf16[57,128,128]{2,1,0:T(8,128)(2,1)} %bitcast.20), channel_id=1, source_target_pairs={{0,8},{8,0},{16,24},{24,16},{1,9},{9,1},{17,25},{25,17},{2,10},{10... | collective-permute-start | bytes 5603336 | tf_op jit(solution)/shard_map/ppermute | solution.py:109
  536.3 50.4 %collective-permute-start.80 = (bf16[57,128,128]{2,1,0:T(8,128)(2,1)}, bf16[57,128,128]{2,1,0:T(8,128)(2,1)}, u32[]{:S(2)}, u32[]{:S(2)}) collective-permute-start(bf16[57,128,128]{2,1,0:T(8,128)(2,1)} %collective-permute-done.42), channel_id=1, source_target_pairs={{0,8},{8,0},{16,24},{24,16},{1,9},{9,1},{17,25},{25,17},{2,10},{10... | collective-permute-start | bytes 5603336 | tf_op jit(solution)/shard_map/ppermute | solution.py:109
  537.6 49.8 %collective-permute-start.77 = (bf16[57,16,144]{2,1,0:T(8,128)(2,1)S(1)}, bf16[57,16,144]{2,1,0:T(8,128)(2,1)}, u32[]{:S(2)}, u32[]{:S(2)}) collective-permute-start(bf16[57,16,144]{2,1,0:T(8,128)(2,1)S(1)} %get-tuple-element.96), channel_id=1, source_target_pairs={{0,8},{8,0},{16,24},{24,16},{1,9},{9,1},{17,25},{25,17},{2,10},{10... | collective-permute-start | bytes 787976 | tf_op jit(solution)/shard_map/ppermute | solution.py:109
  550.9 36.6 %collective-permute-start.75 = (bf16[57,144,128]{2,1,0:T(8,128)(2,1)S(1)}, bf16[57,144,128]{2,1,0:T(8,128)(2,1)}, u32[]{:S(2)}, u32[]{:S(2)}) collective-permute-start(bf16[57,144,128]{2,1,0:T(8,128)(2,1)S(1)} %get-tuple-element.92), channel_id=1, source_target_pairs={{0,8},{8,0},{16,24},{24,16},{1,9},{9,1},{17,25},{25,17},{2,10},{10... | collective-permute-start | bytes 6303752 | tf_op jit(solution)/shard_map/ppermute | solution.py:109
  550.9 37.0 %collective-permute-start.60 = (bf16[144,1792]{1,0:T(8,128)(2,1)}, bf16[144,1792]{1,0:T(8,128)(2,1)}, u32[]{:S(2)}, u32[]{:S(2)}) collective-permute-start(bf16[144,1792]{1,0:T(8,128)(2,1)} %reduce-scatter.3.cloned.1.call-done), channel_id=1, source_target_pairs={{0,16},{8,24},{16,0},{24,8},{1,17},{9,25},{17,1},{25,9},{2,18},{10... | collective-permute-start | bytes 1548296 | tf_op jit(solution)/shard_map/ppermute | solution.py:115
  586.8 50.4 %collective-permute-start.78 = (bf16[57,16,144]{2,1,0:T(8,128)(2,1)}, bf16[57,16,144]{2,1,0:T(8,128)(2,1)}, u32[]{:S(2)}, u32[]{:S(2)}) collective-permute-start(bf16[57,16,144]{2,1,0:T(8,128)(2,1)} %collective-permute-done.56), channel_id=1, source_target_pairs={{0,8},{8,0},{16,24},{24,16},{1,9},{9,1},{17,25},{25,17},{2,10},{10... | collective-permute-start | bytes 787976 | tf_op jit(solution)/shard_map/ppermute | solution.py:109
  587.4 49.9 %collective-permute-start.76 = (bf16[57,144,128]{2,1,0:T(8,128)(2,1)}, bf16[57,144,128]{2,1,0:T(8,128)(2,1)}, u32[]{:S(2)}, u32[]{:S(2)}) collective-permute-start(bf16[57,144,128]{2,1,0:T(8,128)(2,1)} %collective-permute-done.55), channel_id=1, source_target_pairs={{0,8},{8,0},{16,24},{24,16},{1,9},{9,1},{17,25},{25,17},{2,10},{10... | collective-permute-start | bytes 6303752 | tf_op jit(solution)/shard_map/ppermute | solution.py:109
  587.5 95.0 %collective-permute-start.61 = (bf16[144,1792]{1,0:T(8,128)(2,1)}, bf16[144,1792]{1,0:T(8,128)(2,1)}, u32[]{:S(2)}, u32[]{:S(2)}) collective-permute-start(bf16[144,1792]{1,0:T(8,128)(2,1)} %reduce-scatter.3.cloned.1.call-done), channel_id=1, source_target_pairs={{0,8},{8,0},{16,24},{24,16},{1,9},{9,1},{17,25},{25,17},{2,10},{10... | collective-permute-start | bytes 1548296 | tf_op jit(solution)/shard_map/ppermute | solution.py:109
  587.9 98.8 %collective-permute-start.62 = (bf16[144,1792]{1,0:T(8,128)(2,1)}, bf16[144,1792]{1,0:T(8,128)(2,1)}, u32[]{:S(2)}, u32[]{:S(2)}) collective-permute-start(bf16[144,1792]{1,0:T(8,128)(2,1)} %collective-permute-done.60), channel_id=1, source_target_pairs={{0,8},{8,0},{16,24},{24,16},{1,9},{9,1},{17,25},{25,17},{2,10},{10... | collective-permute-start | bytes 1548296 | tf_op jit(solution)/shard_map/ppermute | solution.py:109
  631.9 39.0 %all-to-all-start = ((bf16[8,144,640]{2,1,0:T(8,128)(2,1)}), bf16[8,144,640]{2,1,0:T(8,128)(2,1)}, u32[]{:S(2)}, u32[]{:S(2)}) async-start(bf16[8,144,640]{2,1,0:T(8,128)(2,1)} %bitcast.260), calls=%async_computation.2 | async-start | bytes 2949120 | tf_op jit(solution)/shard_map/all_to_all | solution.py:184
  686.3 46.2 %collective-permute-start.74 = (f32[5120]{0:T(1024)S(1)}, f32[5120]{0:T(1024)S(1)}, u32[]{:S(2)}, u32[]{:S(2)}) collective-permute-start(f32[5120]{0:T(1024)S(1)} %add.732), channel_id=1, source_target_pairs={{0,4},{1,5},{2,6},{3,7},{4,0},{5,1},{6,2},{7,3},{8,12},{9,13},{10,... | collective-permute-start | bytes 61448 | tf_op jit(solution)/shard_map/ppermute | solution.py:154
  (227 other events, 2375.1 us)
Sparse Core Ops, SparseCore 0:
  20.4 141.5 all-gather.2
  164.2 75.2 all-gather.4
  338.0 85.8 reduce-scatter.2
  428.4 153.9 reduce-scatter.4

commit v5 on v4

--- a/solution.py
+++ b/solution.py
@@ -179,9 +179,10 @@
     return whole
 
 
-def direct_reduce(terms, nf):
+def direct_reduce(terms, nf, meanwhile):
     band, width = (terms.shape[0] // nf, terms.shape[1])
     spread = lax.all_to_all(terms.reshape(nf, band, width), "fsdp", split_axis=0, concat_axis=0)
+    spread = after(spread, meanwhile)
     return jnp.sum(spread.astype(F32), axis=0).astype(BF)
 
 
@@ -651,8 +652,6 @@
     qkv_sum, qkv_away = term_over_dp(after(normed, both_band), low_projected, qkv_per)
     attn_sum = jnp.concatenate([qkv_sum, out_sum], axis=1).astype(BF)
     ff_all = gather_columns([both_band, down_band])
-    attn_band = direct_reduce(after(attn_sum, both_band), nf)
-    attn_all = gather_relative([attn_band])
 
     def all_parts(mine, *ties):
         parts = mine + [swap_core(piece, nd) for piece in mine]
@@ -702,13 +701,15 @@
     late = tuple(table[:LATE] for table in places)
     root_of = relative(owners) * capacity + ranks
     root_args = (left_roots, right_roots, master)
-    fresh_arrays = update_blocks(
-        [ff_all], early, root_of[LATE:], *root_args, LATE, NBLK - LATE, 7, None
-    )
     slot_places = tuple(of_slot(table) for table in places)
     group = 3 if (capacity - LATE) % 3 == 0 else 1
     stat_args = (slot_places, used, stat_left[0], stat_right[0])
     fresh_stats = owner_stats([ff_all], *stat_args, LATE, capacity - LATE, group, None)
+    attn_band = direct_reduce(after(attn_sum, both_band), nf, fresh_stats[0])
+    attn_all = gather_relative([attn_band])
+    fresh_arrays = update_blocks(
+        [ff_all], early, root_of[LATE:], left_roots, right_roots, after(master, attn_band), LATE, NBLK - LATE, 7, None
+    )
     both = [ff_all, attn_all]
     new_master, new_weights = update_blocks(
         both, late, root_of[:LATE], *root_args, 0, LATE, 7, fresh_arrays

time: 772 us -> 767 us (level)
  waiting for transfers between devices: 226 us -> 234 us
    ppermute x16, waiting for transfers between devices: 134 us -> 146 us  [shift_x(): return lax.ppermute(value, 'dp', pairs)]
    dynamic_update_slice x8, local copies, waits for them, and re-layouts: 16.4 us -> 7.59 us  [gather_columns(): out = lax.dynamic_update_slice(out, piece[None, None], (place, 0, 0, at))]
    unnamed x343 -> x357, local copies, waits for them, and re-layouts: 23.1 us -> 25.8 us
  transfers between devices with their start and end apart: 86 -> 86, of which waited for: 33 -> 32; matrix products, arithmetic and copies ran while one was open for 39% -> 38% of each run, Pallas kernels for 6% -> 6%
where the time goes in v5:
time: 767 us; the launch traced here: 757 us
  waiting for transfers between devices  234 us (31%)
  matrix products  177 us (23%)
  starting transfers between devices  110 us (14%)
  local copies, waits for them, and re-layouts  84.5 us (11%)
  other arithmetic  71.7 us (9%)
  Pallas kernels  59.8 us (8%)
  between operations  19.9 us (3%)
    ppermute x16, waiting for transfers between devices, shift_x(): return lax.ppermute(value, 'dp', pairs)  146 us
    dot_general x8, matrix products, dot_nn(): return jnp.dot(left, right, preferred_element_type=F32)  66.1 us
    dot_general x15, matrix products, dot_nt(): lax.dot_general(left, right, (((1,), (1,)), ((), ())), preferred_element_...  55.4 us
    ppermute x14, starting transfers between devices, swap_fsdp(): return lax.ppermute(value, 'fsdp', [(e, e ^ flip) for e in range(nf)])  47 us
    dot_general x11, matrix products, dot_tn(): lax.dot_general(left, right, (((0,), (0,)), ((), ())), preferred_element_...  42.5 us
    pallas_call x2, Pallas kernels, update_blocks(): pl.pallas_call(lambda *refs: update_body(group, len(sources), len(left_ro...  37.8 us
    dynamic_update_slice x12, local copies, waits for them, and re-layouts, all_parts(): lax.dynamic_update_slice(out, piece[None], (place,) + (0,) * piece.ndim)  26 us
    unnamed x357, local copies, waits for them, and re-layouts  25.8 us
  transfers between devices with their start and end apart: 86, of which 32 were waited for; matrix products, arithmetic and copies ran while one was open for 38% of the time, Pallas kernels for 6%

profile of v5, /device:TPU:0, one launch (start us, length us, event | category | flops | bytes accessed | tf_op | source)
XLA Modules:
  0.0 757.3 jit_solution(12938884399307855206)
XLA Ops:
  35.0 15.3 %collective-permute-done.2 = bf16[144,768]{1,0:T(8,128)(2,1)S(1)} collective-permute-done((bf16[144,768]{1,0:T(8,128)(2,1)}, bf16[144,768]{1,0:T(8,128)(2,1)S(1)}, u32[]{:S(2)}, u32[]{:S(2)}) %collective-permute-start.2) | collective-permute-done | bytes 221216 | tf_op jit(solution)/shard_map/ppermute | solution.py:164
  88.7 23.4 %collective-permute-start.18 = (bf16[144,512]{1,0:T(8,128)(2,1)S(1)}, bf16[144,512]{1,0:T(8,128)(2,1)S(1)}, u32[]{:S(2)}, u32[]{:S(2)}) collective-permute-start(bf16[144,512]{1,0:T(8,128)(2,1)S(1)} %dynamic-slice_convert_fusion.4), channel_id=1, source_target_pairs={{0,6},{1,7},{2,4},{3,5},{4,2},{5,3},{6,0},{7,1},{8,14},{9,15},{10,... | collective-permute-start | bytes 442376 | tf_op jit(solution)/shard_map/ppermute | solution.py:164
  117.3 8.2 %collective-permute-start.26 = (bf16[256,512]{1,0:T(8,128)(2,1)S(1)}, bf16[256,512]{1,0:T(8,128)(2,1)S(1)}, u32[]{:S(2)}, u32[]{:S(2)}) collective-permute-start(bf16[256,512]{1,0:T(8,128)(2,1)S(1)} %get-tuple-element.253), channel_id=1, source_target_pairs={{0,1},{1,2},{2,3},{8,9},{9,10},{10,11},{16,17},{17,18},{18,19},{24... | collective-permute-start | bytes 786440 | tf_op jit(solution)/shard_map/ppermute | solution.py:384
  155.5 14.2 %collective-permute-done.21 = bf16[256,1152]{1,0:T(8,128)(2,1)S(1)} collective-permute-done((bf16[256,1152]{1,0:T(8,128)(2,1)}, bf16[256,1152]{1,0:T(8,128)(2,1)S(1)}, u32[]{:S(2)}, u32[]{:S(2)}) %collective-permute-start.21) | collective-permute-done | bytes 589856 | tf_op jit(solution)/shard_map/ppermute | solution.py:115
  175.6 14.3 %collective-permute-done.29 = bf16[256,1152]{1,0:T(8,128)(2,1)S(1)} collective-permute-done((bf16[256,1152]{1,0:T(8,128)(2,1)S(1)}, bf16[256,1152]{1,0:T(8,128)(2,1)S(1)}, u32[]{:S(2)}, u32[]{:S(2)}) %collective-permute-start.29) | collective-permute-done | bytes 589856 | tf_op jit(solution)/shard_map/ppermute | solution.py:115
  201.9 11.6 %multiply_convert_fusion.3 = (bf16[1024,1792]{1,0:T(8,128)(2,1)}, f32[1024,1792]{1,0:T(8,128)}) fusion(f32[1024,1792]{1,0:T(8,128)S(1)} %fusion.64, bf16[1152,3584]{1,0:T(8,128)(2,1)S(1)} %copy-done.152, bf16[256,1152]{1,0:T(8,128)(2,1)S(1)} %copy-done.85, bf16[256,1152]{1,0:T(8,128)(2,1)S(1)} %collective-permute-done.22, ...), kind=kOutput, calls=%fused_computation.36 | convolution fusion | flops 4255645696 | bytes 24838144 | tf_op jit(solution)/shard_map/dot_general | solution.py:97
  218.4 8.5 %multiply_convert_fusion.2 = (bf16[1024,1792]{1,0:T(8,128)(2,1)}, f32[1024,1792]{1,0:T(8,128)}) fusion(f32[1024,1792]{1,0:T(8,128)S(1)} %fusion.62, bf16[1024,1152]{1,0:T(8,128)(2,1)S(1)} %copy-done.74, bf16[1152,3584]{1,0:T(8,128)(2,1)S(1)} %copy-done.152), kind=kOutput, calls=%fused_computation.35 | convolution fusion | flops 4246208512 | bytes 24838144 | tf_op jit(solution)/shard_map/dot_general | solution.py:97
  226.9 12.6 %all-gather.5.cloned.1.call-done = bf16[1152,1792]{1,0:T(8,128)(2,1)} async-done(((bf16[144,1792]{1,0:T(8,128)(2,1)}), bf16[1152,1792]{1,0:T(8,128)(2,1)}) %all-gather.5.cloned.1.call-update) | async-done | bytes 4128784 | tf_op jit(solution)/shard_map/all_gather | solution.py:498
  260.1 9.5 %collective-permute-done.33 = bf16[256,1152]{1,0:T(8,128)(2,1)S(1)} collective-permute-done((bf16[256,1152]{1,0:T(8,128)(2,1)S(1)}, bf16[256,1152]{1,0:T(8,128)(2,1)S(1)}, u32[]{:S(2)}, u32[]{:S(2)}) %collective-permute-start.33) | collective-permute-done | bytes 589856 | tf_op jit(solution)/shard_map/ppermute | solution.py:115
  269.9 11.8 %collective-permute-done.35 = bf16[256,1152]{1,0:T(8,128)(2,1)S(1)} collective-permute-done((bf16[256,1152]{1,0:T(8,128)(2,1)S(1)}, bf16[256,1152]{1,0:T(8,128)(2,1)S(1)}, u32[]{:S(2)}, u32[]{:S(2)}) %collective-permute-start.35) | collective-permute-done | bytes 589856 | tf_op jit(solution)/shard_map/ppermute | solution.py:115
  289.3 10.7 %collective-permute-done.36 = bf16[256,1152]{1,0:T(8,128)(2,1)S(1)} collective-permute-done((bf16[256,1152]{1,0:T(8,128)(2,1)S(1)}, bf16[256,1152]{1,0:T(8,128)(2,1)S(1)}, u32[]{:S(2)}, u32[]{:S(2)}) %collective-permute-start.36) | collective-permute-done | bytes 589856 | tf_op jit(solution)/shard_map/ppermute | solution.py:115
  304.4 13.6 %fusion.8 = (bf16[1024,1792]{1,0:T(8,128)(2,1)}, bf16[1024,1792]{1,0:T(8,128)(2,1)}) fusion(f32[1024,1792]{1,0:T(8,128)} %copy-done.163, f32[1024,1792]{1,0:T(8,128)} %get-tuple-element.279, bf16[1024,1152]{1,0:T(8,128)(2,1)S(1)} %pad_maximum_fusion.3, bf16[1152,1792]{1,0:T(8,128)(2,1)S(1)} %copy-done.153), kind=kOutput, calls=%fused_computation.16 | convolution fusion | flops 4271898624 | bytes 28508160 | tf_op jit(solution)/shard_map/dot_general | solution.py:97
  327.2 10.7 %convolution_convert_fusion.2 = bf16[1152,1792]{1,0:T(8,128)(2,1)} fusion(bf16[2048,1152]{1,0:T(8,128)(2,1)S(1)} %constant_dynamic-update-slice_fusion.8, bf16[1024,1792]{1,0:T(8,128)(2,1)S(1)} %copy-done.83, bf16[1024,1792]{1,0:T(8,128)(2,1)S(1)} %copy-done.82), kind=kOutput, calls=%fused_computation.9 | convolution fusion | flops 8472461312 | bytes 16187392 | tf_op jit(solution)/shard_map/dot_general | solution.py:105
  339.9 14.2 %fusion.15 = (bf16[1024,1792]{1,0:T(8,128)(2,1)}, bf16[1024,1792]{1,0:T(8,128)(2,1)S(1)}) fusion(f32[1024,1792]{1,0:T(8,128)} %copy-done.162, f32[1024,1792]{1,0:T(8,128)} %get-tuple-element.281, bf16[1024,1152]{1,0:T(8,128)(2,1)S(1)} %pad_maximum_fusion.4, bf16[1152,1792]{1,0:T(8,128)(2,1)} %all-gather.5.cloned.1.call-done), kind=kOutput, calls=%fused_computation.23 | convolution fusion | flops 4271898624 | bytes 28508160 | tf_op jit(solution)/shard_map/dot_general | solution.py:97
  355.4 12.8 %convolution_convert_fusion.1 = bf16[1152,1792]{1,0:T(8,128)(2,1)} fusion(bf16[2048,1152]{1,0:T(8,128)(2,1)S(1)} %bitcast.302, bf16[1024,1792]{1,0:T(8,128)(2,1)} %get-tuple-element.79, bf16[1024,1792]{1,0:T(8,128)(2,1)S(1)} %copy-done.158), kind=kOutput, calls=%fused_computation.8 | convolution fusion | flops 8472461312 | bytes 16187392 | tf_op jit(solution)/shard_map/dot_general | solution.py:105
  368.1 11.0 %convolution_convert_fusion = bf16[1152,1792]{1,0:T(8,128)(2,1)} fusion(bf16[2048,1152]{1,0:T(8,128)(2,1)S(1)} %bitcast.302, bf16[1024,1792]{1,0:T(8,128)(2,1)S(1)} %get-tuple-element.227, bf16[1024,1792]{1,0:T(8,128)(2,1)S(1)} %copy-done.156), kind=kOutput, calls=%fused_computation.7 | convolution fusion | flops 8472461312 | bytes 16187392 | tf_op jit(solution)/shard_map/dot_general | solution.py:105
  427.8 11.8 %collective-permute-done.46 = bf16[256,1152]{1,0:T(8,128)(2,1)} collective-permute-done((bf16[256,1152]{1,0:T(8,128)(2,1)}, bf16[256,1152]{1,0:T(8,128)(2,1)}, u32[]{:S(2)}, u32[]{:S(2)}) %collective-permute-start.46) | collective-permute-done | bytes 589856 | tf_op jit(solution)/shard_map/ppermute | solution.py:115
  439.6 11.8 %collective-permute-done.44 = bf16[256,1152]{1,0:T(8,128)(2,1)} collective-permute-done((bf16[256,1152]{1,0:T(8,128)(2,1)}, bf16[256,1152]{1,0:T(8,128)(2,1)}, u32[]{:S(2)}, u32[]{:S(2)}) %collective-permute-start.44) | collective-permute-done | bytes 589856 | tf_op jit(solution)/shard_map/ppermute | solution.py:115
  538.9 10.0 %collective-permute-done.56 = bf16[57,16,144]{2,1,0:T(8,128)(2,1)} collective-permute-done((bf16[57,16,144]{2,1,0:T(8,128)(2,1)S(1)}, bf16[57,16,144]{2,1,0:T(8,128)(2,1)}, u32[]{:S(2)}, u32[]{:S(2)}) %collective-permute-start.56) | collective-permute-done | bytes 262688 | tf_op jit(solution)/shard_map/ppermute | solution.py:115
  565.0 16.6 %reduce-scatter.5.cloned.1.call-done = bf16[144,3584]{1,0:T(8,128)(2,1)} async-done(((bf16[1152,3584]{1,0:T(8,128)(2,1)}), bf16[144,3584]{1,0:T(8,128)(2,1)}) %reduce-scatter.5.cloned.1.call-update) | async-done | bytes 1032208 | tf_op jit(solution)/shard_map/reduce_scatter | solution.py:564
  608.1 11.6 %collective-permute-done.57 = bf16[144,3584]{1,0:T(8,128)(2,1)} collective-permute-done((bf16[144,3584]{1,0:T(8,128)(2,1)S(1)}, bf16[144,3584]{1,0:T(8,128)(2,1)}, u32[]{:S(2)}, u32[]{:S(2)}) %collective-permute-start.57) | collective-permute-done | bytes 1032224 | tf_op jit(solution)/shard_map/ppermute | solution.py:115
  623.8 20.1 %collective-permute-done.64 = bf16[1152,384]{1,0:T(8,128)(2,1)S(1)} collective-permute-done((bf16[1152,384]{1,0:T(8,128)(2,1)S(1)}, bf16[1152,384]{1,0:T(8,128)(2,1)S(1)}, u32[]{:S(2)}, u32[]{:S(2)}) %collective-permute-start.64) | collective-permute-done | bytes 884768 | tf_op jit(solution)/shard_map/ppermute | solution.py:115
  666.2 11.7 %owner_stats.2 = (f32[57,144,128]{2,1,0:T(8,128)}, f32[57,144,144]{2,1,0:T(8,128)}, f32[57,128,128]{2,1,0:T(8,128)}) custom-call(s32[57]{0:T(128)S(1)} %get-tuple-element.197.refs_0_, s32[57]{0:T(128)S(1)} %broadcast.987.refs_1_, s32[57]{0:T(128)S(1)} %get-tuple-element.196.refs_2_, s32[57]{0:T(128)S(1)} %get-tuple-element.195.refs_3_, ...), custom_call_target="tpu_custom_call" | custom-call | tf_op jit(solution)/shard_map/owner_stats/pallas_call | solution.py:334
  702.8 31.0 %update_blocks.2 = (f32[144,23296]{1,0:T(8,128)}, bf16[144,23296]{1,0:T(8,128)(2,1)}) custom-call(s32[161]{0:T(256)S(1)} %slice.310.refs_0_, s32[161]{0:T(256)S(1)} %broadcast.985.refs_1_, s32[161]{0:T(256)S(1)} %copy-done.5, s32[161]{0:T(256)S(1)} %slice.313.refs_3_, s32[161]{0:T(256)S(1)} %slice.314.refs_4_, bf16[4,1,144,5376]{3,2,1,0:T(8,128)(2,1)S(1)} %bitcast.222, ...), custom_call_target="tpu_custom_call" | custom-call | tf_op jit(solution)/shard_map/update_blocks/pallas_call | solution.py:288
  (764 shorter events, 410.4 us)
Async XLA Ops:
  7.2 187.1 %all-gather.3.cloned.1.call-start = ((), (), s32[]{:S(2)}) async-start(), calls=%async_computation.3 | async-start | bytes 9289728 | tf_op jit(solution)/shard_map/all_gather | solution.py:496
  20.3 219.2 %all-gather.5.cloned.1.call-start = ((), (), s32[]{:S(2)}) async-start(), calls=%async_computation.4 | async-start | bytes 4644864 | tf_op jit(solution)/shard_map/all_gather | solution.py:498
  60.4 28.3 %collective-permute-start.14 = (bf16[144,512]{1,0:T(8,128)(2,1)S(1)}, bf16[144,512]{1,0:T(8,128)(2,1)S(1)}, u32[]{:S(2)}, u32[]{:S(2)}) collective-permute-start(bf16[144,512]{1,0:T(8,128)(2,1)S(1)} %dynamic-slice_convert_fusion.4), channel_id=1, source_target_pairs={{0,2},{1,3},{2,0},{3,1},{4,6},{5,7},{6,4},{7,5},{8,10},{9,11},{10,... | collective-permute-start | bytes 442376 | tf_op jit(solution)/shard_map/ppermute | solution.py:164
  62.1 55.2 %collective-permute-start.10 = (bf16[256,512]{1,0:T(8,128)(2,1)S(1)}, bf16[256,512]{1,0:T(8,128)(2,1)}, u32[]{:S(2)}, u32[]{:S(2)}) collective-permute-start(bf16[256,512]{1,0:T(8,128)(2,1)S(1)} %get-tuple-element.252), channel_id=1, source_target_pairs={{0,1},{1,2},{2,3},{8,9},{9,10},{10,11},{16,17},{17,18},{18,19},{24... | collective-permute-start | bytes 786440 | tf_op jit(solution)/shard_map/ppermute | solution.py:384
  78.1 47.4 %collective-permute-start.11 = (bf16[256,512]{1,0:T(8,128)(2,1)}, bf16[256,512]{1,0:T(8,128)(2,1)S(1)}, u32[]{:S(2)}, u32[]{:S(2)}) collective-permute-start(bf16[256,512]{1,0:T(8,128)(2,1)} %collective-permute-done.8), channel_id=1, source_target_pairs={{4,5},{5,4},{12,13},{13,12},{20,21},{21,20},{28,29},{29,28}} | collective-permute-start | bytes 786440 | tf_op jit(solution)/shard_map/ppermute | solution.py:386
  86.2 26.8 %collective-permute-start.25 = (bf16[256,512]{1,0:T(8,128)(2,1)}, bf16[256,512]{1,0:T(8,128)(2,1)S(1)}, u32[]{:S(2)}, u32[]{:S(2)}) collective-permute-start(bf16[256,512]{1,0:T(8,128)(2,1)} %collective-permute-done.24), channel_id=1, source_target_pairs={{4,6},{5,7},{12,14},{13,15},{20,22},{21,23},{28,30},{29,31}} | collective-permute-start | bytes 786440 | tf_op jit(solution)/shard_map/ppermute | solution.py:385
  86.9 39.3 %collective-permute-start.12 = (bf16[256,512]{1,0:T(8,128)(2,1)S(1)}, bf16[256,512]{1,0:T(8,128)(2,1)S(1)}, u32[]{:S(2)}, u32[]{:S(2)}) collective-permute-start(bf16[256,512]{1,0:T(8,128)(2,1)S(1)} %collective-permute-done.9), channel_id=1, source_target_pairs={{6,7},{7,6},{14,15},{15,14},{22,23},{23,22},{30,31},{31,30}} | collective-permute-start | bytes 786440 | tf_op jit(solution)/shard_map/ppermute | solution.py:387
  88.7 39.8 %collective-permute-start.18 = (bf16[144,512]{1,0:T(8,128)(2,1)S(1)}, bf16[144,512]{1,0:T(8,128)(2,1)S(1)}, u32[]{:S(2)}, u32[]{:S(2)}) collective-permute-start(bf16[144,512]{1,0:T(8,128)(2,1)S(1)} %dynamic-slice_convert_fusion.4), channel_id=1, source_target_pairs={{0,6},{1,7},{2,4},{3,5},{4,2},{5,3},{6,0},{7,1},{8,14},{9,15},{10,... | collective-permute-start | bytes 442376 | tf_op jit(solution)/shard_map/ppermute | solution.py:164
  155.3 329.4 %reduce-scatter.3.cloned.1.call-start = ((), (), s32[]{:S(2)}) async-start(), calls=%async_computation.5 | async-start | bytes 4644864 | tf_op jit(solution)/shard_map/reduce_scatter | solution.py:564
  337.9 243.7 %reduce-scatter.5.cloned.1.call-start = ((), (), s32[]{:S(2)}) async-start(), calls=%async_computation.6 | async-start | bytes 9289728 | tf_op jit(solution)/shard_map/reduce_scatter | solution.py:564
  354.2 43.2 %collective-permute-start.42 = (bf16[57,128,128]{2,1,0:T(8,128)(2,1)}, bf16[57,128,128]{2,1,0:T(8,128)(2,1)}, u32[]{:S(2)}, u32[]{:S(2)}) collective-permute-start(bf16[57,128,128]{2,1,0:T(8,128)(2,1)} %bitcast.20), channel_id=1, source_target_pairs={{0,16},{8,24},{16,0},{24,8},{1,17},{9,25},{17,1},{25,9},{2,18},{10... | collective-permute-start | bytes 5603336 | tf_op jit(solution)/shard_map/ppermute | solution.py:115
  475.1 60.6 %collective-permute-start.55 = (bf16[57,144,128]{2,1,0:T(8,128)(2,1)S(1)}, bf16[57,144,128]{2,1,0:T(8,128)(2,1)}, u32[]{:S(2)}, u32[]{:S(2)}) collective-permute-start(bf16[57,144,128]{2,1,0:T(8,128)(2,1)S(1)} %get-tuple-element.95), channel_id=1, source_target_pairs={{0,16},{8,24},{16,0},{24,8},{1,17},{9,25},{17,1},{25,9},{2,18},{10... | collective-permute-start | bytes 6303752 | tf_op jit(solution)/shard_map/ppermute | solution.py:115
  499.2 28.5 %collective-permute-start.47 = (bf16[256,512]{1,0:T(8,128)(2,1)}, bf16[256,512]{1,0:T(8,128)(2,1)}, u32[]{:S(2)}, u32[]{:S(2)}) collective-permute-start(bf16[256,512]{1,0:T(8,128)(2,1)} %fusion.106), channel_id=1, source_target_pairs={{1,0},{2,1},{3,2},{9,8},{10,9},{11,10},{17,16},{18,17},{19,18},{25... | collective-permute-start | bytes 786440 | tf_op jit(solution)/shard_map/ppermute | solution.py:398
  527.7 74.6 %collective-permute-start.79 = (bf16[57,128,128]{2,1,0:T(8,128)(2,1)}, bf16[57,128,128]{2,1,0:T(8,128)(2,1)}, u32[]{:S(2)}, u32[]{:S(2)}) collective-permute-start(bf16[57,128,128]{2,1,0:T(8,128)(2,1)} %bitcast.20), channel_id=1, source_target_pairs={{0,8},{8,0},{16,24},{24,16},{1,9},{9,1},{17,25},{25,17},{2,10},{10... | collective-permute-start | bytes 5603336 | tf_op jit(solution)/shard_map/ppermute | solution.py:109
  534.3 154.1 %collective-permute-start.80 = (bf16[57,128,128]{2,1,0:T(8,128)(2,1)}, bf16[57,128,128]{2,1,0:T(8,128)(2,1)}, u32[]{:S(2)}, u32[]{:S(2)}) collective-permute-start(bf16[57,128,128]{2,1,0:T(8,128)(2,1)} %collective-permute-done.42), channel_id=1, source_target_pairs={{0,8},{8,0},{16,24},{24,16},{1,9},{9,1},{17,25},{25,17},{2,10},{10... | collective-permute-start | bytes 5603336 | tf_op jit(solution)/shard_map/ppermute | solution.py:109
  537.2 65.6 %collective-permute-start.75 = (bf16[57,144,128]{2,1,0:T(8,128)(2,1)S(1)}, bf16[57,144,128]{2,1,0:T(8,128)(2,1)}, u32[]{:S(2)}, u32[]{:S(2)}) collective-permute-start(bf16[57,144,128]{2,1,0:T(8,128)(2,1)S(1)} %get-tuple-element.95), channel_id=1, source_target_pairs={{0,8},{8,0},{16,24},{24,16},{1,9},{9,1},{17,25},{25,17},{2,10},{10... | collective-permute-start | bytes 6303752 | tf_op jit(solution)/shard_map/ppermute | solution.py:109
  537.4 64.9 %collective-permute-start.76 = (bf16[57,144,128]{2,1,0:T(8,128)(2,1)}, bf16[57,144,128]{2,1,0:T(8,128)(2,1)}, u32[]{:S(2)}, u32[]{:S(2)}) collective-permute-start(bf16[57,144,128]{2,1,0:T(8,128)(2,1)} %collective-permute-done.55), channel_id=1, source_target_pairs={{0,8},{8,0},{16,24},{24,16},{1,9},{9,1},{17,25},{25,17},{2,10},{10... | collective-permute-start | bytes 6303752 | tf_op jit(solution)/shard_map/ppermute | solution.py:109
  602.3 92.5 %collective-permute-start.77 = (bf16[57,16,144]{2,1,0:T(8,128)(2,1)S(1)}, bf16[57,16,144]{2,1,0:T(8,128)(2,1)}, u32[]{:S(2)}, u32[]{:S(2)}) collective-permute-start(bf16[57,16,144]{2,1,0:T(8,128)(2,1)S(1)} %get-tuple-element.99), channel_id=1, source_target_pairs={{0,8},{8,0},{16,24},{24,16},{1,9},{9,1},{17,25},{25,17},{2,10},{10... | collective-permute-start | bytes 787976 | tf_op jit(solution)/shard_map/ppermute | solution.py:109
  602.3 94.9 %collective-permute-start.78 = (bf16[57,16,144]{2,1,0:T(8,128)(2,1)}, bf16[57,16,144]{2,1,0:T(8,128)(2,1)}, u32[]{:S(2)}, u32[]{:S(2)}) collective-permute-start(bf16[57,16,144]{2,1,0:T(8,128)(2,1)} %collective-permute-done.56), channel_id=1, source_target_pairs={{0,8},{8,0},{16,24},{24,16},{1,9},{9,1},{17,25},{25,17},{2,10},{10... | collective-permute-start | bytes 787976 | tf_op jit(solution)/shard_map/ppermute | solution.py:109
  620.9 36.1 %collective-permute-start.59 = (bf16[144,3584]{1,0:T(8,128)(2,1)}, bf16[144,3584]{1,0:T(8,128)(2,1)S(1)}, u32[]{:S(2)}, u32[]{:S(2)}) collective-permute-start(bf16[144,3584]{1,0:T(8,128)(2,1)} %collective-permute-done.57), channel_id=1, source_target_pairs={{0,8},{8,0},{16,24},{24,16},{1,9},{9,1},{17,25},{25,17},{2,10},{10... | collective-permute-start | bytes 3096584 | tf_op jit(solution)/shard_map/ppermute | solution.py:109
  647.0 38.0 %all-to-all-start = ((bf16[8,144,640]{2,1,0:T(8,128)(2,1)}), bf16[8,144,640]{2,1,0:T(8,128)(2,1)S(1)}, u32[]{:S(2)}, u32[]{:S(2)}) async-start(bf16[8,144,640]{2,1,0:T(8,128)(2,1)} %bitcast.41), calls=%async_computation.2 | async-start | bytes 2949120 | tf_op jit(solution)/shard_map/all_to_all | solution.py:184
  700.0 33.8 %collective-permute-start.74 = (f32[5120]{0:T(1024)S(1)}, f32[5120]{0:T(1024)S(1)}, u32[]{:S(2)}, u32[]{:S(2)}) collective-permute-start(f32[5120]{0:T(1024)S(1)} %add.732), channel_id=1, source_target_pairs={{0,4},{1,5},{2,6},{3,7},{4,0},{5,1},{6,2},{7,3},{8,12},{9,13},{10,... | collective-permute-start | bytes 61448 | tf_op jit(solution)/shard_map/ppermute | solution.py:154
  701.1 33.6 %collective-permute-start.68 = (bf16[144,640]{1,0:T(8,128)(2,1)S(1)}, bf16[144,640]{1,0:T(8,128)(2,1)S(1)}, u32[]{:S(2)}, u32[]{:S(2)}) collective-permute-start(bf16[144,640]{1,0:T(8,128)(2,1)S(1)} %reduce_sum.428), channel_id=1, source_target_pairs={{0,8},{8,0},{16,24},{24,16},{1,9},{9,1},{17,25},{25,17},{2,10},{10... | collective-permute-start | bytes 552968 | tf_op jit(solution)/shard_map/ppermute | solution.py:109
  701.1 33.3 %collective-permute-start.67 = (bf16[144,640]{1,0:T(8,128)(2,1)S(1)}, bf16[144,640]{1,0:T(8,128)(2,1)S(1)}, u32[]{:S(2)}, u32[]{:S(2)}) collective-permute-start(bf16[144,640]{1,0:T(8,128)(2,1)S(1)} %reduce_sum.428), channel_id=1, source_target_pairs={{0,16},{8,24},{16,0},{24,8},{1,17},{9,25},{17,1},{25,9},{2,18},{10... | collective-permute-start | bytes 552968 | tf_op jit(solution)/shard_map/ppermute | solution.py:115
  (234 other events, 2404.2 us)
Sparse Core Ops, SparseCore 0:
  20.4 141.5 all-gather.2
  164.2 75.2 all-gather.4
  338.0 85.7 reduce-scatter.2
  428.5 153.1 reduce-scatter.4

commit v6 on v5

--- a/solution.py
+++ b/solution.py
@@ -651,7 +651,7 @@
 
     qkv_sum, qkv_away = term_over_dp(after(normed, both_band), low_projected, qkv_per)
     attn_sum = jnp.concatenate([qkv_sum, out_sum], axis=1).astype(BF)
-    ff_all = gather_columns([both_band, down_band])
+    ff_all = gather_columns([after(both_band, qkv_sum), down_band])
 
     def all_parts(mine, *ties):
         parts = mine + [swap_core(piece, nd) for piece in mine]

time: 767 us -> 752 us (0.980)
  waiting for transfers between devices: 234 us -> 216 us
    ppermute x16, waiting for transfers between devices: 146 us -> 133 us  [shift_x(): return lax.ppermute(value, 'dp', pairs)]
  transfers between devices with their start and end apart: 86 -> 86, of which waited for: 32 -> 33; matrix products, arithmetic and copies ran while one was open for 38% -> 38% of each run, Pallas kernels for 6% -> 6%
where the time goes in v6:
time: 752 us; the launch traced here: 743 us
  waiting for transfers between devices  216 us (29%)
  matrix products  178 us (24%)
  starting transfers between devices  112 us (15%)
  local copies, waits for them, and re-layouts  86 us (11%)
  other arithmetic  71.8 us (10%)
  Pallas kernels  59.7 us (8%)
  between operations  20 us (3%)
    ppermute x16, waiting for transfers between devices, shift_x(): return lax.ppermute(value, 'dp', pairs)  133 us
    dot_general x8, matrix products, dot_nn(): return jnp.dot(left, right, preferred_element_type=F32)  66.1 us
    dot_general x15, matrix products, dot_nt(): lax.dot_general(left, right, (((1,), (1,)), ((), ())), preferred_element_...  55.9 us
    ppermute x14, starting transfers between devices, swap_fsdp(): return lax.ppermute(value, 'fsdp', [(e, e ^ flip) for e in range(nf)])  47 us
    dot_general x11, matrix products, dot_tn(): lax.dot_general(left, right, (((0,), (0,)), ((), ())), preferred_element_...  42.3 us
    pallas_call x2, Pallas kernels, update_blocks(): pl.pallas_call(lambda *refs: update_body(group, len(sources), len(left_ro...  37.8 us
    dynamic_update_slice x12, local copies, waits for them, and re-layouts, all_parts(): lax.dynamic_update_slice(out, piece[None], (place,) + (0,) * piece.ndim)  29.2 us
    unnamed x357, local copies, waits for them, and re-layouts  28.3 us
  transfers between devices with their start and end apart: 86, of which 33 were waited for; matrix products, arithmetic and copies ran while one was open for 38% of the time, Pallas kernels for 6%

profile of v6, /device:TPU:0, one launch (start us, length us, event | category | flops | bytes accessed | tf_op | source)
XLA Modules:
  0.0 742.8 jit_solution(843962942480284334)
XLA Ops:
  35.0 15.3 %collective-permute-done.2 = bf16[144,768]{1,0:T(8,128)(2,1)S(1)} collective-permute-done((bf16[144,768]{1,0:T(8,128)(2,1)}, bf16[144,768]{1,0:T(8,128)(2,1)S(1)}, u32[]{:S(2)}, u32[]{:S(2)}) %collective-permute-start.2) | collective-permute-done | bytes 221216 | tf_op jit(solution)/shard_map/ppermute | solution.py:164
  88.7 23.4 %collective-permute-start.18 = (bf16[144,512]{1,0:T(8,128)(2,1)S(1)}, bf16[144,512]{1,0:T(8,128)(2,1)S(1)}, u32[]{:S(2)}, u32[]{:S(2)}) collective-permute-start(bf16[144,512]{1,0:T(8,128)(2,1)S(1)} %dynamic-slice_convert_fusion.4), channel_id=1, source_target_pairs={{0,6},{1,7},{2,4},{3,5},{4,2},{5,3},{6,0},{7,1},{8,14},{9,15},{10,... | collective-permute-start | bytes 442376 | tf_op jit(solution)/shard_map/ppermute | solution.py:164
  117.3 8.2 %collective-permute-start.26 = (bf16[256,512]{1,0:T(8,128)(2,1)S(1)}, bf16[256,512]{1,0:T(8,128)(2,1)S(1)}, u32[]{:S(2)}, u32[]{:S(2)}) collective-permute-start(bf16[256,512]{1,0:T(8,128)(2,1)S(1)} %get-tuple-element.255), channel_id=1, source_target_pairs={{0,1},{1,2},{2,3},{8,9},{9,10},{10,11},{16,17},{17,18},{18,19},{24... | collective-permute-start | bytes 786440 | tf_op jit(solution)/shard_map/ppermute | solution.py:384
  155.5 14.2 %collective-permute-done.21 = bf16[256,1152]{1,0:T(8,128)(2,1)S(1)} collective-permute-done((bf16[256,1152]{1,0:T(8,128)(2,1)}, bf16[256,1152]{1,0:T(8,128)(2,1)S(1)}, u32[]{:S(2)}, u32[]{:S(2)}) %collective-permute-start.21) | collective-permute-done | bytes 589856 | tf_op jit(solution)/shard_map/ppermute | solution.py:115
  175.6 14.3 %collective-permute-done.29 = bf16[256,1152]{1,0:T(8,128)(2,1)S(1)} collective-permute-done((bf16[256,1152]{1,0:T(8,128)(2,1)S(1)}, bf16[256,1152]{1,0:T(8,128)(2,1)S(1)}, u32[]{:S(2)}, u32[]{:S(2)}) %collective-permute-start.29) | collective-permute-done | bytes 589856 | tf_op jit(solution)/shard_map/ppermute | solution.py:115
  201.9 11.6 %multiply_convert_fusion.3 = (bf16[1024,1792]{1,0:T(8,128)(2,1)}, f32[1024,1792]{1,0:T(8,128)}) fusion(f32[1024,1792]{1,0:T(8,128)S(1)} %fusion.63, bf16[1152,3584]{1,0:T(8,128)(2,1)S(1)} %copy-done.152, bf16[256,1152]{1,0:T(8,128)(2,1)S(1)} %copy-done.85, bf16[256,1152]{1,0:T(8,128)(2,1)S(1)} %collective-permute-done.22, ...), kind=kOutput, calls=%fused_computation.36 | convolution fusion | flops 4255645696 | bytes 24838144 | tf_op jit(solution)/shard_map/dot_general | solution.py:97
  218.4 8.5 %multiply_convert_fusion.2 = (bf16[1024,1792]{1,0:T(8,128)(2,1)}, f32[1024,1792]{1,0:T(8,128)}) fusion(f32[1024,1792]{1,0:T(8,128)S(1)} %fusion.61, bf16[1024,1152]{1,0:T(8,128)(2,1)S(1)} %copy-done.74, bf16[1152,3584]{1,0:T(8,128)(2,1)S(1)} %copy-done.152), kind=kOutput, calls=%fused_computation.35 | convolution fusion | flops 4246208512 | bytes 24838144 | tf_op jit(solution)/shard_map/dot_general | solution.py:97
  226.9 12.6 %all-gather.5.cloned.1.call-done = bf16[1152,1792]{1,0:T(8,128)(2,1)} async-done(((bf16[144,1792]{1,0:T(8,128)(2,1)}), bf16[1152,1792]{1,0:T(8,128)(2,1)}) %all-gather.5.cloned.1.call-update) | async-done | bytes 4128784 | tf_op jit(solution)/shard_map/all_gather | solution.py:498
  260.1 9.5 %collective-permute-done.33 = bf16[256,1152]{1,0:T(8,128)(2,1)S(1)} collective-permute-done((bf16[256,1152]{1,0:T(8,128)(2,1)S(1)}, bf16[256,1152]{1,0:T(8,128)(2,1)S(1)}, u32[]{:S(2)}, u32[]{:S(2)}) %collective-permute-start.33) | collective-permute-done | bytes 589856 | tf_op jit(solution)/shard_map/ppermute | solution.py:115
  269.9 11.8 %collective-permute-done.35 = bf16[256,1152]{1,0:T(8,128)(2,1)S(1)} collective-permute-done((bf16[256,1152]{1,0:T(8,128)(2,1)S(1)}, bf16[256,1152]{1,0:T(8,128)(2,1)S(1)}, u32[]{:S(2)}, u32[]{:S(2)}) %collective-permute-start.35) | collective-permute-done | bytes 589856 | tf_op jit(solution)/shard_map/ppermute | solution.py:115
  289.3 10.7 %collective-permute-done.36 = bf16[256,1152]{1,0:T(8,128)(2,1)S(1)} collective-permute-done((bf16[256,1152]{1,0:T(8,128)(2,1)S(1)}, bf16[256,1152]{1,0:T(8,128)(2,1)S(1)}, u32[]{:S(2)}, u32[]{:S(2)}) %collective-permute-start.36) | collective-permute-done | bytes 589856 | tf_op jit(solution)/shard_map/ppermute | solution.py:115
  304.4 13.6 %fusion.8 = (bf16[1024,1792]{1,0:T(8,128)(2,1)}, bf16[1024,1792]{1,0:T(8,128)(2,1)}) fusion(f32[1024,1792]{1,0:T(8,128)} %copy-done.163, f32[1024,1792]{1,0:T(8,128)} %get-tuple-element.281, bf16[1024,1152]{1,0:T(8,128)(2,1)S(1)} %pad_maximum_fusion.3, bf16[1152,1792]{1,0:T(8,128)(2,1)S(1)} %copy-done.153), kind=kOutput, calls=%fused_computation.16 | convolution fusion | flops 4271898624 | bytes 28508160 | tf_op jit(solution)/shard_map/dot_general | solution.py:97
  327.2 10.7 %convolution_convert_fusion.2 = bf16[1152,1792]{1,0:T(8,128)(2,1)} fusion(bf16[2048,1152]{1,0:T(8,128)(2,1)S(1)} %constant_dynamic-update-slice_fusion.8, bf16[1024,1792]{1,0:T(8,128)(2,1)S(1)} %copy-done.83, bf16[1024,1792]{1,0:T(8,128)(2,1)S(1)} %copy-done.82), kind=kOutput, calls=%fused_computation.9 | convolution fusion | flops 8472461312 | bytes 16187392 | tf_op jit(solution)/shard_map/dot_general | solution.py:105
  339.9 14.2 %fusion.15 = (bf16[1024,1792]{1,0:T(8,128)(2,1)}, bf16[1024,1792]{1,0:T(8,128)(2,1)S(1)}) fusion(f32[1024,1792]{1,0:T(8,128)} %copy-done.162, f32[1024,1792]{1,0:T(8,128)} %get-tuple-element.283, bf16[1024,1152]{1,0:T(8,128)(2,1)S(1)} %pad_maximum_fusion.4, bf16[1152,1792]{1,0:T(8,128)(2,1)} %all-gather.5.cloned.1.call-done), kind=kOutput, calls=%fused_computation.23 | convolution fusion | flops 4271898624 | bytes 28508160 | tf_op jit(solution)/shard_map/dot_general | solution.py:97
  355.4 12.8 %convolution_convert_fusion.1 = bf16[1152,1792]{1,0:T(8,128)(2,1)} fusion(bf16[2048,1152]{1,0:T(8,128)(2,1)S(1)} %bitcast.287, bf16[1024,1792]{1,0:T(8,128)(2,1)} %get-tuple-element.80, bf16[1024,1792]{1,0:T(8,128)(2,1)S(1)} %copy-done.158), kind=kOutput, calls=%fused_computation.8 | convolution fusion | flops 8472461312 | bytes 16187392 | tf_op jit(solution)/shard_map/dot_general | solution.py:105
  368.1 11.0 %convolution_convert_fusion = bf16[1152,1792]{1,0:T(8,128)(2,1)} fusion(bf16[2048,1152]{1,0:T(8,128)(2,1)S(1)} %bitcast.287, bf16[1024,1792]{1,0:T(8,128)(2,1)S(1)} %get-tuple-element.229, bf16[1024,1792]{1,0:T(8,128)(2,1)S(1)} %copy-done.156), kind=kOutput, calls=%fused_computation.7 | convolution fusion | flops 8472461312 | bytes 16187392 | tf_op jit(solution)/shard_map/dot_general | solution.py:105
  427.9 11.8 %collective-permute-done.46 = bf16[256,1152]{1,0:T(8,128)(2,1)} collective-permute-done((bf16[256,1152]{1,0:T(8,128)(2,1)}, bf16[256,1152]{1,0:T(8,128)(2,1)}, u32[]{:S(2)}, u32[]{:S(2)}) %collective-permute-start.46) | collective-permute-done | bytes 589856 | tf_op jit(solution)/shard_map/ppermute | solution.py:115
  439.6 11.8 %collective-permute-done.44 = bf16[256,1152]{1,0:T(8,128)(2,1)} collective-permute-done((bf16[256,1152]{1,0:T(8,128)(2,1)}, bf16[256,1152]{1,0:T(8,128)(2,1)}, u32[]{:S(2)}, u32[]{:S(2)}) %collective-permute-start.44) | collective-permute-done | bytes 589856 | tf_op jit(solution)/shard_map/ppermute | solution.py:115
  539.1 9.9 %collective-permute-done.56 = bf16[57,16,144]{2,1,0:T(8,128)(2,1)S(1)} collective-permute-done((bf16[57,16,144]{2,1,0:T(8,128)(2,1)S(1)}, bf16[57,16,144]{2,1,0:T(8,128)(2,1)S(1)}, u32[]{:S(2)}, u32[]{:S(2)}) %collective-permute-start.56) | collective-permute-done | bytes 262688 | tf_op jit(solution)/shard_map/ppermute | solution.py:115
  565.7 15.8 %reduce-scatter.5.cloned.1.call-done = bf16[144,3584]{1,0:T(8,128)(2,1)} async-done(((bf16[1152,3584]{1,0:T(8,128)(2,1)}), bf16[144,3584]{1,0:T(8,128)(2,1)}) %reduce-scatter.5.cloned.1.call-update) | async-done | bytes 1032208 | tf_op jit(solution)/shard_map/reduce_scatter | solution.py:564
  639.4 12.6 %collective-permute-done.62 = bf16[144,1792]{1,0:T(8,128)(2,1)S(1)} collective-permute-done((bf16[144,1792]{1,0:T(8,128)(2,1)S(1)}, bf16[144,1792]{1,0:T(8,128)(2,1)S(1)}, u32[]{:S(2)}, u32[]{:S(2)}) %collective-permute-start.62) | collective-permute-done | bytes 516128 | tf_op jit(solution)/shard_map/ppermute | solution.py:115
  654.7 11.7 %owner_stats.2 = (f32[57,144,128]{2,1,0:T(8,128)}, f32[57,144,144]{2,1,0:T(8,128)}, f32[57,128,128]{2,1,0:T(8,128)}) custom-call(s32[57]{0:T(128)S(1)} %get-tuple-element.199.refs_0_, s32[57]{0:T(128)S(1)} %broadcast.987.refs_1_, s32[57]{0:T(128)S(1)} %get-tuple-element.198.refs_2_, s32[57]{0:T(128)S(1)} %get-tuple-element.197.refs_3_, ...), custom_call_target="tpu_custom_call" | custom-call | tf_op jit(solution)/shard_map/owner_stats/pallas_call | solution.py:334
  688.3 31.0 %update_blocks.2 = (f32[144,23296]{1,0:T(8,128)}, bf16[144,23296]{1,0:T(8,128)(2,1)}) custom-call(s32[161]{0:T(256)S(1)} %slice.310.refs_0_, s32[161]{0:T(256)S(1)} %broadcast.985.refs_1_, s32[161]{0:T(256)S(1)} %copy-done.4, s32[161]{0:T(256)S(1)} %slice.313.refs_3_, s32[161]{0:T(256)S(1)} %slice.314.refs_4_, bf16[4,1,144,5376]{3,2,1,0:T(8,128)(2,1)S(1)} %bitcast.222, ...), custom_call_target="tpu_custom_call" | custom-call | tf_op jit(solution)/shard_map/update_blocks/pallas_call | solution.py:288
  721.5 7.8 %owner_stats.3 = (f32[57,144,128]{2,1,0:T(8,128)}, f32[57,144,144]{2,1,0:T(8,128)}, f32[57,128,128]{2,1,0:T(8,128)}) custom-call(s32[57]{0:T(128)S(1)} %get-tuple-element.199.refs_0_, s32[57]{0:T(128)S(1)} %broadcast.987.refs_1_, s32[57]{0:T(128)S(1)} %get-tuple-element.198.refs_2_, ...), custom_call_target="tpu_custom_call", output_to_operand_aliasing={{0}: (13, {}), {1}: (14, {}), {2}: (15, {})} | custom-call | tf_op jit(solution)/shard_map/owner_stats/pallas_call | solution.py:334
  (764 shorter events, 408.1 us)
Async XLA Ops:
  7.2 187.1 %all-gather.3.cloned.1.call-start = ((), (), s32[]{:S(2)}) async-start(), calls=%async_computation.3 | async-start | bytes 9289728 | tf_op jit(solution)/shard_map/all_gather | solution.py:496
  20.3 219.2 %all-gather.5.cloned.1.call-start = ((), (), s32[]{:S(2)}) async-start(), calls=%async_computation.4 | async-start | bytes 4644864 | tf_op jit(solution)/shard_map/all_gather | solution.py:498
  60.4 28.3 %collective-permute-start.14 = (bf16[144,512]{1,0:T(8,128)(2,1)S(1)}, bf16[144,512]{1,0:T(8,128)(2,1)S(1)}, u32[]{:S(2)}, u32[]{:S(2)}) collective-permute-start(bf16[144,512]{1,0:T(8,128)(2,1)S(1)} %dynamic-slice_convert_fusion.4), channel_id=1, source_target_pairs={{0,2},{1,3},{2,0},{3,1},{4,6},{5,7},{6,4},{7,5},{8,10},{9,11},{10,... | collective-permute-start | bytes 442376 | tf_op jit(solution)/shard_map/ppermute | solution.py:164
  62.1 55.2 %collective-permute-start.10 = (bf16[256,512]{1,0:T(8,128)(2,1)S(1)}, bf16[256,512]{1,0:T(8,128)(2,1)}, u32[]{:S(2)}, u32[]{:S(2)}) collective-permute-start(bf16[256,512]{1,0:T(8,128)(2,1)S(1)} %get-tuple-element.254), channel_id=1, source_target_pairs={{0,1},{1,2},{2,3},{8,9},{9,10},{10,11},{16,17},{17,18},{18,19},{24... | collective-permute-start | bytes 786440 | tf_op jit(solution)/shard_map/ppermute | solution.py:384
  78.1 47.4 %collective-permute-start.11 = (bf16[256,512]{1,0:T(8,128)(2,1)}, bf16[256,512]{1,0:T(8,128)(2,1)S(1)}, u32[]{:S(2)}, u32[]{:S(2)}) collective-permute-start(bf16[256,512]{1,0:T(8,128)(2,1)} %collective-permute-done.8), channel_id=1, source_target_pairs={{4,5},{5,4},{12,13},{13,12},{20,21},{21,20},{28,29},{29,28}} | collective-permute-start | bytes 786440 | tf_op jit(solution)/shard_map/ppermute | solution.py:386
  86.2 26.8 %collective-permute-start.25 = (bf16[256,512]{1,0:T(8,128)(2,1)}, bf16[256,512]{1,0:T(8,128)(2,1)S(1)}, u32[]{:S(2)}, u32[]{:S(2)}) collective-permute-start(bf16[256,512]{1,0:T(8,128)(2,1)} %collective-permute-done.24), channel_id=1, source_target_pairs={{4,6},{5,7},{12,14},{13,15},{20,22},{21,23},{28,30},{29,31}} | collective-permute-start | bytes 786440 | tf_op jit(solution)/shard_map/ppermute | solution.py:385
  86.9 39.3 %collective-permute-start.12 = (bf16[256,512]{1,0:T(8,128)(2,1)S(1)}, bf16[256,512]{1,0:T(8,128)(2,1)S(1)}, u32[]{:S(2)}, u32[]{:S(2)}) collective-permute-start(bf16[256,512]{1,0:T(8,128)(2,1)S(1)} %collective-permute-done.9), channel_id=1, source_target_pairs={{6,7},{7,6},{14,15},{15,14},{22,23},{23,22},{30,31},{31,30}} | collective-permute-start | bytes 786440 | tf_op jit(solution)/shard_map/ppermute | solution.py:387
  88.7 39.8 %collective-permute-start.18 = (bf16[144,512]{1,0:T(8,128)(2,1)S(1)}, bf16[144,512]{1,0:T(8,128)(2,1)S(1)}, u32[]{:S(2)}, u32[]{:S(2)}) collective-permute-start(bf16[144,512]{1,0:T(8,128)(2,1)S(1)} %dynamic-slice_convert_fusion.4), channel_id=1, source_target_pairs={{0,6},{1,7},{2,4},{3,5},{4,2},{5,3},{6,0},{7,1},{8,14},{9,15},{10,... | collective-permute-start | bytes 442376 | tf_op jit(solution)/shard_map/ppermute | solution.py:164
  155.3 329.4 %reduce-scatter.3.cloned.1.call-start = ((), (), s32[]{:S(2)}) async-start(), calls=%async_computation.5 | async-start | bytes 4644864 | tf_op jit(solution)/shard_map/reduce_scatter | solution.py:564
  337.9 243.6 %reduce-scatter.5.cloned.1.call-start = ((), (), s32[]{:S(2)}) async-start(), calls=%async_computation.6 | async-start | bytes 9289728 | tf_op jit(solution)/shard_map/reduce_scatter | solution.py:564
  354.2 43.2 %collective-permute-start.42 = (bf16[57,128,128]{2,1,0:T(8,128)(2,1)}, bf16[57,128,128]{2,1,0:T(8,128)(2,1)}, u32[]{:S(2)}, u32[]{:S(2)}) collective-permute-start(bf16[57,128,128]{2,1,0:T(8,128)(2,1)} %bitcast.20), channel_id=1, source_target_pairs={{0,16},{8,24},{16,0},{24,8},{1,17},{9,25},{17,1},{25,9},{2,18},{10... | collective-permute-start | bytes 5603336 | tf_op jit(solution)/shard_map/ppermute | solution.py:115
  475.1 60.7 %collective-permute-start.55 = (bf16[57,144,128]{2,1,0:T(8,128)(2,1)S(1)}, bf16[57,144,128]{2,1,0:T(8,128)(2,1)}, u32[]{:S(2)}, u32[]{:S(2)}) collective-permute-start(bf16[57,144,128]{2,1,0:T(8,128)(2,1)S(1)} %get-tuple-element.97), channel_id=1, source_target_pairs={{0,16},{8,24},{16,0},{24,8},{1,17},{9,25},{17,1},{25,9},{2,18},{10... | collective-permute-start | bytes 6303752 | tf_op jit(solution)/shard_map/ppermute | solution.py:115
  499.3 28.5 %collective-permute-start.47 = (bf16[256,512]{1,0:T(8,128)(2,1)}, bf16[256,512]{1,0:T(8,128)(2,1)}, u32[]{:S(2)}, u32[]{:S(2)}) collective-permute-start(bf16[256,512]{1,0:T(8,128)(2,1)} %fusion.105), channel_id=1, source_target_pairs={{1,0},{2,1},{3,2},{9,8},{10,9},{11,10},{17,16},{18,17},{19,18},{25... | collective-permute-start | bytes 786440 | tf_op jit(solution)/shard_map/ppermute | solution.py:398
  511.2 26.1 %collective-permute-start.51 = (bf16[256,512]{1,0:T(8,128)(2,1)}, bf16[256,512]{1,0:T(8,128)(2,1)}, u32[]{:S(2)}, u32[]{:S(2)}) collective-permute-start(bf16[256,512]{1,0:T(8,128)(2,1)} %fusion.100), channel_id=1, source_target_pairs={{1,0},{2,1},{3,2},{9,8},{10,9},{11,10},{17,16},{18,17},{19,18},{25... | collective-permute-start | bytes 786440 | tf_op jit(solution)/shard_map/ppermute | solution.py:398
  527.8 87.8 %collective-permute-start.79 = (bf16[57,128,128]{2,1,0:T(8,128)(2,1)}, bf16[57,128,128]{2,1,0:T(8,128)(2,1)}, u32[]{:S(2)}, u32[]{:S(2)}) collective-permute-start(bf16[57,128,128]{2,1,0:T(8,128)(2,1)} %bitcast.20), channel_id=1, source_target_pairs={{0,8},{8,0},{16,24},{24,16},{1,9},{9,1},{17,25},{25,17},{2,10},{10... | collective-permute-start | bytes 5603336 | tf_op jit(solution)/shard_map/ppermute | solution.py:109
  534.4 138.2 %collective-permute-start.80 = (bf16[57,128,128]{2,1,0:T(8,128)(2,1)}, bf16[57,128,128]{2,1,0:T(8,128)(2,1)}, u32[]{:S(2)}, u32[]{:S(2)}) collective-permute-start(bf16[57,128,128]{2,1,0:T(8,128)(2,1)} %collective-permute-done.42), channel_id=1, source_target_pairs={{0,8},{8,0},{16,24},{24,16},{1,9},{9,1},{17,25},{25,17},{2,10},{10... | collective-permute-start | bytes 5603336 | tf_op jit(solution)/shard_map/ppermute | solution.py:109
  537.3 78.9 %collective-permute-start.75 = (bf16[57,144,128]{2,1,0:T(8,128)(2,1)S(1)}, bf16[57,144,128]{2,1,0:T(8,128)(2,1)}, u32[]{:S(2)}, u32[]{:S(2)}) collective-permute-start(bf16[57,144,128]{2,1,0:T(8,128)(2,1)S(1)} %get-tuple-element.97), channel_id=1, source_target_pairs={{0,8},{8,0},{16,24},{24,16},{1,9},{9,1},{17,25},{25,17},{2,10},{10... | collective-permute-start | bytes 6303752 | tf_op jit(solution)/shard_map/ppermute | solution.py:109
  537.5 78.1 %collective-permute-start.76 = (bf16[57,144,128]{2,1,0:T(8,128)(2,1)}, bf16[57,144,128]{2,1,0:T(8,128)(2,1)}, u32[]{:S(2)}, u32[]{:S(2)}) collective-permute-start(bf16[57,144,128]{2,1,0:T(8,128)(2,1)} %collective-permute-done.55), channel_id=1, source_target_pairs={{0,8},{8,0},{16,24},{24,16},{1,9},{9,1},{17,25},{25,17},{2,10},{10... | collective-permute-start | bytes 6303752 | tf_op jit(solution)/shard_map/ppermute | solution.py:109
  615.6 63.4 %collective-permute-start.77 = (bf16[57,16,144]{2,1,0:T(8,128)(2,1)S(1)}, bf16[57,16,144]{2,1,0:T(8,128)(2,1)}, u32[]{:S(2)}, u32[]{:S(2)}) collective-permute-start(bf16[57,16,144]{2,1,0:T(8,128)(2,1)S(1)} %get-tuple-element.101), channel_id=1, source_target_pairs={{0,8},{8,0},{16,24},{24,16},{1,9},{9,1},{17,25},{25,17},{2,10},{10... | collective-permute-start | bytes 787976 | tf_op jit(solution)/shard_map/ppermute | solution.py:109
  615.7 66.9 %collective-permute-start.78 = (bf16[57,16,144]{2,1,0:T(8,128)(2,1)S(1)}, bf16[57,16,144]{2,1,0:T(8,128)(2,1)}, u32[]{:S(2)}, u32[]{:S(2)}) collective-permute-start(bf16[57,16,144]{2,1,0:T(8,128)(2,1)S(1)} %copy-done.94), channel_id=1, source_target_pairs={{0,8},{8,0},{16,24},{24,16},{1,9},{9,1},{17,25},{25,17},{2,10},{10... | collective-permute-start | bytes 787976 | tf_op jit(solution)/shard_map/ppermute | solution.py:109
  625.3 43.8 %all-to-all-start = ((bf16[8,144,640]{2,1,0:T(8,128)(2,1)}), bf16[8,144,640]{2,1,0:T(8,128)(2,1)S(1)}, u32[]{:S(2)}, u32[]{:S(2)}) async-start(bf16[8,144,640]{2,1,0:T(8,128)(2,1)} %bitcast.41), calls=%async_computation.2 | async-start | bytes 2949120 | tf_op jit(solution)/shard_map/all_to_all | solution.py:184
  685.1 34.3 %collective-permute-start.74 = (f32[5120]{0:T(1024)S(1)}, f32[5120]{0:T(1024)S(1)}, u32[]{:S(2)}, u32[]{:S(2)}) collective-permute-start(f32[5120]{0:T(1024)S(1)} %add.732), channel_id=1, source_target_pairs={{0,4},{1,5},{2,6},{3,7},{4,0},{5,1},{6,2},{7,3},{8,12},{9,13},{10,... | collective-permute-start | bytes 61448 | tf_op jit(solution)/shard_map/ppermute | solution.py:154
  687.5 32.7 %collective-permute-start.68 = (bf16[144,640]{1,0:T(8,128)(2,1)S(1)}, bf16[144,640]{1,0:T(8,128)(2,1)S(1)}, u32[]{:S(2)}, u32[]{:S(2)}) collective-permute-start(bf16[144,640]{1,0:T(8,128)(2,1)S(1)} %reduce_sum.428), channel_id=1, source_target_pairs={{0,8},{8,0},{16,24},{24,16},{1,9},{9,1},{17,25},{25,17},{2,10},{10... | collective-permute-start | bytes 552968 | tf_op jit(solution)/shard_map/ppermute | solution.py:109
  687.6 32.4 %collective-permute-start.67 = (bf16[144,640]{1,0:T(8,128)(2,1)S(1)}, bf16[144,640]{1,0:T(8,128)(2,1)S(1)}, u32[]{:S(2)}, u32[]{:S(2)}) collective-permute-start(bf16[144,640]{1,0:T(8,128)(2,1)S(1)} %reduce_sum.428), channel_id=1, source_target_pairs={{0,16},{8,24},{16,0},{24,8},{1,17},{9,25},{17,1},{25,9},{2,18},{10... | collective-permute-start | bytes 552968 | tf_op jit(solution)/shard_map/ppermute | solution.py:115
  (234 other events, 2268.5 us)
Sparse Core Ops, SparseCore 0:
  20.4 141.5 all-gather.2
  164.2 75.2 all-gather.4
  338.0 85.7 reduce-scatter.2
  428.5 153.0 reduce-scatter.4
